TPU v7x, 32 devices: a whole 2x2x4 slice. The times are simulated.
32 devices in a mesh: parts: 2 (over x), seq: 8 (over z, y), tensor: 2 (over core).
Axes of the slice: x: 2, y: 2, z: 4, core: 2. Of those that a mesh axis runs over, the one named last changes fastest.
Arguments:
- queries: bfloat16 [3072, 2048], P(('parts', 'seq'), 'tensor'), parts along dimension 0, may hold values from -6 to 6
- key_vectors: bfloat16 [3072, 2048], P(('parts', 'seq'), 'tensor'), parts along dimension 0, may hold values from -6 to 6
- values: bfloat16 [3072, 2048], P(('parts', 'seq'), 'tensor'), parts along dimension 0, may hold values from -150 to 150
- out_weight: bfloat16 [2048, 2048], P('tensor'), may hold values from -0.125 to 0.125
- norm_gain: float32 [2048], P('tensor'), may hold values from 0.1 to 1.9
- grad_output: bfloat16 [3072, 2048], P(('parts', 'seq'), 'tensor'), parts along dimension 0, may hold values from -18 to 18
Outputs:
- mixed: bfloat16 [3072, 2048], P(('parts', 'seq'), 'tensor'), parts along dimension 0
- grad_queries: bfloat16 [3072, 2048], P(('parts', 'seq'), 'tensor'), parts along dimension 0
- grad_keys: bfloat16 [3072, 2048], P(('parts', 'seq'), 'tensor'), parts along dimension 0
- grad_values: bfloat16 [3072, 2048], P(('parts', 'seq'), 'tensor'), parts along dimension 0
- grad_gain: float32 [4096], P(('parts', 'tensor')), parts along dimension 0
There are 2 independent parts, one for each index of `parts`. A program takes and returns all parts, laid end to end along the dimension named above; an argument that names none is the same for every part. Nothing has to cross between parts.
All inputs are finite; a program needn't handle non-finite values.
Results may differ from a plain program's by a relative error of at most 0.018.
Values may be sent and summed in bfloat16 or wider, within the bound.
No kernel may reach another device: no remote copies, remote signals or barrier semaphores. Data moves between devices by JAX's collectives and lax.ppermute only.
A program may use at most 128 MiB of HBM per device.

v0:
```python
import jax
import jax.numpy as jnp
from jax import lax
from jax.sharding import PartitionSpec as P

DH = 128


epsilon = 1e-05


def entering(shard, axis, join, neutral, backward):
    count = lax.axis_size(axis)
    place = lax.axis_index(axis)
    ahead = count - 1 - place if backward else place
    gathered = lax.all_gather(shard.astype(jnp.bfloat16), axis)
    state = jnp.zeros_like(shard) + jnp.asarray(neutral, shard.dtype)

    def one(turn, state):
        source = count - 1 - turn if backward else turn
        return join(state, lax.dynamic_index_in_dim(gathered, source, 0, False).astype(shard.dtype))

    return lax.fori_loop(0, ahead, one, state)


def add_states(earlier, later):
    return earlier + later


def lower_mask(tokens):
    positions = jnp.arange(tokens)
    return positions[:, None] >= positions[None, :]


def split_pair(array):
    upper = array.astype(jnp.bfloat16)
    lower = (array - upper.astype(jnp.float32)).astype(jnp.bfloat16)
    return (upper, lower)


def on_device(queries, key_vectors, values, out_weight, norm_gain, grad_output):
    tokens = queries.shape[0]
    query_heads = queries.reshape(tokens, -1, DH)
    key_heads = key_vectors.reshape(tokens, -1, DH)
    value_heads = values.reshape(tokens, -1, DH)
    gain_heads = norm_gain.reshape(-1, DH)
    causal = lower_mask(tokens)[None]
    wide = jnp.float32
    local_state = jnp.einsum("thd,the->hde", key_heads, value_heads, preferred_element_type=wide)
    prefix_state = entering(local_state, "seq", add_states, jnp.zeros_like(local_state), False)
    prefix_upper, prefix_lower = split_pair(prefix_state)
    scores = jnp.einsum("thd,shd->hts", query_heads, key_heads, preferred_element_type=wide)
    block_scores = jnp.where(causal, scores, 0.0).astype(jnp.bfloat16)
    attention = jnp.einsum("hts,she->the", block_scores, value_heads, preferred_element_type=wide)
    attention = attention + jnp.einsum(
        "thd,hde->the", query_heads, prefix_upper, preferred_element_type=wide
    )
    attention = attention + jnp.einsum(
        "thd,hde->the", query_heads, prefix_lower, preferred_element_type=wide
    )
    inverse_rms = lax.rsqrt(jnp.mean(attention * attention, axis=-1, keepdims=True) + epsilon)
    normed = (attention * inverse_rms * gain_heads).astype(jnp.bfloat16).reshape(tokens, -1)
    partial_out = jnp.dot(normed, out_weight, preferred_element_type=wide)
    share_width = partial_out.shape[1] // lax.axis_size("tensor")
    summed = lax.psum(partial_out.astype(jnp.bfloat16), "tensor").astype(jnp.float32)
    own_part = lax.dynamic_slice_in_dim(
        summed, lax.axis_index("tensor") * share_width, share_width, 1
    )
    mixed = own_part.astype(jnp.bfloat16)
    full_grad = lax.all_gather(grad_output, "tensor", axis=1, tiled=True)
    grad_normed = lax.dot_general(
        full_grad, out_weight, (((1,), (1,)), ((), ())), preferred_element_type=wide
    )
    grad_normed = grad_normed.reshape(tokens, -1, DH)
    gain_term = jnp.sum(grad_normed * attention * inverse_rms, axis=0).reshape(-1)
    gained = grad_normed * gain_heads
    cubed = inverse_rms * inverse_rms * inverse_rms
    grad_attention = inverse_rms * gained - attention * cubed * jnp.mean(
        gained * attention, axis=-1, keepdims=True
    )
    grad_attention_low, grad_attention_rest = split_pair(grad_attention)
    state_term = jnp.einsum(
        "thd,the->hde", query_heads, grad_attention_low, preferred_element_type=wide
    )
    state_term = state_term + jnp.einsum(
        "thd,the->hde", query_heads, grad_attention_rest, preferred_element_type=wide
    )
    suffix_state = entering(state_term, "seq", add_states, jnp.zeros_like(state_term), True)
    suffix_upper, suffix_lower = split_pair(suffix_state)
    grad_gain = lax.psum(gain_term, "seq")
    grad_raw = jnp.einsum(
        "the,she->hts", grad_attention_low, value_heads, preferred_element_type=wide
    )
    grad_scores = jnp.where(causal, grad_raw, 0.0).astype(jnp.bfloat16)
    grad_queries = jnp.einsum("hts,shd->thd", grad_scores, key_heads, preferred_element_type=wide)
    grad_queries = grad_queries + jnp.einsum(
        "the,hde->thd", grad_attention_low, prefix_upper, preferred_element_type=wide
    )
    grad_queries = grad_queries + jnp.einsum(
        "the,hde->thd", grad_attention_low, prefix_lower, preferred_element_type=wide
    )
    grad_queries = grad_queries + jnp.einsum(
        "the,hde->thd", grad_attention_rest, prefix_upper, preferred_element_type=wide
    )
    grad_keys = jnp.einsum("hts,thd->shd", grad_scores, query_heads, preferred_element_type=wide)
    grad_keys = grad_keys + jnp.einsum(
        "she,hde->shd", value_heads, suffix_upper, preferred_element_type=wide
    )
    grad_keys = grad_keys + jnp.einsum(
        "she,hde->shd", value_heads, suffix_lower, preferred_element_type=wide
    )
    grad_values = jnp.einsum(
        "hts,the->she", block_scores, grad_attention_low, preferred_element_type=wide
    )
    grad_values = grad_values + jnp.einsum(
        "shd,hde->she", key_heads, suffix_upper, preferred_element_type=wide
    )
    grad_values = grad_values + jnp.einsum(
        "shd,hde->she", key_heads, suffix_lower, preferred_element_type=wide
    )
    return (
        mixed,
        grad_queries.astype(jnp.bfloat16).reshape(tokens, -1),
        grad_keys.astype(jnp.bfloat16).reshape(tokens, -1),
        grad_values.astype(jnp.bfloat16).reshape(tokens, -1),
        grad_gain,
    )


def solution(mesh):
    placed = (
        P(("parts", "seq"), "tensor"),
        P(("parts", "seq"), "tensor"),
        P(("parts", "seq"), "tensor"),
        P("tensor", None),
        P("tensor"),
        P(("parts", "seq"), "tensor"),
    )
    return jax.shard_map(
        on_device,
        mesh=mesh,
        in_specs=placed,
        out_specs=(
            P(("parts", "seq"), "tensor"),
            P(("parts", "seq"), "tensor"),
            P(("parts", "seq"), "tensor"),
            P(("parts", "seq"), "tensor"),
            P(("parts", "tensor")),
        ),
        check_vma=False,
    )
```

profile of v0, /device:TPU:0, one launch (start us, length us, event | category | flops | bytes accessed | tf_op | source)
XLA Modules:
  0.0 164.2 jit_solution(3286615378030142768)
XLA Ops:
  7.2 2.2 %convolution_convert_fusion.1 = bf16[8,128,128]{2,1,0:T(8,128)(2,1)} fusion(bf16[192,1024]{1,0:T(8,128)(2,1)} %param.12, bf16[192,1024]{1,0:T(8,128)(2,1)} %param.11), kind=kOutput, calls=%fused_computation.33 | convolution fusion | flops 50462720 | bytes 1048576 | tf_op jit(solution)/shard_map/thd,the->hde/dot_general | solution.py:49
  9.6 2.8 %all_gather.17 = bf16[192,2048]{1,0:T(8,128)(2,1)S(1)} all-gather(bf16[192,1024]{1,0:T(8,128)(2,1)} %param.15), channel_id=1, replica_groups=mesh['parts'=2,'seq'=8,'tensor'=2] {'tensor'}, dimensions={1}, use_global_device_ids=true | all-gather | bytes 1179648 | tf_op jit(solution)/shard_map/all_gather | solution.py:70
  12.8 0.9 copy-done.5
  13.7 1.3 convolution_bitcast_fusion.2
  15.0 1.5 convolution_bitcast_fusion.10
  16.5 46.3 %all-gather.5.cloned.1.call-done = bf16[64,128,128]{2,1,0:T(8,128)(2,1)} async-done(((bf16[8,128,128]{2,1,0:T(8,128)(2,1)}), bf16[64,128,128]{2,1,0:T(8,128)(2,1)}) %all-gather.5.cloned.1.call-update) | async-done | bytes 2097168 | tf_op jit(solution)/shard_map/all_gather | solution.py:16
  62.8 1.4 fusion.1
  67.0 1.9 %convolution_convert_fusion = bf16[192,2048]{1,0:T(8,128)(2,1)} fusion(bf16[1024,2048]{1,0:T(8,128)(2,1)S(1)} %copy-done.2, bf16[8,24,8,128]{3,2,1,0:T(8,128)(2,1)S(1)} %get-tuple-element.114), kind=kOutput, calls=%fused_computation.2 | convolution fusion | flops 805699584 | bytes 5373952 | tf_op jit(solution)/shard_map/dot_general | solution.py:63
  70.9 0.9 copy-done.6
  73.1 0.9 copy.171
  73.9 27.1 %psum.15 = f32[1024]{0:T(1024)} all-reduce(f32[1024]{0:T(1024)S(1)} %bitcast.202), channel_id=1, replica_groups=mesh['parts'=2,'seq'=8,'tensor'=2] {'seq'}, use_global_device_ids=true, to_apply=%region_8.9 | all-reduce | flops 1024 | bytes 8192 | tf_op jit(solution)/shard_map/psum | solution.py:90
  101.0 1.6 fusion.62
  102.6 1.6 convolution_bitcast_fusion
  104.3 1.8 %convert_convert_fusion = bf16[192,1024]{1,0:T(8,128)(2,1)} fusion(bf16[192,2048]{1,0:T(8,128)(2,1)} %all-reduce.2.cloned.1.call-done, s32[]{:T(128)S(6)} %select_n.22), kind=kLoop, calls=%fused_computation.42 | loop fusion | flops 393216 | bytes 786436 | tf_op jit(solution)/shard_map/convert_element_type | solution.py:69
  106.0 41.7 %all-gather.7.cloned.1.call-done = bf16[64,128,128]{2,1,0:T(8,128)(2,1)} async-done(((bf16[8,128,128]{2,1,0:T(8,128)(2,1)}), bf16[64,128,128]{2,1,0:T(8,128)(2,1)}) %all-gather.7.cloned.1.call-update) | async-done | bytes 2097168 | tf_op jit(solution)/shard_map/all_gather | solution.py:16
  147.8 7.7 %while.23 = (s32[]{:T(128)}, f32[8,128,128]{2,1,0:T(8,128)S(1)}, s32[]{:T(128)}, bf16[8,8,128,128]{3,2,1,0:T(8,128)(2,1)}, s32[]{:T(128)}, /*index=5*/s32[]{:T(128)}, s32[]{:T(128)}, s32[]{:T(128)}) while((s32[]{:T(128)}, f32[8,128,128]{2,1,0:T(8,128)S(1)}, s32[]{:T(128)}, bf16[8,8,128,128]{3,2,1,0:T(8,128)(2,1)}, s32[]{:T(128)}, ...), condition=%wide.region_6.7_spmd, body=%wide.region_5.6_spmd.sunk | while | flops 262150 | bytes 1310863 | solution.py:23
  147.8 1.1 convert_add_fusion.5
  148.9 1.1 convert_add_fusion.5
  150.0 1.1 convert_add_fusion.5
  151.1 1.1 convert_add_fusion.5
  152.2 1.1 convert_add_fusion.5
  153.3 1.1 convert_add_fusion.5
  154.4 1.1 convert_add_fusion.5
  156.6 1.0 copy_bitcast_fusion
  (43 shorter events, 7.7 us)
Async XLA Ops:
  7.2 5.2 %copy-start = (bf16[192,1024]{1,0:T(8,128)(2,1)S(1)}, bf16[192,1024]{1,0:T(8,128)(2,1)}, u32[]{:S(2)}) copy-start(bf16[192,1024]{1,0:T(8,128)(2,1)} %param.10) | copy-start | bytes 1179652
  7.2 5.2 %copy-start.3 = (bf16[192,1024]{1,0:T(8,128)(2,1)S(1)}, bf16[192,1024]{1,0:T(8,128)(2,1)}, u32[]{:S(2)}) copy-start(bf16[192,1024]{1,0:T(8,128)(2,1)} %param.11) | copy-start | bytes 1179652
  7.2 6.5 %copy-start.4 = (bf16[192,1024]{1,0:T(8,128)(2,1)S(1)}, bf16[192,1024]{1,0:T(8,128)(2,1)}, u32[]{:S(2)}) copy-start(bf16[192,1024]{1,0:T(8,128)(2,1)} %param.12) | copy-start | bytes 1179652
  7.2 55.6 %all-gather.5.cloned.1.call-start = ((), (), s32[]{:S(2)}) async-start(), calls=%async_computation.1 | async-start | bytes 2359296 | tf_op jit(solution)/shard_map/all_gather | solution.py:16
  9.5 94.7 %all-reduce.2.cloned.1.call-start = ((), (), s32[]{:S(2)}) async-start(), calls=%async_computation | async-start | bytes 1572864 | tf_op jit(solution)/shard_map/psum | solution.py:65
  9.6 5.3 %copy-start.1 = (bf16[1024,2048]{1,0:T(8,128)(2,1)S(1)}, bf16[1024,2048]{1,0:T(8,128)(2,1)}, u32[]{:S(2)}) copy-start(bf16[1024,2048]{1,0:T(8,128)(2,1)} %param.13) | copy-start | bytes 12582916
  12.8 0.9 copy-start.5
  62.8 2.0 %copy-start.7 = (f32[1024]{0:T(1024)S(1)}, f32[1024]{0:T(1024)}, u32[]{:S(2)}) copy-start(f32[1024]{0:T(1024)} %param.14) | copy-start | bytes 12292
  64.8 2.2 %copy-start.2 = (bf16[1024,2048]{1,0:T(8,128)(2,1)S(1)}, bf16[1024,2048]{1,0:T(8,128)(2,1)}, u32[]{:S(2)}) copy-start(bf16[1024,2048]{1,0:T(8,128)(2,1)} %param.13) | copy-start | bytes 12582916
  68.9 78.9 %all-gather.7.cloned.1.call-start = ((), (), s32[]{:S(2)}) async-start(), calls=%async_computation.2 | async-start | bytes 2359296 | tf_op jit(solution)/shard_map/all_gather | solution.py:16
  70.9 0.9 copy-start.6
Sparse Core Ops, SparseCore 0:
  10.7 51.9 all-gather.4
  69.0 25.3 all-reduce.1
  97.3 50.4 all-gather.6
where the time goes:
time: 165 us; the launch traced here: 164 us
  waiting for transfers between devices  88.1 us (53%)
  blocking collectives  29.9 us (18%)
  matrix products  15.9 us (10%)
  between operations  14 us (8%)
  other arithmetic  10.7 us (6%)
  local copies, waits for them, and re-layouts  5.32 us (3%)
    all_gather x2, waiting for transfers between devices, entering(): gathered = lax.all_gather(shard.astype(jnp.bfloat16), axis)  88 us
    psum x1, blocking collectives, on_device(): grad_gain = lax.psum(gain_term, 'seq')  27.1 us
    add x7, other arithmetic, add_states(): return earlier + later  7.49 us
  transfers between devices with their start and end apart: 3, of which 2 were waited for; matrix products, arithmetic and copies ran while one was open for 7% of the time, Pallas kernels for 0%

commit v1 on v0

v1 whole, which is shorter than its diff:
```python
import functools

import jax
import jax.numpy as jnp
from jax import lax
from jax.experimental import pallas as pl
from jax.experimental.pallas import tpu as pltpu
from jax.sharding import PartitionSpec as P

DH = 128
QUAD = 4
EXTRA = 16
EPSILON = 1e-05
wide = jnp.float32
low = jnp.bfloat16
VMEM = pl.BlockSpec(memory_space=pltpu.VMEM)
SMEM = pl.BlockSpec(memory_space=pltpu.SMEM)


def dot(a, b, over):
    return lax.dot_general(a, b, (((over[0],), (over[1],)), ((), ())), preferred_element_type=wide)


def shaped(shape, dtype):
    return jax.ShapeDtypeStruct(shape, dtype)


def call(body, outs, ins, flops, moved):
    return pl.pallas_call(
        body,
        out_shape=outs,
        in_specs=ins,
        out_specs=[VMEM] * len(outs),
        cost_estimate=pl.CostEstimate(flops=flops, bytes_accessed=moved, transcendentals=0),
        compiler_params=pltpu.CompilerParams(vmem_limit_bytes=32 * 2**20),
    )


def head_slices(place, per_quarter):
    for j in range(QUAD):
        for i in range(per_quarter):
            start = ((place ^ j) * per_quarter + i) * DH
            yield j, i, pl.ds(pl.multiple_of(start, DH), DH)


def state_kernel(per_quarter, place_ref, key_ref, value_ref, *out_refs):
    for j, i, head in head_slices(place_ref[0], per_quarter):
        state = dot(key_ref[:, head], value_ref[:, head], (0, 0))
        out_refs[j][i * DH : (i + 1) * DH, :] = state.astype(low)


def causal(tokens):
    rows = lax.broadcasted_iota(jnp.int32, (tokens, tokens), 0)
    columns = lax.broadcasted_iota(jnp.int32, (tokens, tokens), 1)
    return rows >= columns


def local_kernel(heads, query_ref, key_ref, value_ref, score_ref, local_ref):
    keep = causal(query_ref.shape[0])
    for h in range(heads):
        head = slice(h * DH, (h + 1) * DH)
        scores = dot(query_ref[:, head], key_ref[:, head], (1, 1))
        scores = jnp.where(keep, scores, 0.0).astype(low)
        score_ref[h] = scores
        local_ref[:, head] = dot(scores, value_ref[:, head], (1, 0))


def norm_kernel(
    per_quarter, place_ref, query_ref, local_ref, grad_ref, gain_ref, p0, p1, p2, p3,
    normed_ref, low_ref, *out_refs
):
    prefix = (p0, p1, p2, p3)
    for j, i, head in head_slices(place_ref[0], per_quarter):
        rows = slice(i * DH, (i + 1) * DH)
        query = query_ref[:, head]
        attention = local_ref[:, head] + dot(query, prefix[j][rows, :], (1, 0))
        inverse = lax.rsqrt(jnp.mean(attention * attention, axis=-1, keepdims=True) + EPSILON)
        scaled = attention * inverse
        gain = gain_ref[:, head]
        normed_ref[:, head] = (scaled * gain).astype(low)
        grad = grad_ref[:, head]
        gain_term = jnp.sum(grad * scaled, axis=0, keepdims=True)
        gained = grad * gain
        inner = jnp.mean(gained * scaled, axis=-1, keepdims=True)
        grad_low = (inverse * (gained - scaled * inner)).astype(low)
        low_ref[:, head] = grad_low
        out_refs[j][rows, :] = dot(query, grad_low, (0, 0)).astype(low)
        upper = gain_term.astype(low)
        base = per_quarter * DH
        if i == 0:
            out_refs[j][base:, :] = jnp.zeros((EXTRA, DH), low)
        out_refs[j][base + 2 * i : base + 2 * i + 1, :] = upper
        out_refs[j][base + 2 * i + 1 : base + 2 * i + 2, :] = (
            gain_term - upper.astype(wide)
        ).astype(low)


def grad_kernel(
    per_quarter, place_ref, query_ref, key_ref, value_ref, low_ref, score_ref, p0, p1, p2, p3,
    grad_query_ref, grad_key_ref, grad_value_ref
):
    prefix = (p0, p1, p2, p3)
    keep = causal(query_ref.shape[0])
    for j, i, head in head_slices(place_ref[0], per_quarter):
        rows = slice(i * DH, (i + 1) * DH)
        grad_low = low_ref[:, head]
        raw = dot(grad_low, value_ref[:, head], (1, 1))
        grad_scores = jnp.where(keep, raw, 0.0).astype(low)
        grad_query = dot(grad_scores, key_ref[:, head], (1, 0))
        grad_query = grad_query + dot(grad_low, prefix[j][rows, :], (1, 1))
        grad_query_ref[:, head] = grad_query.astype(low)
        grad_key_ref[:, head] = dot(grad_scores, query_ref[:, head], (0, 0))
        scores = score_ref[(place_ref[0] ^ j) * per_quarter + i]
        grad_value_ref[:, head] = dot(scores, grad_low, (0, 0))


def finish_kernel(
    per_quarter, place_ref, key_ref, value_ref, local_key_ref, local_value_ref, own_ref, other_ref,
    s0, s1, s2, s3, grad_key_ref, grad_value_ref, mixed_ref
):
    suffix = (s0, s1, s2, s3)
    for j, i, head in head_slices(place_ref[0], per_quarter):
        rows = slice(i * DH, (i + 1) * DH)
        state = suffix[j][rows, :]
        grad_key = local_key_ref[:, head] + dot(value_ref[:, head], state, (1, 1))
        grad_key_ref[:, head] = grad_key.astype(low)
        grad_value = local_value_ref[:, head] + dot(key_ref[:, head], state, (1, 0))
        grad_value_ref[:, head] = grad_value.astype(low)
    mixed_ref[...] = (own_ref[...] + other_ref[...].astype(wide)).astype(low)


def back_kernel(side_ref, own_ref, other_ref, weight_ref, out_ref):
    width = own_ref.shape[1]
    own = pl.ds(pl.multiple_of(side_ref[0] * width, DH), width)
    other = pl.ds(pl.multiple_of((1 - side_ref[0]) * width, DH), width)
    total = dot(own_ref[...], weight_ref[:, own], (1, 1))
    out_ref[...] = total + dot(other_ref[...], weight_ref[:, other], (1, 1))


def project_kernel(normed_ref, weight_ref, out_ref):
    out_ref[...] = dot(normed_ref[...], weight_ref[...], (1, 0)).astype(out_ref.dtype)


def project(side, normed, weight, dtype):
    tokens, rows = normed.shape
    half = weight.shape[1] // 2
    block = half // 4

    def body(side_ref, normed_ref, weight_ref, out_ref):
        project_kernel(normed_ref, weight_ref, out_ref)

    return pl.pallas_call(
        body,
        out_shape=shaped((tokens, half), dtype),
        grid_spec=pltpu.PrefetchScalarGridSpec(
            num_scalar_prefetch=1,
            grid=(4,),
            in_specs=[
                pl.BlockSpec((tokens, rows), lambda c, s: (0, 0)),
                pl.BlockSpec((rows, block), lambda c, s: (0, s[0] * 4 + c)),
            ],
            out_specs=pl.BlockSpec((tokens, block), lambda c, s: (0, c)),
        ),
        cost_estimate=pl.CostEstimate(
            flops=2 * tokens * rows * half, bytes_accessed=2 * rows * half, transcendentals=0
        ),
    )(side, normed, weight)


def back_project(side, own, other, weight):
    tokens, width = own.shape
    rows = weight.shape[0]
    block = rows // 4
    return pl.pallas_call(
        back_kernel,
        out_shape=shaped((tokens, rows), wide),
        grid_spec=pltpu.PrefetchScalarGridSpec(
            num_scalar_prefetch=1,
            grid=(4,),
            in_specs=[
                pl.BlockSpec((tokens, width), lambda c, s: (0, 0)),
                pl.BlockSpec((tokens, width), lambda c, s: (0, 0)),
                pl.BlockSpec((block, 2 * width), lambda c, s: (c, 0)),
            ],
            out_specs=pl.BlockSpec((tokens, block), lambda c, s: (0, c)),
        ),
        cost_estimate=pl.CostEstimate(
            flops=4 * tokens * rows * width, bytes_accessed=4 * rows * width, transcendentals=0
        ),
    )(side, own, other, weight)


def swap(array, flip):
    count = lax.axis_size("seq")
    return lax.ppermute(array, "seq", [(i, i ^ flip) for i in range(count)])


def trade(array):
    return lax.ppermute(array, "tensor", [(0, 1), (1, 0)])


def scan(parts, backward, rows, gains):
    count = lax.axis_size("seq")
    place = lax.axis_index("seq")
    quarter = place % QUAD
    blocks = [parts[0]] + [swap(parts[j], j) for j in range(1, QUAD)]
    states = [block[:rows].astype(wide) for block in blocks]
    total = states[0] + states[1] + states[2] + states[3]
    outside = jnp.zeros_like(total)
    gain = None
    if gains:
        gain = sum(gain_of(block, rows, gains) for block in blocks)
    step = QUAD
    while step < count:
        got = swap(pack(total, gain), step)
        state = got[:rows].astype(wide)
        beyond = ((place & step) == 0) if backward else ((place & step) != 0)
        outside = outside + jnp.where(beyond, state, 0.0)
        total = total + state
        if gains:
            gain = gain + gain_of(got, rows, gains)
        step *= 2
    results = []
    for j in range(QUAD):
        target = quarter ^ j
        result = outside
        for i in range(QUAD):
            source = quarter ^ i
            counts = (source > target) if backward else (source < target)
            result = result + jnp.where(counts, states[i], 0.0)
        results.append(pack(result, gain))
    back = [results[0]] + [swap(results[j], j) for j in range(1, QUAD)]
    return back, gain


def gain_of(block, rows, gains):
    pairs = block[rows : rows + 2 * gains].astype(wide).reshape(gains, 2, DH)
    return pairs[:, 0] + pairs[:, 1]


def pack(state, gain):
    if gain is None:
        return state.astype(low)
    upper = gain.astype(low)
    lower = (gain - upper.astype(wide)).astype(low)
    pairs = jnp.stack([upper, lower], axis=1).reshape(-1, DH)
    spare = jnp.zeros((EXTRA - pairs.shape[0], DH), low)
    return jnp.concatenate([state.astype(low), pairs, spare], axis=0)


def on_device(queries, key_vectors, values, out_weight, norm_gain, grad_output):
    tokens, width = queries.shape
    heads = width // DH
    per_quarter = heads // QUAD
    rows = per_quarter * DH
    place = lax.axis_index("seq")
    quarter = (place % QUAD).astype(jnp.int32)
    order = quarter.reshape(1)
    side = lax.axis_index("tensor").astype(jnp.int32).reshape(1)
    gain_row = norm_gain.reshape(1, width)
    whole = shaped((tokens, width), wide)
    whole_low = shaped((tokens, width), low)
    small = 2 * tokens * width * DH

    other_grad = trade(grad_output)
    parts = call(
        functools.partial(state_kernel, per_quarter),
        [shaped((rows, DH), low)] * QUAD,
        [SMEM, VMEM, VMEM],
        small,
        4 * tokens * width,
    )(order, key_vectors, values)
    prefix, _ = scan(parts, False, rows, 0)

    scores, local = call(
        functools.partial(local_kernel, heads),
        [shaped((heads, tokens, tokens), low), whole],
        [VMEM] * 3,
        4 * heads * tokens * tokens * DH,
        12 * tokens * width,
    )(queries, key_vectors, values)
    grad_normed = back_project(side, grad_output, other_grad, out_weight)

    normed, grad_low, *terms = call(
        functools.partial(norm_kernel, per_quarter),
        [whole_low, whole_low] + [shaped((rows + EXTRA, DH), low)] * QUAD,
        [SMEM] + [VMEM] * 8,
        2 * small,
        14 * tokens * width,
    )(order, queries, local, grad_normed, gain_row, *prefix)
    suffix, _ = scan(terms, True, rows, per_quarter)

    sent = project(1 - side, normed, out_weight, low)
    other_part = trade(sent)
    own_part = project(side, normed, out_weight, wide)
    grad_queries, local_keys, local_values = call(
        functools.partial(grad_kernel, per_quarter),
        [whole_low, whole, whole],
        [SMEM] + [VMEM] * 9,
        8 * heads * tokens * tokens * DH + small,
        20 * tokens * width,
    )(order, queries, key_vectors, values, grad_low, scores, *prefix)

    grad_keys, grad_values, mixed = call(
        functools.partial(finish_kernel, per_quarter),
        [whole_low, whole_low, whole_low],
        [SMEM] + [VMEM] * 10,
        2 * small,
        20 * tokens * width,
    )(order, key_vectors, values, local_keys, local_values, own_part, other_part, *suffix)

    gains = jnp.stack([gain_of(part, rows, per_quarter) for part in suffix])
    natural = jnp.zeros_like(gains)
    for t in range(QUAD):
        for j in range(QUAD):
            natural = natural.at[t].add(jnp.where((quarter ^ j) == t, gains[j], 0.0))
    return mixed, grad_queries, grad_keys, grad_values, natural.reshape(width)


def solution(mesh):
    placed = (
        P(("parts", "seq"), "tensor"),
        P(("parts", "seq"), "tensor"),
        P(("parts", "seq"), "tensor"),
        P("tensor", None),
        P("tensor"),
        P(("parts", "seq"), "tensor"),
    )
    return jax.shard_map(
        on_device,
        mesh=mesh,
        in_specs=placed,
        out_specs=(
            P(("parts", "seq"), "tensor"),
            P(("parts", "seq"), "tensor"),
            P(("parts", "seq"), "tensor"),
            P(("parts", "seq"), "tensor"),
            P(("parts", "tensor")),
        ),
        check_vma=False,
    )
```

time: 165 us -> 72.6 us (0.44)
  waiting for transfers between devices: 88.1 us -> 11.6 us
  blocking collectives: 29.9 us -> 0 us
  Pallas kernels: 0 us -> 21.9 us
  starting transfers between devices: 0.12 us -> 19.1 us
  matrix products: 15.9 us -> 0 us
  between operations: 14 us -> 0.99 us
  local copies, waits for them, and re-layouts: 5.32 us -> 14.1 us
  other arithmetic: 10.7 us -> 3.85 us
    all_gather x2 -> x0, waiting for transfers between devices: 88 us -> none  [entering(): gathered = lax.all_gather(shard.astype(jnp.bfloat16), axis)]
    psum x1 -> x0, blocking collectives: 27.1 us -> none  [on_device(): grad_gain = lax.psum(gain_term, 'seq')]
    pallas_call x0 -> x8, Pallas kernels: none -> 21.9 us  [the longest x2 8.33 us: project(): pl.pallas_call(body, out_shape=shaped((tokens, half), dtype), grid_spec=p...]
    ppermute x0 -> x16, starting transfers between devices: none -> 19.1 us  [the longest x14 19.1 us: swap(): return lax.ppermute(array, 'seq', [(i, i ^ flip) for i in range(count)])]
    dot_general x20 -> x0, matrix products: 15.9 us -> none  [the longest x1 2.25 us: on_device(): jnp.einsum('thd,the->hde', key_heads, value_heads, preferred_element_type...]
    ppermute x0 -> x16, waiting for transfers between devices: none -> 11.6 us  [the longest x14 11.6 us: swap(): return lax.ppermute(array, 'seq', [(i, i ^ flip) for i in range(count)])]
    unnamed x16 -> x62, local copies, waits for them, and re-layouts: 2.54 us -> 13.2 us
    add x7 -> x0, other arithmetic: 7.49 us -> none  [add_states(): return earlier + later]
  transfers between devices with their start and end apart: 3 -> 16, of which waited for: 2 -> 9; matrix products, arithmetic and copies ran while one was open for 7% -> 7% of each run, Pallas kernels for 0% -> 18%
where the time goes in v1:
time: 72.6 us; the launch traced here: 71.6 us
  Pallas kernels  21.9 us (30%)
  starting transfers between devices  19.1 us (26%)
  local copies, waits for them, and re-layouts  14.1 us (19%)
  waiting for transfers between devices  11.6 us (16%)
  other arithmetic  3.85 us (5%)
  between operations  0.99 us (1%)
    ppermute x14, starting transfers between devices, swap(): return lax.ppermute(array, 'seq', [(i, i ^ flip) for i in range(count)])  19.1 us
    unnamed x62, local copies, waits for them, and re-layouts  13.2 us
    ppermute x14, waiting for transfers between devices, swap(): return lax.ppermute(array, 'seq', [(i, i ^ flip) for i in range(count)])  11.6 us
    pallas_call x2, Pallas kernels, project(): pl.pallas_call(body, out_shape=shaped((tokens, half), dtype), grid_spec=p...  8.33 us
    pallas_call x1, Pallas kernels, back_project(): pl.pallas_call(back_kernel, out_shape=shaped((tokens, rows), wide), grid_...  5.14 us
    pallas_call x1, Pallas kernels, on_device(): call(functools.partial(grad_kernel, per_quarter), [whole_low, whole, whol...  3.03 us
    pallas_call x1, Pallas kernels, on_device(): call(functools.partial(finish_kernel, per_quarter), [whole_low, whole_low...  2.47 us
    convert_element_type x3, other arithmetic, pack(): return jnp.concatenate([state.astype(low), pairs, spare], axis=0)  1.91 us
  transfers between devices with their start and end apart: 16, of which 9 were waited for; matrix products, arithmetic and copies ran while one was open for 7% of the time, Pallas kernels for 18%

profile of v1, /device:TPU:0, one launch (start us, length us, event | category | flops | bytes accessed | tf_op | source)
XLA Modules:
  0.0 71.6 jit_solution(5750109481900537125)
XLA Ops:
  1.6 1.0 %copy-done.3 = bf16[192,1024]{1,0:T(8,128)(2,1)S(1)} copy-done((bf16[192,1024]{1,0:T(8,128)(2,1)S(1)}, bf16[192,1024]{1,0:T(8,128)(2,1)}, u32[]{:S(2)}) %copy-start.3) | copy-done | bytes 393240
  3.1 3.0 %collective-permute-start.1 = (bf16[256,128]{1,0:T(8,128)(2,1)S(1)}, bf16[256,128]{1,0:T(8,128)(2,1)S(1)}, u32[]{:S(2)}, u32[]{:S(2)}) collective-permute-start(bf16[256,128]{1,0:T(8,128)(2,1)S(1)} %get-tuple-element.217), channel_id=1, source_target_pairs={{0,2},{2,0},{4,6},{6,4},{8,10},{10,8},{12,14},{14,12},{1,3},{3,1},... | collective-permute-start | bytes 196616 | tf_op jit(solution)/shard_map/ppermute | solution.py:195
  6.1 1.6 %collective-permute-start.2 = (bf16[256,128]{1,0:T(8,128)(2,1)S(1)}, bf16[256,128]{1,0:T(8,128)(2,1)S(1)}, u32[]{:S(2)}, u32[]{:S(2)}) collective-permute-start(bf16[256,128]{1,0:T(8,128)(2,1)S(1)} %get-tuple-element.218), channel_id=1, source_target_pairs={{0,4},{2,6},{4,0},{6,2},{8,12},{10,14},{12,8},{14,10},{1,5},{3,7},... | collective-permute-start | bytes 196616 | tf_op jit(solution)/shard_map/ppermute | solution.py:195
  8.3 2.5 %collective-permute-done.2 = bf16[256,128]{1,0:T(8,128)(2,1)S(1)} collective-permute-done((bf16[256,128]{1,0:T(8,128)(2,1)S(1)}, bf16[256,128]{1,0:T(8,128)(2,1)S(1)}, u32[]{:S(2)}, u32[]{:S(2)}) %collective-permute-start.2) | collective-permute-done | bytes 65568 | tf_op jit(solution)/shard_map/ppermute | solution.py:195
  10.9 1.9 %collective-permute-done.3 = bf16[256,128]{1,0:T(8,128)(2,1)S(1)} collective-permute-done((bf16[256,128]{1,0:T(8,128)(2,1)S(1)}, bf16[256,128]{1,0:T(8,128)(2,1)S(1)}, u32[]{:S(2)}, u32[]{:S(2)}) %collective-permute-start.3) | collective-permute-done | bytes 65568 | tf_op jit(solution)/shard_map/ppermute | solution.py:195
  12.9 2.7 %collective-permute-start.4 = (bf16[256,128]{1,0:T(8,128)(2,1)S(1)}, bf16[256,128]{1,0:T(8,128)(2,1)S(1)}, u32[]{:S(2)}, u32[]{:S(2)}) collective-permute-start(bf16[256,128]{1,0:T(8,128)(2,1)S(1)} %fusion.16), channel_id=1, source_target_pairs={{0,8},{2,10},{4,12},{6,14},{8,0},{10,2},{12,4},{14,6},{1,9},{3,11}... | collective-permute-start | bytes 196616 | tf_op jit(solution)/shard_map/ppermute | solution.py:195
  15.6 1.0 %copy-done.1 = bf16[192,1024]{1,0:T(8,128)(2,1)S(1)} copy-done((bf16[192,1024]{1,0:T(8,128)(2,1)S(1)}, bf16[192,1024]{1,0:T(8,128)(2,1)}, u32[]{:S(2)}) %copy-start.1) | copy-done | bytes 393240
  16.6 1.0 %copy-done.4 = bf16[192,1024]{1,0:T(8,128)(2,1)S(1)} copy-done((bf16[192,1024]{1,0:T(8,128)(2,1)S(1)}, bf16[192,1024]{1,0:T(8,128)(2,1)}, u32[]{:S(2)}) %copy-start.4) | copy-done | bytes 393240
  21.5 2.2 %collective-permute-start.7 = (bf16[256,128]{1,0:T(8,128)(2,1)S(1)}, bf16[256,128]{1,0:T(8,128)(2,1)S(1)}, u32[]{:S(2)}, u32[]{:S(2)}) collective-permute-start(bf16[256,128]{1,0:T(8,128)(2,1)S(1)} %get-tuple-element.261), channel_id=1, source_target_pairs={{0,6},{2,4},{4,2},{6,0},{8,14},{10,12},{12,10},{14,8},{1,7},{3,5},... | collective-permute-start | bytes 196616 | tf_op jit(solution)/shard_map/ppermute | solution.py:195
  23.7 5.1 %shard_map.102.grad_ref = f32[192,1024]{1,0:T(8,128)} custom-call(s32[1]{0:T(128)} %bitcast.1.side_ref, bf16[192,1024]{1,0:T(8,128)(2,1)} %own_ref.1, bf16[192,1024]{1,0:T(8,128)(2,1)} %collective-permute-done.other_ref, bf16[1024,2048]{1,0:T(8,128)(2,1)} %weight_ref.5), custom_call_target="tpu_custom_call" | custom-call | flops 805306368 | bytes 4194304 | tf_op jit(solution)/shard_map/pallas_call | solution.py:174
  28.9 1.2 %copy-done.8 = f32[192,1024]{1,0:T(8,128)S(1)} copy-done((f32[192,1024]{1,0:T(8,128)S(1)}, f32[192,1024]{1,0:T(8,128)}, u32[]{:S(2)}) %copy-start.8) | copy-done | bytes 786456
  30.2 1.7 %shard_map.104 = (bf16[192,1024]{1,0:T(8,128)(2,1)S(1)}, bf16[192,1024]{1,0:T(8,128)(2,1)S(1)}, bf16[272,128]{1,0:T(8,128)(2,1)S(1)}, bf16[272,128]{1,0:T(8,128)...) custom-call(s32[1]{0:T(128)} %bitcast.place_ref, bf16[192,1024]{1,0:T(8,128)(2,1)S(1)} %copy-done.7, ...), custom_call_target="tpu_custom_call" | custom-call | flops 100663296 | bytes 2752512 | tf_op jit(solution)/shard_map/pallas_call | solution.py:284
  33.4 4.1 %shard_map.107 = bf16[192,1024]{1,0:T(8,128)(2,1)} custom-call(s32[1]{0:T(128)S(6)} %sub.14.side_ref, bf16[192,1024]{1,0:T(8,128)(2,1)} %copy-done.10, bf16[1024,2048]{1,0:T(8,128)(2,1)} %weight_ref.5), custom_call_target="tpu_custom_call" | custom-call | flops 402653184 | bytes 2097152 | tf_op jit(solution)/shard_map/pallas_call | solution.py:152
  38.3 1.3 %collective-permute-start.10 = (bf16[272,128]{1,0:T(8,128)(2,1)S(1)}, bf16[272,128]{1,0:T(8,128)(2,1)S(1)}, u32[]{:S(2)}, u32[]{:S(2)}) collective-permute-start(bf16[272,128]{1,0:T(8,128)(2,1)S(1)} %get-tuple-element.227), channel_id=1, source_target_pairs={{0,4},{2,6},{4,0},{6,2},{8,12},{10,14},{12,8},{14,10},{1,5},{3,7},... | collective-permute-start | bytes 208904 | tf_op jit(solution)/shard_map/ppermute | solution.py:195
  39.5 1.5 %collective-permute-start.9 = (bf16[272,128]{1,0:T(8,128)(2,1)S(1)}, bf16[272,128]{1,0:T(8,128)(2,1)S(1)}, u32[]{:S(2)}, u32[]{:S(2)}) collective-permute-start(bf16[272,128]{1,0:T(8,128)(2,1)S(1)} %get-tuple-element.226), channel_id=1, source_target_pairs={{0,2},{2,0},{4,6},{6,4},{8,10},{10,8},{12,14},{14,12},{1,3},{3,1},... | collective-permute-start | bytes 208904 | tf_op jit(solution)/shard_map/ppermute | solution.py:195
  41.1 2.4 %collective-permute-done.11 = bf16[272,128]{1,0:T(8,128)(2,1)S(1)} collective-permute-done((bf16[272,128]{1,0:T(8,128)(2,1)S(1)}, bf16[272,128]{1,0:T(8,128)(2,1)S(1)}, u32[]{:S(2)}, u32[]{:S(2)}) %collective-permute-start.11) | collective-permute-done | bytes 69664 | tf_op jit(solution)/shard_map/ppermute | solution.py:195
  45.3 1.3 %collective-permute-start.12 = (bf16[272,128]{1,0:T(8,128)(2,1)}, bf16[272,128]{1,0:T(8,128)(2,1)}, u32[]{:S(2)}, u32[]{:S(2)}) collective-permute-start(bf16[272,128]{1,0:T(8,128)(2,1)} %maximum_maximum_fusion), channel_id=1, source_target_pairs={{0,8},{2,10},{4,12},{6,14},{8,0},{10,2},{12,4},{14,6},{1,9},{3,11}... | collective-permute-start | bytes 208904 | tf_op jit(solution)/shard_map/ppermute | solution.py:195
  51.0 3.0 %shard_map.105 = (bf16[192,1024]{1,0:T(8,128)(2,1)}, f32[192,1024]{1,0:T(8,128)S(1)}, f32[192,1024]{1,0:T(8,128)S(1)}) custom-call(s32[1]{0:T(128)} %bitcast.place_ref, bf16[192,1024]{1,0:T(8,128)(2,1)S(1)} %copy-done.7, bf16[192,1024]{1,0:T(8,128)(2,1)S(1)} %copy-done.2, bf16[192,1024]{1,0:T(8,128)(2,1)S(1)} %copy-done.5, bf16[192,1024]{1,0:T(8,128)(2,1)S(1)} %copy-done.16, ...), custom_call_target="tpu_custom_call" | custom-call | flops 352321536 | bytes 3932160 | tf_op jit(solution)/shard_map/pallas_call | solution.py:296
  54.0 4.2 %shard_map.106.own_ref = f32[192,1024]{1,0:T(8,128)} custom-call(s32[1]{0:T(128)} %bitcast.1.side_ref, bf16[192,1024]{1,0:T(8,128)(2,1)} %copy-done.10, bf16[1024,2048]{1,0:T(8,128)(2,1)} %weight_ref.5), custom_call_target="tpu_custom_call" | custom-call | flops 402653184 | bytes 2097152 | tf_op jit(solution)/shard_map/pallas_call | solution.py:152
  62.5 2.1 %collective-permute-start.15 = (bf16[272,128]{1,0:T(8,128)(2,1)S(1)}, bf16[272,128]{1,0:T(8,128)(2,1)S(1)}, u32[]{:S(2)}, u32[]{:S(2)}) collective-permute-start(bf16[272,128]{1,0:T(8,128)(2,1)S(1)} %get-tuple-element.267), channel_id=1, source_target_pairs={{0,6},{2,4},{4,2},{6,0},{8,14},{10,12},{12,10},{14,8},{1,7},{3,5},... | collective-permute-start | bytes 208904 | tf_op jit(solution)/shard_map/ppermute | solution.py:195
  64.6 1.6 %collective-permute-done.13.s1 = bf16[272,128]{1,0:T(8,128)(2,1)S(1)} collective-permute-done((bf16[272,128]{1,0:T(8,128)(2,1)S(1)}, bf16[272,128]{1,0:T(8,128)(2,1)S(1)}, u32[]{:S(2)}, u32[]{:S(2)}) %collective-permute-start.13) | collective-permute-done | bytes 69664 | tf_op jit(solution)/shard_map/ppermute | solution.py:195
  66.3 1.4 %collective-permute-done.15.s3 = bf16[272,128]{1,0:T(8,128)(2,1)S(1)} collective-permute-done((bf16[272,128]{1,0:T(8,128)(2,1)S(1)}, bf16[272,128]{1,0:T(8,128)(2,1)S(1)}, u32[]{:S(2)}, u32[]{:S(2)}) %collective-permute-start.15) | collective-permute-done | bytes 69664 | tf_op jit(solution)/shard_map/ppermute | solution.py:195
  68.0 1.1 %copy-done.9 = f32[192,1024]{1,0:T(8,128)S(1)} copy-done((f32[192,1024]{1,0:T(8,128)S(1)}, f32[192,1024]{1,0:T(8,128)}, u32[]{:S(2)}) %copy-start.9) | copy-done | bytes 786456
  69.1 2.5 %shard_map.108 = (bf16[192,1024]{1,0:T(8,128)(2,1)}, bf16[192,1024]{1,0:T(8,128)(2,1)}, bf16[192,1024]{1,0:T(8,128)(2,1)}) custom-call(s32[1]{0:T(128)} %bitcast.place_ref, bf16[192,1024]{1,0:T(8,128)(2,1)S(1)} %copy-done.2, bf16[192,1024]{1,0:T(8,128)(2,1)S(1)} %copy-done.5, f32[192,1024]{1,0:T(8,128)S(1)} %get-tuple-element.222.local_key_ref, ...), custom_call_target="tpu_custom_call" | custom-call | flops 100663296 | bytes 3932160 | tf_op jit(solution)/shard_map/pallas_call | solution.py:304
  (128 shorter events, 19.1 us)
Async XLA Ops:
  2.6 26.3 %copy-start.7 = (bf16[192,1024]{1,0:T(8,128)(2,1)S(1)}, bf16[192,1024]{1,0:T(8,128)(2,1)}, u32[]{:S(2)}) copy-start(bf16[192,1024]{1,0:T(8,128)(2,1)} %query_ref.5) | copy-start | bytes 1179652
  2.6 26.3 %copy-start.23 = (f32[1024]{0:T(1024)S(1)}, f32[1024]{0:T(1024)}, u32[]{:S(2)}) copy-start(f32[1024]{0:T(1024)} %param.42) | copy-start | bytes 12292
  3.1 5.3 %collective-permute-start.1 = (bf16[256,128]{1,0:T(8,128)(2,1)S(1)}, bf16[256,128]{1,0:T(8,128)(2,1)S(1)}, u32[]{:S(2)}, u32[]{:S(2)}) collective-permute-start(bf16[256,128]{1,0:T(8,128)(2,1)S(1)} %get-tuple-element.217), channel_id=1, source_target_pairs={{0,2},{2,0},{4,6},{6,4},{8,10},{10,8},{12,14},{14,12},{1,3},{3,1},... | collective-permute-start | bytes 196616 | tf_op jit(solution)/shard_map/ppermute | solution.py:195
  6.1 4.8 %collective-permute-start.2 = (bf16[256,128]{1,0:T(8,128)(2,1)S(1)}, bf16[256,128]{1,0:T(8,128)(2,1)S(1)}, u32[]{:S(2)}, u32[]{:S(2)}) collective-permute-start(bf16[256,128]{1,0:T(8,128)(2,1)S(1)} %get-tuple-element.218), channel_id=1, source_target_pairs={{0,4},{2,6},{4,0},{6,2},{8,12},{10,14},{12,8},{14,10},{1,5},{3,7},... | collective-permute-start | bytes 196616 | tf_op jit(solution)/shard_map/ppermute | solution.py:195
  7.7 5.2 %collective-permute-start.3 = (bf16[256,128]{1,0:T(8,128)(2,1)S(1)}, bf16[256,128]{1,0:T(8,128)(2,1)S(1)}, u32[]{:S(2)}, u32[]{:S(2)}) collective-permute-start(bf16[256,128]{1,0:T(8,128)(2,1)S(1)} %get-tuple-element.219), channel_id=1, source_target_pairs={{0,6},{2,4},{4,2},{6,0},{8,14},{10,12},{12,10},{14,8},{1,7},{3,5},... | collective-permute-start | bytes 196616 | tf_op jit(solution)/shard_map/ppermute | solution.py:195
  7.7 16.0 %collective-permute-start = (bf16[192,1024]{1,0:T(8,128)(2,1)}, bf16[192,1024]{1,0:T(8,128)(2,1)}, u32[]{:S(2)}, u32[]{:S(2)}) collective-permute-start(bf16[192,1024]{1,0:T(8,128)(2,1)} %own_ref.1), channel_id=1, source_target_pairs={{0,1},{1,0},{2,3},{3,2},{4,5},{5,4},{6,7},{7,6},{8,9},{9,8},{10,11... | collective-permute-start | bytes 1179656 | tf_op jit(solution)/shard_map/ppermute | solution.py:199
  12.9 6.5 %collective-permute-start.4 = (bf16[256,128]{1,0:T(8,128)(2,1)S(1)}, bf16[256,128]{1,0:T(8,128)(2,1)S(1)}, u32[]{:S(2)}, u32[]{:S(2)}) collective-permute-start(bf16[256,128]{1,0:T(8,128)(2,1)S(1)} %fusion.16), channel_id=1, source_target_pairs={{0,8},{2,10},{4,12},{6,14},{8,0},{10,2},{12,4},{14,6},{1,9},{3,11}... | collective-permute-start | bytes 196616 | tf_op jit(solution)/shard_map/ppermute | solution.py:195
  20.2 17.3 %copy-start.11 = (bf16[256,128]{1,0:T(8,128)(2,1)}, bf16[256,128]{1,0:T(8,128)(2,1)S(1)}, u32[]{:S(2)}) copy-start(bf16[256,128]{1,0:T(8,128)(2,1)S(1)} %get-tuple-element.262.p0) | copy-start | bytes 196612
  20.2 8.6 %collective-permute-start.5 = (bf16[256,128]{1,0:T(8,128)(2,1)}, bf16[256,128]{1,0:T(8,128)(2,1)S(1)}, u32[]{:S(2)}, u32[]{:S(2)}) collective-permute-start(bf16[256,128]{1,0:T(8,128)(2,1)} %get-tuple-element.263), channel_id=1, source_target_pairs={{0,2},{2,0},{4,6},{6,4},{8,10},{10,8},{12,14},{14,12},{1,3},{3,1},... | collective-permute-start | bytes 196616 | tf_op jit(solution)/shard_map/ppermute | solution.py:195
  20.7 8.2 %collective-permute-start.6 = (bf16[256,128]{1,0:T(8,128)(2,1)S(1)}, bf16[256,128]{1,0:T(8,128)(2,1)S(1)}, u32[]{:S(2)}, u32[]{:S(2)}) collective-permute-start(bf16[256,128]{1,0:T(8,128)(2,1)S(1)} %get-tuple-element.264), channel_id=1, source_target_pairs={{0,4},{2,6},{4,0},{6,2},{8,12},{10,14},{12,8},{14,10},{1,5},{3,7},... | collective-permute-start | bytes 196616 | tf_op jit(solution)/shard_map/ppermute | solution.py:195
  21.5 7.4 %collective-permute-start.7 = (bf16[256,128]{1,0:T(8,128)(2,1)S(1)}, bf16[256,128]{1,0:T(8,128)(2,1)S(1)}, u32[]{:S(2)}, u32[]{:S(2)}) collective-permute-start(bf16[256,128]{1,0:T(8,128)(2,1)S(1)} %get-tuple-element.261), channel_id=1, source_target_pairs={{0,6},{2,4},{4,2},{6,0},{8,14},{10,12},{12,10},{14,8},{1,7},{3,5},... | collective-permute-start | bytes 196616 | tf_op jit(solution)/shard_map/ppermute | solution.py:195
  28.9 17.8 %copy-start.2 = (bf16[192,1024]{1,0:T(8,128)(2,1)S(1)}, bf16[192,1024]{1,0:T(8,128)(2,1)}, u32[]{:S(2)}) copy-start(bf16[192,1024]{1,0:T(8,128)(2,1)} %key_ref.7) | copy-start | bytes 1179652
  28.9 17.8 %copy-start.5 = (bf16[192,1024]{1,0:T(8,128)(2,1)S(1)}, bf16[192,1024]{1,0:T(8,128)(2,1)}, u32[]{:S(2)}) copy-start(bf16[192,1024]{1,0:T(8,128)(2,1)} %value_ref.7) | copy-start | bytes 1179652
  28.9 17.7 %copy-start.17 = (bf16[256,128]{1,0:T(8,128)(2,1)}, bf16[256,128]{1,0:T(8,128)(2,1)S(1)}, u32[]{:S(2)}) copy-start(bf16[256,128]{1,0:T(8,128)(2,1)S(1)} %collective-permute-done.5.p1) | copy-start | bytes 196612
  28.9 17.7 %copy-start.19 = (bf16[256,128]{1,0:T(8,128)(2,1)}, bf16[256,128]{1,0:T(8,128)(2,1)S(1)}, u32[]{:S(2)}) copy-start(bf16[256,128]{1,0:T(8,128)(2,1)S(1)} %collective-permute-done.6.p2) | copy-start | bytes 196612
  28.9 17.7 %copy-start.21 = (bf16[256,128]{1,0:T(8,128)(2,1)}, bf16[256,128]{1,0:T(8,128)(2,1)S(1)}, u32[]{:S(2)}) copy-start(bf16[256,128]{1,0:T(8,128)(2,1)S(1)} %collective-permute-done.7.p3) | copy-start | bytes 196612
  37.5 30.5 %collective-permute-start.8 = (bf16[192,1024]{1,0:T(8,128)(2,1)}, bf16[192,1024]{1,0:T(8,128)(2,1)}, u32[]{:S(2)}, u32[]{:S(2)}) collective-permute-start(bf16[192,1024]{1,0:T(8,128)(2,1)} %shard_map.107), channel_id=1, source_target_pairs={{0,1},{1,0},{2,3},{3,2},{4,5},{5,4},{6,7},{7,6},{8,9},{9,8},{10,11... | collective-permute-start | bytes 1179656 | tf_op jit(solution)/shard_map/ppermute | solution.py:199
  37.5 5.9 %collective-permute-start.11 = (bf16[272,128]{1,0:T(8,128)(2,1)S(1)}, bf16[272,128]{1,0:T(8,128)(2,1)S(1)}, u32[]{:S(2)}, u32[]{:S(2)}) collective-permute-start(bf16[272,128]{1,0:T(8,128)(2,1)S(1)} %get-tuple-element.228), channel_id=1, source_target_pairs={{0,6},{2,4},{4,2},{6,0},{8,14},{10,12},{12,10},{14,8},{1,7},{3,5},... | collective-permute-start | bytes 208904 | tf_op jit(solution)/shard_map/ppermute | solution.py:195
  38.3 5.3 %collective-permute-start.10 = (bf16[272,128]{1,0:T(8,128)(2,1)S(1)}, bf16[272,128]{1,0:T(8,128)(2,1)S(1)}, u32[]{:S(2)}, u32[]{:S(2)}) collective-permute-start(bf16[272,128]{1,0:T(8,128)(2,1)S(1)} %get-tuple-element.227), channel_id=1, source_target_pairs={{0,4},{2,6},{4,0},{6,2},{8,12},{10,14},{12,8},{14,10},{1,5},{3,7},... | collective-permute-start | bytes 208904 | tf_op jit(solution)/shard_map/ppermute | solution.py:195
  39.5 5.0 %collective-permute-start.9 = (bf16[272,128]{1,0:T(8,128)(2,1)S(1)}, bf16[272,128]{1,0:T(8,128)(2,1)S(1)}, u32[]{:S(2)}, u32[]{:S(2)}) collective-permute-start(bf16[272,128]{1,0:T(8,128)(2,1)S(1)} %get-tuple-element.226), channel_id=1, source_target_pairs={{0,2},{2,0},{4,6},{6,4},{8,10},{10,8},{12,14},{14,12},{1,3},{3,1},... | collective-permute-start | bytes 208904 | tf_op jit(solution)/shard_map/ppermute | solution.py:195
  45.3 13.0 %collective-permute-start.12 = (bf16[272,128]{1,0:T(8,128)(2,1)}, bf16[272,128]{1,0:T(8,128)(2,1)}, u32[]{:S(2)}, u32[]{:S(2)}) collective-permute-start(bf16[272,128]{1,0:T(8,128)(2,1)} %maximum_maximum_fusion), channel_id=1, source_target_pairs={{0,8},{2,10},{4,12},{6,14},{8,0},{10,2},{12,4},{14,6},{1,9},{3,11}... | collective-permute-start | bytes 208904 | tf_op jit(solution)/shard_map/ppermute | solution.py:195
  61.1 5.1 %collective-permute-start.13 = (bf16[272,128]{1,0:T(8,128)(2,1)S(1)}, bf16[272,128]{1,0:T(8,128)(2,1)S(1)}, u32[]{:S(2)}, u32[]{:S(2)}) collective-permute-start(bf16[272,128]{1,0:T(8,128)(2,1)S(1)} %get-tuple-element.268), channel_id=1, source_target_pairs={{0,2},{2,0},{4,6},{6,4},{8,10},{10,8},{12,14},{14,12},{1,3},{3,1},... | collective-permute-start | bytes 208904 | tf_op jit(solution)/shard_map/ppermute | solution.py:195
  62.0 4.3 %collective-permute-start.14 = (bf16[272,128]{1,0:T(8,128)(2,1)S(1)}, bf16[272,128]{1,0:T(8,128)(2,1)S(1)}, u32[]{:S(2)}, u32[]{:S(2)}) collective-permute-start(bf16[272,128]{1,0:T(8,128)(2,1)S(1)} %get-tuple-element.269), channel_id=1, source_target_pairs={{0,4},{2,6},{4,0},{6,2},{8,12},{10,14},{12,8},{14,10},{1,5},{3,7},... | collective-permute-start | bytes 208904 | tf_op jit(solution)/shard_map/ppermute | solution.py:195
  62.5 5.2 %collective-permute-start.15 = (bf16[272,128]{1,0:T(8,128)(2,1)S(1)}, bf16[272,128]{1,0:T(8,128)(2,1)S(1)}, u32[]{:S(2)}, u32[]{:S(2)}) collective-permute-start(bf16[272,128]{1,0:T(8,128)(2,1)S(1)} %get-tuple-element.267), channel_id=1, source_target_pairs={{0,6},{2,4},{4,2},{6,0},{8,14},{10,12},{12,10},{14,8},{1,7},{3,5},... | collective-permute-start | bytes 208904 | tf_op jit(solution)/shard_map/ppermute | solution.py:195
  (23 other events, 58.4 us)

commit v2 on v1

v2 whole, which is shorter than its diff:
```python
import functools

import jax
import jax.numpy as jnp
from jax import lax
from jax.experimental import pallas as pl
from jax.experimental.pallas import tpu as pltpu
from jax.sharding import PartitionSpec as P

DH = 128
QUAD = 4
EXTRA = 16
CHUNK = 512
COST = 1000
EPSILON = 1e-05
wide = jnp.float32
low = jnp.bfloat16
VMEM = pl.BlockSpec(memory_space=pltpu.VMEM)
SMEM = pl.BlockSpec(memory_space=pltpu.SMEM)
HBM = pl.BlockSpec(memory_space=pltpu.HBM)
FREE = pl.BlockSpec(memory_space=pltpu.VMEM)


def dot(a, b, over):
    return lax.dot_general(a, b, (((over[0],), (over[1],)), ((), ())), preferred_element_type=wide)


def shaped(shape, dtype):
    return jax.ShapeDtypeStruct(shape, dtype)


def call(body, outs, ins, out_specs=None, scratch=(), room=6):
    out_specs = out_specs or [VMEM] * len(outs)
    placed = [
        pltpu.VMEM(out.shape, out.dtype) if spec is VMEM else out for out, spec in zip(outs, out_specs)
    ]
    kernel = pl.pallas_call(
        body,
        out_shape=placed,
        in_specs=[VMEM if spec is FREE else spec for spec in ins],
        out_specs=[VMEM if spec is FREE else spec for spec in out_specs],
        scratch_shapes=list(scratch),
        cost_estimate=pl.CostEstimate(flops=COST, bytes_accessed=COST, transcendentals=0),
        compiler_params=pltpu.CompilerParams(vmem_limit_bytes=room * 2**20),
    )

    def pinned(*operands):
        spaces = {id(VMEM): pltpu.VMEM, id(HBM): pltpu.HBM}
        fixed = [
            pltpu.with_memory_space_constraint(operand, spaces[id(spec)]) if id(spec) in spaces else operand
            for operand, spec in zip(operands, ins, strict=True)
        ]
        return kernel(*fixed)

    return pinned


def head_slices(place, per_quarter):
    for j in range(QUAD):
        for i in range(per_quarter):
            start = ((place ^ j) * per_quarter + i) * DH
            yield j, i, pl.ds(pl.multiple_of(start, DH), DH)


def state_kernel(per_quarter, place_ref, key_hbm, value_hbm, *rest):
    out_refs, key_ref, value_ref, sems = rest[:QUAD], rest[QUAD], rest[QUAD + 1], rest[QUAD + 2]
    copies = [
        pltpu.make_async_copy(key_hbm, key_ref, sems.at[0]),
        pltpu.make_async_copy(value_hbm, value_ref, sems.at[1]),
    ]
    for copy in copies:
        copy.start()
    for copy in copies:
        copy.wait()
    for j, i, head in head_slices(place_ref[0], per_quarter):
        state = dot(key_ref[:, head], value_ref[:, head], (0, 0))
        out_refs[j][i * DH : (i + 1) * DH, :] = state.astype(low)


def causal(tokens):
    rows = lax.broadcasted_iota(jnp.int32, (tokens, tokens), 0)
    columns = lax.broadcasted_iota(jnp.int32, (tokens, tokens), 1)
    return rows >= columns


def local_kernel(heads, query_hbm, key_ref, value_ref, local_ref, query_ref, sems):
    copy = pltpu.make_async_copy(query_hbm, query_ref, sems.at[0])
    copy.start()
    keep = causal(query_ref.shape[0])
    copy.wait()
    for h in range(heads):
        head = slice(h * DH, (h + 1) * DH)
        scores = dot(query_ref[:, head], key_ref[:, head], (1, 1))
        scores = jnp.where(keep, scores, 0.0).astype(low)
        local_ref[:, head] = dot(scores, value_ref[:, head], (1, 0))


def norm_kernel(
    per_quarter, place_ref, query_ref, local_ref, grad_ref, gain_ref, p0, p1, p2, p3,
    normed_ref, low_ref, *out_refs
):
    prefix = (p0, p1, p2, p3)
    for j, i, head in head_slices(place_ref[0], per_quarter):
        rows = slice(i * DH, (i + 1) * DH)
        query = query_ref[:, head]
        attention = local_ref[:, head] + dot(query, prefix[j][rows, :], (1, 0))
        inverse = lax.rsqrt(jnp.mean(attention * attention, axis=-1, keepdims=True) + EPSILON)
        scaled = attention * inverse
        gain = gain_ref[:, head]
        normed_ref[:, head] = (scaled * gain).astype(low)
        grad = grad_ref[:, head]
        gain_term = jnp.sum(grad * scaled, axis=0, keepdims=True)
        gained = grad * gain
        inner = jnp.mean(gained * scaled, axis=-1, keepdims=True)
        grad_low = (inverse * (gained - scaled * inner)).astype(low)
        low_ref[:, head] = grad_low
        out_refs[j][rows, :] = dot(query, grad_low, (0, 0)).astype(low)
        if i == 0:
            out_refs[j][per_quarter * DH :, :] = jnp.zeros((EXTRA, DH), low)
        put_pair(out_refs[j], per_quarter, i, gain_term)


def grad_kernel(
    per_quarter, place_ref, query_ref, key_ref, value_ref, low_ref, p0, p1, p2, p3,
    grad_query_ref, grad_key_ref, grad_value_ref
):
    prefix = (p0, p1, p2, p3)
    keep = causal(query_ref.shape[0])
    for j, i, head in head_slices(place_ref[0], per_quarter):
        rows = slice(i * DH, (i + 1) * DH)
        grad_low = low_ref[:, head]
        raw = dot(grad_low, value_ref[:, head], (1, 1))
        grad_scores = jnp.where(keep, raw, 0.0).astype(low)
        grad_query = dot(grad_scores, key_ref[:, head], (1, 0))
        grad_query = grad_query + dot(grad_low, prefix[j][rows, :], (1, 1))
        grad_query_ref[:, head] = grad_query.astype(low)
        grad_key_ref[:, head] = dot(grad_scores, query_ref[:, head], (0, 0)).astype(low)
        scores = dot(query_ref[:, head], key_ref[:, head], (1, 1))
        scores = jnp.where(keep, scores, 0.0).astype(low)
        grad_value_ref[:, head] = dot(scores, grad_low, (0, 0)).astype(low)


def finish_kernel(
    per_quarter, place_ref, key_ref, value_ref, local_key_ref, local_value_ref,
    s0, s1, s2, s3, grad_key_hbm, grad_value_hbm, gain_ref, key_out, value_out, sems
):
    suffix = (s0, s1, s2, s3)
    copies = []
    for j, i, head in head_slices(place_ref[0], per_quarter):
        rows = slice(i * DH, (i + 1) * DH)
        slot = j * per_quarter + i
        state = suffix[j][rows, :]
        grad_key = local_key_ref[:, head].astype(wide) + dot(value_ref[:, head], state, (1, 1))
        key_out[:, head] = grad_key.astype(low)
        grad_value = local_value_ref[:, head].astype(wide) + dot(key_ref[:, head], state, (1, 0))
        value_out[:, head] = grad_value.astype(low)
        copies.append(pltpu.make_async_copy(key_out.at[:, head], grad_key_hbm.at[:, head], sems.at[0, slot]))
        copies.append(pltpu.make_async_copy(value_out.at[:, head], grad_value_hbm.at[:, head], sems.at[1, slot]))
        for copy in copies[-2:]:
            copy.start()
        gain_ref[:, head] = pair_sum(suffix[j], per_quarter, i)
    for copy in copies:
        copy.wait()


def pair_sum(ref, per_quarter, i):
    base = per_quarter * DH + 2 * i
    return ref[base : base + 1, :].astype(wide) + ref[base + 1 : base + 2, :].astype(wide)


def put_pair(ref, per_quarter, i, gain):
    base = per_quarter * DH + 2 * i
    upper = gain.astype(low)
    ref[base : base + 1, :] = upper
    ref[base + 1 : base + 2, :] = (gain - upper.astype(wide)).astype(low)


def back_kernel(side_ref, own_hbm, other_ref, weight_hbm, out_ref, own_ref, weight_ref, own_sem, sems):
    width = own_ref.shape[1]
    own = pl.ds(pl.multiple_of(side_ref[0] * width, DH), width)
    other = pl.ds(pl.multiple_of((1 - side_ref[0]) * width, DH), width)
    own_copy = pltpu.make_async_copy(own_hbm, own_ref, own_sem.at[0])
    own_copy.start()
    chunks = [slice(start, start + CHUNK) for start in range(0, weight_ref.shape[0], CHUNK)]
    copies = [
        pltpu.make_async_copy(weight_hbm.at[rows, :], weight_ref.at[rows, :], sems.at[c])
        for c, rows in enumerate(chunks)
    ]
    for copy in copies:
        copy.start()
    own_copy.wait()
    for copy, rows in zip(copies, chunks):
        copy.wait()
        total = dot(own_ref[...], weight_ref[rows, own], (1, 1))
        out_ref[:, rows] = total + dot(other_ref[...], weight_ref[rows, other], (1, 1))


def column_chunks(start, weight_hbm, weight_ref, sems):
    copies = []
    for c, column in enumerate(range(0, weight_ref.shape[1], CHUNK)):
        source = pl.ds(pl.multiple_of(start + column, DH), CHUNK)
        columns = slice(column, column + CHUNK)
        copy = pltpu.make_async_copy(weight_hbm.at[:, source], weight_ref.at[:, columns], sems.at[c])
        copy.start()
        copies.append((copy, columns))
    return copies


def send_kernel(side_ref, normed_ref, weight_hbm, out_ref, weight_ref, sems):
    start = (1 - side_ref[0]) * out_ref.shape[1]
    for copy, columns in column_chunks(start, weight_hbm, weight_ref, sems):
        copy.wait()
        out_ref[:, columns] = dot(normed_ref[...], weight_ref[:, columns], (1, 0)).astype(low)


def mixed_kernel(side_ref, normed_ref, weight_hbm, other_ref, out_ref, weight_ref, sems):
    start = side_ref[0] * out_ref.shape[1]
    for copy, columns in column_chunks(start, weight_hbm, weight_ref, sems):
        copy.wait()
        total = dot(normed_ref[...], weight_ref[:, columns], (1, 0))
        out_ref[:, columns] = (total + other_ref[:, columns].astype(wide)).astype(low)


def first_kernel(gains, keep, b0, b1, b2, b3, send_ref, *refs):
    rows = send_ref.shape[0] - (EXTRA if gains else 0)
    blocks = (b0, b1, b2, b3)
    total = sum(block[:rows, :].astype(wide) for block in blocks)
    send_ref[:rows, :] = total.astype(low)
    gain_refs = refs[keep:]
    if keep:
        refs[0][...] = total
    spread_gain(gains, send_ref, gain_refs, blocks, None)


def spread_gain(gains, send_ref, gain_refs, blocks, earlier):
    if not gains:
        return
    send_ref[gains * DH :, :] = jnp.zeros((EXTRA, DH), low)
    for i in range(gains):
        gain = sum(pair_sum(block, gains, i) for block in blocks)
        if earlier is not None:
            gain = gain + earlier[i : i + 1, :]
        gain_refs[0][i : i + 1, :] = gain
        put_pair(send_ref, gains, i, gain)


def step_kernel(gains, past, beyond_ref, total_ref, got_ref, *refs):
    refs = list(refs)
    outside_ref = refs.pop(0) if past else None
    earlier = refs.pop(0) if gains else None
    total_out, outside_out, send_ref = refs[:3]
    rows = total_ref.shape[0]
    state = got_ref[:rows, :].astype(wide)
    outside = jnp.where(beyond_ref[0] != 0, state, 0.0)
    outside_out[...] = outside + outside_ref[...] if past else outside
    total = total_ref[...] + state
    total_out[...] = total
    send_ref[:rows, :] = total.astype(low)
    spread_gain(gains, send_ref, refs[3:], (got_ref,), earlier)


def last_kernel(gains, past, backward, place_ref, beyond_ref, b0, b1, b2, b3, got_ref, *refs):
    refs = list(refs)
    outside_ref = refs.pop(0) if past else None
    earlier = refs.pop(0) if gains else None
    blocks = (b0, b1, b2, b3)
    rows = got_ref.shape[0] - (EXTRA if gains else 0)
    quarter = place_ref[0]
    outside = jnp.where(beyond_ref[0] != 0, got_ref[:rows, :].astype(wide), 0.0)
    if past:
        outside = outside + outside_ref[...]
    states = [block[:rows, :].astype(wide) for block in blocks]
    for j in range(QUAD):
        result = outside
        for i in range(QUAD):
            if i == j:
                continue
            source, target = quarter ^ i, quarter ^ j
            counts = (source > target) if backward else (source < target)
            result = result + jnp.where(counts, states[i], 0.0)
        refs[j][:rows, :] = result.astype(low)
        if gains:
            refs[j][rows:, :] = jnp.zeros((EXTRA, DH), low)
    for i in range(gains):
        gain = earlier[i : i + 1, :] + pair_sum(got_ref, gains, i)
        for j in range(QUAD):
            put_pair(refs[j], gains, i, gain)


def swap(array, flip):
    count = lax.axis_size("seq")
    return lax.ppermute(array, "seq", [(i, i ^ flip) for i in range(count)])


def trade(array):
    return lax.ppermute(array, "tensor", [(0, 1), (1, 0)])


def scan(order, parts, backward, rows, gains, before_first, before_last):
    count = lax.axis_size("seq")
    place = lax.axis_index("seq")
    blocks = [parts[0]] + [swap(parts[j], j) for j in range(1, QUAD)]
    blocks, before_first = lax.optimization_barrier((blocks, before_first))
    total_shape = [shaped((rows, DH), wide)]
    part_shape = [shaped(parts[0].shape, low)]
    gain_shape = [shaped((gains, DH), wide)] if gains else []
    keep = int(count > 2 * QUAD)
    send, *rest = call(
        functools.partial(first_kernel, gains, keep),
        part_shape + total_shape * keep + gain_shape,
        [VMEM] * QUAD,
    )(*blocks)
    total, gain = rest[:keep], rest[keep:]
    outside = []
    step = QUAD
    while True:
        got = swap(send, step)
        bit = (place & step) != 0
        beyond = (jnp.logical_not(bit) if backward else bit).astype(jnp.int32).reshape(1)
        if 2 * step >= count:
            break
        new_total, new_outside, send, *gain = call(
            functools.partial(step_kernel, gains, len(outside)),
            total_shape * 2 + part_shape + gain_shape,
            [SMEM] + [VMEM] * (2 + len(outside) + len(gain)),
        )(beyond, *total, got, *outside, *gain)
        total, outside = [new_total], [new_outside]
        step *= 2
    got, before_last = lax.optimization_barrier((got, before_last))
    results = call(
        functools.partial(last_kernel, gains, len(outside), backward),
        part_shape * QUAD,
        [SMEM, SMEM] + [VMEM] * (QUAD + 1 + len(outside) + len(gain)),
    )(order, beyond, *blocks, got, *outside, *gain)
    back = [results[0]] + [swap(results[j], j) for j in range(1, QUAD)]
    return back, before_first, before_last


def on_device(queries, key_vectors, values, out_weight, norm_gain, grad_output):
    tokens, width = queries.shape
    model = out_weight.shape[1]
    heads = width // DH
    per_quarter = heads // QUAD
    rows = per_quarter * DH
    place = lax.axis_index("seq")
    order = (place & (QUAD - 1)).astype(jnp.int32).reshape(1)
    side = lax.axis_index("tensor").astype(jnp.int32).reshape(1)
    gain_row = norm_gain.reshape(1, width)
    whole = shaped((tokens, width), wide)
    whole_low = shaped((tokens, width), low)
    head_sems = pltpu.SemaphoreType.DMA((2, heads))
    half = model // 2
    weight_half = [pltpu.VMEM((width, half), low), pltpu.SemaphoreType.DMA((half // CHUNK,))]
    weight_whole = [pltpu.VMEM((width, model), low), pltpu.SemaphoreType.DMA((1,)), pltpu.SemaphoreType.DMA((width // CHUNK,))]

    other_grad = trade(grad_output)
    *parts, key_near, value_near = call(
        functools.partial(state_kernel, per_quarter),
        [shaped((rows, DH), low)] * QUAD + [whole_low, whole_low],
        [SMEM, HBM, HBM],
        scratch=[pltpu.SemaphoreType.DMA((2,))],
    )(order, key_vectors, values)
    local, query_near = call(
        functools.partial(local_kernel, heads),
        [whole, whole_low],
        [HBM, VMEM, VMEM],
        scratch=[pltpu.SemaphoreType.DMA((1,))],
    )(queries, key_near, value_near)
    (grad_normed,) = call(
        back_kernel,
        [whole],
        [SMEM, HBM, VMEM, HBM],
        scratch=[pltpu.VMEM((tokens, half), low)] + weight_whole,
        room=12,
    )(side, grad_output, other_grad, out_weight)
    prefix, grad_normed, local = scan(order, parts, False, rows, 0, grad_normed, local)

    normed, grad_low, *terms = call(
        functools.partial(norm_kernel, per_quarter),
        [whole_low, whole_low] + [shaped((rows + EXTRA, DH), low)] * QUAD,
        [SMEM, VMEM, VMEM, VMEM, FREE] + [VMEM] * 4,
    )(order, query_near, local, grad_normed, gain_row, *prefix)

    (sent,) = call(
        send_kernel, [whole_low], [SMEM, VMEM, HBM], out_specs=[FREE], scratch=weight_half, room=8
    )(
        side, normed, out_weight
    )
    grad_queries, local_keys, local_values = call(
        functools.partial(grad_kernel, per_quarter),
        [whole_low, whole_low, whole_low],
        [SMEM] + [VMEM] * 8,
        out_specs=[FREE, VMEM, VMEM],
    )(order, query_near, key_near, value_near, grad_low, *prefix)
    suffix, local_keys, sent = scan(order, terms, True, rows, per_quarter, local_keys, sent)
    other_part = trade(sent)
    (mixed,) = call(
        mixed_kernel,
        [whole_low],
        [SMEM, VMEM, HBM, VMEM],
        out_specs=[FREE],
        scratch=weight_half,
        room=8,
    )(side, normed, out_weight, other_part)
    mixed, local_keys = lax.optimization_barrier((mixed, local_keys))

    grad_keys, grad_values, grad_gain = call(
        functools.partial(finish_kernel, per_quarter),
        [whole_low, whole_low, shaped((1, width), wide)],
        [SMEM] + [VMEM] * 8,
        out_specs=[HBM, HBM, FREE],
        scratch=[pltpu.VMEM((tokens, width), low), pltpu.VMEM((tokens, width), low), head_sems],
    )(order, key_near, value_near, local_keys, local_values, *suffix)
    return mixed, grad_queries, grad_keys, grad_values, grad_gain.reshape(width)


def solution(mesh):
    placed = (
        P(("parts", "seq"), "tensor"),
        P(("parts", "seq"), "tensor"),
        P(("parts", "seq"), "tensor"),
        P("tensor", None),
        P("tensor"),
        P(("parts", "seq"), "tensor"),
    )
    return jax.shard_map(
        on_device,
        mesh=mesh,
        in_specs=placed,
        out_specs=(
            P(("parts", "seq"), "tensor"),
            P(("parts", "seq"), "tensor"),
            P(("parts", "seq"), "tensor"),
            P(("parts", "seq"), "tensor"),
            P(("parts", "tensor")),
        ),
        check_vma=False,
    )
```

time: 72.6 us -> 49.9 us (0.69); the launches traced: 71.6 us -> 49.7 us
  local copies, waits for them, and re-layouts: 14.1 us -> 0.01 us
  other arithmetic: 3.85 us -> 0 us
  Pallas kernels: 21.9 us -> 19 us
  waiting for transfers between devices: 11.6 us -> 10.2 us
    unnamed x62 -> x2, local copies, waits for them, and re-layouts: 13.2 us -> 0.01 us
    pallas_call x8 -> x12, Pallas kernels: 21.9 us -> 19 us  [pinned(): return kernel(*fixed)]
    convert_element_type x8 -> x0, other arithmetic: 2.78 us -> none  [the longest x3 1.91 us: pack(): return jnp.concatenate([state.astype(low), pairs, spare], axis=0)]
    ppermute x14, waiting for transfers between devices: 11.6 us -> 10.1 us  [swap(): return lax.ppermute(array, 'seq', [(i, i ^ flip) for i in range(count)])]
    concatenate x2 -> x0, other arithmetic: 0.86 us -> none  [pack(): return jnp.concatenate([state.astype(low), pairs, spare], axis=0)]
    slice x15 -> x0, local copies, waits for them, and re-layouts: 0.75 us -> none  [the longest x8 0.69 us: gain_of(): pairs = block[rows:rows + 2 * gains].astype(wide).reshape(gains, 2, DH)]
  transfers between devices with their start and end apart: 16 -> 16, of which waited for: 9 -> 8; matrix products, arithmetic and copies ran while one was open for 7% -> 0% of each run, Pallas kernels for 18% -> 31%
where the time goes in v2:
time: 49.9 us; the launch traced here: 49.7 us
  starting transfers between devices  19.8 us (40%)
  Pallas kernels  19 us (38%)
  waiting for transfers between devices  10.2 us (20%)
  between operations  0.75 us (2%)
    ppermute x14, starting transfers between devices, swap(): return lax.ppermute(array, 'seq', [(i, i ^ flip) for i in range(count)])  19.3 us
    pallas_call x12, Pallas kernels, pinned(): return kernel(*fixed)  19 us
    ppermute x14, waiting for transfers between devices, swap(): return lax.ppermute(array, 'seq', [(i, i ^ flip) for i in range(count)])  10.1 us
  transfers between devices with their start and end apart: 16, of which 8 were waited for; matrix products, arithmetic and copies ran while one was open for 0% of the time, Pallas kernels for 31%

profile of v2, /device:TPU:0, one launch (start us, length us, event | category | flops | bytes accessed | tf_op | source)
XLA Modules:
  0.0 49.7 jit_solution(15903210185401795847)
XLA Ops:
  1.2 1.6 %shard_map.101 = (bf16[256,128]{1,0:T(8,128)(2,1)S(1)}, bf16[256,128]{1,0:T(8,128)(2,1)S(1)}, bf16[256,128]{1,0:T(8,128)(2,1)S(1)}, bf16[256,128]{1,0:T(8,128)(2...) custom-call(s32[1]{0:T(128)} %bitcast.1.place_ref, bf16[192,1024]{1,0:T(8,128)(2,1)} %key_hbm.1, ...), custom_call_target="tpu_custom_call" | custom-call | flops 1000 | bytes 1000 | tf_op jit(solution)/shard_map/pallas_call | solution.py:53
  2.7 2.6 %collective-permute-start = (bf16[256,128]{1,0:T(8,128)(2,1)S(1)}, bf16[256,128]{1,0:T(8,128)(2,1)S(1)}, u32[]{:S(2)}, u32[]{:S(2)}) collective-permute-start(bf16[256,128]{1,0:T(8,128)(2,1)S(1)} %get-tuple-element.55), channel_id=1, source_target_pairs={{0,2},{2,0},{4,6},{6,4},{8,10},{10,8},{12,14},{14,12},{1,3},{3,1},... | collective-permute-start | bytes 196616 | tf_op jit(solution)/shard_map/ppermute | solution.py:292
  5.3 1.6 %collective-permute-start.1 = (bf16[256,128]{1,0:T(8,128)(2,1)S(1)}, bf16[256,128]{1,0:T(8,128)(2,1)S(1)}, u32[]{:S(2)}, u32[]{:S(2)}) collective-permute-start(bf16[256,128]{1,0:T(8,128)(2,1)S(1)} %get-tuple-element.56), channel_id=1, source_target_pairs={{0,4},{2,6},{4,0},{6,2},{8,12},{10,14},{12,8},{14,10},{1,5},{3,7},... | collective-permute-start | bytes 196616 | tf_op jit(solution)/shard_map/ppermute | solution.py:292
  6.9 3.4 %shard_map.103.grad_ref = f32[192,1024]{1,0:T(8,128)S(1)} custom-call(s32[1]{0:T(128)} %bitcast.side_ref, bf16[192,1024]{1,0:T(8,128)(2,1)} %own_hbm.1, bf16[192,1024]{1,0:T(8,128)(2,1)S(1)} %collective-permute-done.3.other_ref, bf16[1024,2048]{1,0:T(8,128)(2,1)} %weight_hbm.5), custom_call_target="tpu_custom_call" | custom-call | flops 1000 | bytes 1000 | tf_op jit(solution)/shard_map/pallas_call | solution.py:53
  10.3 1.8 %collective-permute-done.2.b3 = bf16[256,128]{1,0:T(8,128)(2,1)S(1)} collective-permute-done((bf16[256,128]{1,0:T(8,128)(2,1)S(1)}, bf16[256,128]{1,0:T(8,128)(2,1)S(1)}, u32[]{:S(2)}, u32[]{:S(2)}) %collective-permute-start.2) | collective-permute-done | bytes 65568 | tf_op jit(solution)/shard_map/ppermute | solution.py:292
  12.1 2.7 %collective-permute-start.4 = (bf16[256,128]{1,0:T(8,128)(2,1)S(1)}, bf16[256,128]{1,0:T(8,128)(2,1)S(1)}, u32[]{:S(2)}, u32[]{:S(2)}) collective-permute-start(bf16[256,128]{1,0:T(8,128)(2,1)S(1)} %shard_map.104), channel_id=1, source_target_pairs={{0,8},{2,10},{4,12},{6,14},{8,0},{10,2},{12,4},{14,6},{1,9},{3,11}... | collective-permute-start | bytes 196616 | tf_op jit(solution)/shard_map/ppermute | solution.py:292
  14.8 1.8 %shard_map.102 = (f32[192,1024]{1,0:T(8,128)S(1)}, bf16[192,1024]{1,0:T(8,128)(2,1)S(1)}) custom-call(bf16[192,1024]{1,0:T(8,128)(2,1)} %query_hbm.1, bf16[192,1024]{1,0:T(8,128)(2,1)S(1)} %get-tuple-element.51.key_ref, bf16[192,1024]{1,0:T(8,128)(2,1)S(1)} %get-tuple-element.52.value_ref), custom_call_target="tpu_custom_call" | custom-call | flops 1000 | bytes 1000 | tf_op jit(solution)/shard_map/pallas_call | solution.py:53
  16.6 1.3 %collective-permute-done.4.got_ref = bf16[256,128]{1,0:T(8,128)(2,1)S(1)} collective-permute-done((bf16[256,128]{1,0:T(8,128)(2,1)S(1)}, bf16[256,128]{1,0:T(8,128)(2,1)S(1)}, u32[]{:S(2)}, u32[]{:S(2)}) %collective-permute-start.4) | collective-permute-done | bytes 65568 | tf_op jit(solution)/shard_map/ppermute | solution.py:292
  18.1 1.3 %collective-permute-start.6 = (bf16[256,128]{1,0:T(8,128)(2,1)S(1)}, bf16[256,128]{1,0:T(8,128)(2,1)S(1)}, u32[]{:S(2)}, u32[]{:S(2)}) collective-permute-start(bf16[256,128]{1,0:T(8,128)(2,1)S(1)} %get-tuple-element.68), channel_id=1, source_target_pairs={{0,4},{2,6},{4,0},{6,2},{8,12},{10,14},{12,8},{14,10},{1,5},{3,7},... | collective-permute-start | bytes 196616 | tf_op jit(solution)/shard_map/ppermute | solution.py:292
  19.4 2.2 %collective-permute-start.7 = (bf16[256,128]{1,0:T(8,128)(2,1)S(1)}, bf16[256,128]{1,0:T(8,128)(2,1)S(1)}, u32[]{:S(2)}, u32[]{:S(2)}) collective-permute-start(bf16[256,128]{1,0:T(8,128)(2,1)S(1)} %get-tuple-element.69), channel_id=1, source_target_pairs={{0,6},{2,4},{4,2},{6,0},{8,14},{10,12},{12,10},{14,8},{1,7},{3,5},... | collective-permute-start | bytes 196616 | tf_op jit(solution)/shard_map/ppermute | solution.py:292
  22.5 2.1 %collective-permute-done.7.p3 = bf16[256,128]{1,0:T(8,128)(2,1)S(1)} collective-permute-done((bf16[256,128]{1,0:T(8,128)(2,1)S(1)}, bf16[256,128]{1,0:T(8,128)(2,1)S(1)}, u32[]{:S(2)}, u32[]{:S(2)}) %collective-permute-start.7) | collective-permute-done | bytes 65568 | tf_op jit(solution)/shard_map/ppermute | solution.py:292
  24.6 1.7 %shard_map.106 = (bf16[192,1024]{1,0:T(8,128)(2,1)S(1)}, bf16[192,1024]{1,0:T(8,128)(2,1)S(1)}, bf16[272,128]{1,0:T(8,128)(2,1)S(1)}, bf16[272,128]{1,0:T(8,128)...) custom-call(s32[1]{0:T(128)} %bitcast.1.place_ref, ...), custom_call_target="tpu_custom_call" | custom-call | flops 1000 | bytes 1000 | tf_op jit(solution)/shard_map/pallas_call | solution.py:53
  26.3 0.8 %collective-permute-start.8 = (bf16[272,128]{1,0:T(8,128)(2,1)S(1)}, bf16[272,128]{1,0:T(8,128)(2,1)S(1)}, u32[]{:S(2)}, u32[]{:S(2)}) collective-permute-start(bf16[272,128]{1,0:T(8,128)(2,1)S(1)} %get-tuple-element.72), channel_id=1, source_target_pairs={{0,2},{2,0},{4,6},{6,4},{8,10},{10,8},{12,14},{14,12},{1,3},{3,1},... | collective-permute-start | bytes 208904 | tf_op jit(solution)/shard_map/ppermute | solution.py:292
  27.1 2.0 %collective-permute-start.9 = (bf16[272,128]{1,0:T(8,128)(2,1)S(1)}, bf16[272,128]{1,0:T(8,128)(2,1)S(1)}, u32[]{:S(2)}, u32[]{:S(2)}) collective-permute-start(bf16[272,128]{1,0:T(8,128)(2,1)S(1)} %get-tuple-element.73), channel_id=1, source_target_pairs={{0,4},{2,6},{4,0},{6,2},{8,12},{10,14},{12,8},{14,10},{1,5},{3,7},... | collective-permute-start | bytes 208904 | tf_op jit(solution)/shard_map/ppermute | solution.py:292
  29.9 3.5 %shard_map.107 = (bf16[192,1024]{1,0:T(8,128)(2,1)}, bf16[192,1024]{1,0:T(8,128)(2,1)S(1)}, bf16[192,1024]{1,0:T(8,128)(2,1)S(1)}) custom-call(s32[1]{0:T(128)} %bitcast.1.place_ref, bf16[192,1024]{1,0:T(8,128)(2,1)S(1)} %get-tuple-element.53.query_ref, bf16[192,1024]{1,0:T(8,128)(2,1)S(1)} %get-tuple-element.51.key_ref, ...), custom_call_target="tpu_custom_call" | custom-call | flops 1000 | bytes 1000 | tf_op jit(solution)/shard_map/pallas_call | solution.py:53
  33.4 1.6 %collective-permute-done.10.b3 = bf16[272,128]{1,0:T(8,128)(2,1)S(1)} collective-permute-done((bf16[272,128]{1,0:T(8,128)(2,1)S(1)}, bf16[272,128]{1,0:T(8,128)(2,1)S(1)}, u32[]{:S(2)}, u32[]{:S(2)}) %collective-permute-start.10) | collective-permute-done | bytes 69664 | tf_op jit(solution)/shard_map/ppermute | solution.py:292
  35.0 1.8 %collective-permute-start.11 = (bf16[272,128]{1,0:T(8,128)(2,1)S(1)}, bf16[272,128]{1,0:T(8,128)(2,1)S(1)}, u32[]{:S(2)}, u32[]{:S(2)}) collective-permute-start(bf16[272,128]{1,0:T(8,128)(2,1)S(1)} %get-tuple-element.81), channel_id=1, source_target_pairs={{0,8},{2,10},{4,12},{6,14},{8,0},{10,2},{12,4},{14,6},{1,9},{3,11}... | collective-permute-start | bytes 208904 | tf_op jit(solution)/shard_map/ppermute | solution.py:292
  36.8 2.0 %shard_map.109 = bf16[192,1024]{1,0:T(8,128)(2,1)S(1)} custom-call(s32[1]{0:T(128)} %bitcast.side_ref, bf16[192,1024]{1,0:T(8,128)(2,1)S(1)} %get-tuple-element.70.normed_ref, bf16[1024,2048]{1,0:T(8,128)(2,1)} %weight_hbm.5), custom_call_target="tpu_custom_call" | custom-call | flops 1000 | bytes 1000 | tf_op jit(solution)/shard_map/pallas_call | solution.py:53
  38.8 1.5 %collective-permute-done.11.got_ref = bf16[272,128]{1,0:T(8,128)(2,1)S(1)} collective-permute-done((bf16[272,128]{1,0:T(8,128)(2,1)S(1)}, bf16[272,128]{1,0:T(8,128)(2,1)S(1)}, u32[]{:S(2)}, u32[]{:S(2)}) %collective-permute-start.11) | collective-permute-done | bytes 69664 | tf_op jit(solution)/shard_map/ppermute | solution.py:292
  40.6 1.4 %collective-permute-start.14 = (bf16[272,128]{1,0:T(8,128)(2,1)S(1)}, bf16[272,128]{1,0:T(8,128)(2,1)S(1)}, u32[]{:S(2)}, u32[]{:S(2)}) collective-permute-start(bf16[272,128]{1,0:T(8,128)(2,1)S(1)} %get-tuple-element.92), channel_id=1, source_target_pairs={{0,4},{2,6},{4,0},{6,2},{8,12},{10,14},{12,8},{14,10},{1,5},{3,7},... | collective-permute-start | bytes 208904 | tf_op jit(solution)/shard_map/ppermute | solution.py:292
  42.0 2.1 %collective-permute-start.15 = (bf16[272,128]{1,0:T(8,128)(2,1)S(1)}, bf16[272,128]{1,0:T(8,128)(2,1)S(1)}, u32[]{:S(2)}, u32[]{:S(2)}) collective-permute-start(bf16[272,128]{1,0:T(8,128)(2,1)S(1)} %get-tuple-element.93), channel_id=1, source_target_pairs={{0,6},{2,4},{4,2},{6,0},{8,14},{10,12},{12,10},{14,8},{1,7},{3,5},... | collective-permute-start | bytes 208904 | tf_op jit(solution)/shard_map/ppermute | solution.py:292
  44.1 2.8 %shard_map.110 = bf16[192,1024]{1,0:T(8,128)(2,1)} custom-call(s32[1]{0:T(128)} %bitcast.side_ref, bf16[192,1024]{1,0:T(8,128)(2,1)S(1)} %get-tuple-element.70.normed_ref, bf16[1024,2048]{1,0:T(8,128)(2,1)} %weight_hbm.5, bf16[192,1024]{1,0:T(8,128)(2,1)S(1)} %collective-permute-done.12.other_ref), custom_call_target="tpu_custom_call" | custom-call | flops 1000 | bytes 1000 | tf_op jit(solution)/shard_map/pallas_call | solution.py:53
  46.8 1.0 %collective-permute-done.15.s3 = bf16[272,128]{1,0:T(8,128)(2,1)S(1)} collective-permute-done((bf16[272,128]{1,0:T(8,128)(2,1)S(1)}, bf16[272,128]{1,0:T(8,128)(2,1)S(1)}, u32[]{:S(2)}, u32[]{:S(2)}) %collective-permute-start.15) | collective-permute-done | bytes 69664 | tf_op jit(solution)/shard_map/ppermute | solution.py:292
  47.8 1.8 %shard_map.112 = (bf16[192,1024]{1,0:T(8,128)(2,1)}, bf16[192,1024]{1,0:T(8,128)(2,1)}, f32[1,1024]{1,0:T(1,128)}) custom-call(s32[1]{0:T(128)} %bitcast.1.place_ref, bf16[192,1024]{1,0:T(8,128)(2,1)S(1)} %get-tuple-element.51.key_ref, bf16[192,1024]{1,0:T(8,128)(2,1)S(1)} %get-tuple-element.52.value_ref, ...), custom_call_target="tpu_custom_call" | custom-call | flops 1000 | bytes 1000 | tf_op jit(solution)/shard_map/pallas_call | solution.py:53
  (22 shorter events, 2.7 us)
Async XLA Ops:
  0.6 6.3 %collective-permute-start.3 = (bf16[192,1024]{1,0:T(8,128)(2,1)}, bf16[192,1024]{1,0:T(8,128)(2,1)S(1)}, u32[]{:S(2)}, u32[]{:S(2)}) collective-permute-start(bf16[192,1024]{1,0:T(8,128)(2,1)} %own_hbm.1), channel_id=1, source_target_pairs={{0,1},{1,0},{2,3},{3,2},{4,5},{5,4},{6,7},{7,6},{8,9},{9,8},{10,11... | collective-permute-start | bytes 1179656 | tf_op jit(solution)/shard_map/ppermute | solution.py:296
  1.1 23.5 %copy-start = (f32[1024]{0:T(1024)S(1)}, f32[1024]{0:T(1024)}, u32[]{:S(2)}) copy-start(f32[1024]{0:T(1024)} %param.10) | copy-start | bytes 12292
  2.7 7.6 %collective-permute-start = (bf16[256,128]{1,0:T(8,128)(2,1)S(1)}, bf16[256,128]{1,0:T(8,128)(2,1)S(1)}, u32[]{:S(2)}, u32[]{:S(2)}) collective-permute-start(bf16[256,128]{1,0:T(8,128)(2,1)S(1)} %get-tuple-element.55), channel_id=1, source_target_pairs={{0,2},{2,0},{4,6},{6,4},{8,10},{10,8},{12,14},{14,12},{1,3},{3,1},... | collective-permute-start | bytes 196616 | tf_op jit(solution)/shard_map/ppermute | solution.py:292
  5.3 5.0 %collective-permute-start.1 = (bf16[256,128]{1,0:T(8,128)(2,1)S(1)}, bf16[256,128]{1,0:T(8,128)(2,1)S(1)}, u32[]{:S(2)}, u32[]{:S(2)}) collective-permute-start(bf16[256,128]{1,0:T(8,128)(2,1)S(1)} %get-tuple-element.56), channel_id=1, source_target_pairs={{0,4},{2,6},{4,0},{6,2},{8,12},{10,14},{12,8},{14,10},{1,5},{3,7},... | collective-permute-start | bytes 196616 | tf_op jit(solution)/shard_map/ppermute | solution.py:292
  6.9 5.2 %collective-permute-start.2 = (bf16[256,128]{1,0:T(8,128)(2,1)S(1)}, bf16[256,128]{1,0:T(8,128)(2,1)S(1)}, u32[]{:S(2)}, u32[]{:S(2)}) collective-permute-start(bf16[256,128]{1,0:T(8,128)(2,1)S(1)} %get-tuple-element.57), channel_id=1, source_target_pairs={{0,6},{2,4},{4,2},{6,0},{8,14},{10,12},{12,10},{14,8},{1,7},{3,5},... | collective-permute-start | bytes 196616 | tf_op jit(solution)/shard_map/ppermute | solution.py:292
  12.1 5.8 %collective-permute-start.4 = (bf16[256,128]{1,0:T(8,128)(2,1)S(1)}, bf16[256,128]{1,0:T(8,128)(2,1)S(1)}, u32[]{:S(2)}, u32[]{:S(2)}) collective-permute-start(bf16[256,128]{1,0:T(8,128)(2,1)S(1)} %shard_map.104), channel_id=1, source_target_pairs={{0,8},{2,10},{4,12},{6,14},{8,0},{10,2},{12,4},{14,6},{1,9},{3,11}... | collective-permute-start | bytes 196616 | tf_op jit(solution)/shard_map/ppermute | solution.py:292
  18.1 4.3 %collective-permute-start.5 = (bf16[256,128]{1,0:T(8,128)(2,1)S(1)}, bf16[256,128]{1,0:T(8,128)(2,1)S(1)}, u32[]{:S(2)}, u32[]{:S(2)}) collective-permute-start(bf16[256,128]{1,0:T(8,128)(2,1)S(1)} %get-tuple-element.67), channel_id=1, source_target_pairs={{0,2},{2,0},{4,6},{6,4},{8,10},{10,8},{12,14},{14,12},{1,3},{3,1},... | collective-permute-start | bytes 196616 | tf_op jit(solution)/shard_map/ppermute | solution.py:292
  18.1 4.3 %collective-permute-start.6 = (bf16[256,128]{1,0:T(8,128)(2,1)S(1)}, bf16[256,128]{1,0:T(8,128)(2,1)S(1)}, u32[]{:S(2)}, u32[]{:S(2)}) collective-permute-start(bf16[256,128]{1,0:T(8,128)(2,1)S(1)} %get-tuple-element.68), channel_id=1, source_target_pairs={{0,4},{2,6},{4,0},{6,2},{8,12},{10,14},{12,8},{14,10},{1,5},{3,7},... | collective-permute-start | bytes 196616 | tf_op jit(solution)/shard_map/ppermute | solution.py:292
  19.4 5.2 %collective-permute-start.7 = (bf16[256,128]{1,0:T(8,128)(2,1)S(1)}, bf16[256,128]{1,0:T(8,128)(2,1)S(1)}, u32[]{:S(2)}, u32[]{:S(2)}) collective-permute-start(bf16[256,128]{1,0:T(8,128)(2,1)S(1)} %get-tuple-element.69), channel_id=1, source_target_pairs={{0,6},{2,4},{4,2},{6,0},{8,14},{10,12},{12,10},{14,8},{1,7},{3,5},... | collective-permute-start | bytes 196616 | tf_op jit(solution)/shard_map/ppermute | solution.py:292
  26.3 7.0 %collective-permute-start.8 = (bf16[272,128]{1,0:T(8,128)(2,1)S(1)}, bf16[272,128]{1,0:T(8,128)(2,1)S(1)}, u32[]{:S(2)}, u32[]{:S(2)}) collective-permute-start(bf16[272,128]{1,0:T(8,128)(2,1)S(1)} %get-tuple-element.72), channel_id=1, source_target_pairs={{0,2},{2,0},{4,6},{6,4},{8,10},{10,8},{12,14},{14,12},{1,3},{3,1},... | collective-permute-start | bytes 208904 | tf_op jit(solution)/shard_map/ppermute | solution.py:292
  27.1 6.3 %collective-permute-start.9 = (bf16[272,128]{1,0:T(8,128)(2,1)S(1)}, bf16[272,128]{1,0:T(8,128)(2,1)S(1)}, u32[]{:S(2)}, u32[]{:S(2)}) collective-permute-start(bf16[272,128]{1,0:T(8,128)(2,1)S(1)} %get-tuple-element.73), channel_id=1, source_target_pairs={{0,4},{2,6},{4,0},{6,2},{8,12},{10,14},{12,8},{14,10},{1,5},{3,7},... | collective-permute-start | bytes 208904 | tf_op jit(solution)/shard_map/ppermute | solution.py:292
  29.1 5.8 %collective-permute-start.10 = (bf16[272,128]{1,0:T(8,128)(2,1)S(1)}, bf16[272,128]{1,0:T(8,128)(2,1)S(1)}, u32[]{:S(2)}, u32[]{:S(2)}) collective-permute-start(bf16[272,128]{1,0:T(8,128)(2,1)S(1)} %get-tuple-element.74), channel_id=1, source_target_pairs={{0,6},{2,4},{4,2},{6,0},{8,14},{10,12},{12,10},{14,8},{1,7},{3,5},... | collective-permute-start | bytes 208904 | tf_op jit(solution)/shard_map/ppermute | solution.py:292
  35.0 5.3 %collective-permute-start.11 = (bf16[272,128]{1,0:T(8,128)(2,1)S(1)}, bf16[272,128]{1,0:T(8,128)(2,1)S(1)}, u32[]{:S(2)}, u32[]{:S(2)}) collective-permute-start(bf16[272,128]{1,0:T(8,128)(2,1)S(1)} %get-tuple-element.81), channel_id=1, source_target_pairs={{0,8},{2,10},{4,12},{6,14},{8,0},{10,2},{12,4},{14,6},{1,9},{3,11}... | collective-permute-start | bytes 208904 | tf_op jit(solution)/shard_map/ppermute | solution.py:292
  40.3 3.8 %collective-permute-start.12 = (bf16[192,1024]{1,0:T(8,128)(2,1)S(1)}, bf16[192,1024]{1,0:T(8,128)(2,1)S(1)}, u32[]{:S(2)}, u32[]{:S(2)}) collective-permute-start(bf16[192,1024]{1,0:T(8,128)(2,1)S(1)} %shard_map.109), channel_id=1, source_target_pairs={{0,1},{1,0},{2,3},{3,2},{4,5},{5,4},{6,7},{7,6},{8,9},{9,8},{10,11... | collective-permute-start | bytes 1179656 | tf_op jit(solution)/shard_map/ppermute | solution.py:296
  40.5 6.3 %collective-permute-start.13 = (bf16[272,128]{1,0:T(8,128)(2,1)S(1)}, bf16[272,128]{1,0:T(8,128)(2,1)S(1)}, u32[]{:S(2)}, u32[]{:S(2)}) collective-permute-start(bf16[272,128]{1,0:T(8,128)(2,1)S(1)} %get-tuple-element.91), channel_id=1, source_target_pairs={{0,2},{2,0},{4,6},{6,4},{8,10},{10,8},{12,14},{14,12},{1,3},{3,1},... | collective-permute-start | bytes 208904 | tf_op jit(solution)/shard_map/ppermute | solution.py:292
  40.6 6.3 %collective-permute-start.14 = (bf16[272,128]{1,0:T(8,128)(2,1)S(1)}, bf16[272,128]{1,0:T(8,128)(2,1)S(1)}, u32[]{:S(2)}, u32[]{:S(2)}) collective-permute-start(bf16[272,128]{1,0:T(8,128)(2,1)S(1)} %get-tuple-element.92), channel_id=1, source_target_pairs={{0,4},{2,6},{4,0},{6,2},{8,12},{10,14},{12,8},{14,10},{1,5},{3,7},... | collective-permute-start | bytes 208904 | tf_op jit(solution)/shard_map/ppermute | solution.py:292
  42.0 5.9 %collective-permute-start.15 = (bf16[272,128]{1,0:T(8,128)(2,1)S(1)}, bf16[272,128]{1,0:T(8,128)(2,1)S(1)}, u32[]{:S(2)}, u32[]{:S(2)}) collective-permute-start(bf16[272,128]{1,0:T(8,128)(2,1)S(1)} %get-tuple-element.93), channel_id=1, source_target_pairs={{0,6},{2,4},{4,2},{6,0},{8,14},{10,12},{12,10},{14,8},{1,7},{3,5},... | collective-permute-start | bytes 208904 | tf_op jit(solution)/shard_map/ppermute | solution.py:292

commit v3 on v2

v3 whole, which is shorter than its diff:
```python
import functools

import jax
import jax.numpy as jnp
from jax import lax
from jax.experimental import pallas as pl
from jax.experimental.pallas import tpu as pltpu
from jax.sharding import PartitionSpec as P

DH = 128
QUAD = 4
EXTRA = 16
CHUNK = 512
COST = 1000
FINISH = ((0, 1), (2, 3))
EPSILON = 1e-05
wide = jnp.float32
low = jnp.bfloat16
VMEM = pl.BlockSpec(memory_space=pltpu.VMEM)
SMEM = pl.BlockSpec(memory_space=pltpu.SMEM)
HBM = pl.BlockSpec(memory_space=pltpu.HBM)
FREE = pl.BlockSpec(memory_space=pltpu.VMEM)


def dot(a, b, over):
    return lax.dot_general(a, b, (((over[0],), (over[1],)), ((), ())), preferred_element_type=wide)


def shaped(shape, dtype):
    return jax.ShapeDtypeStruct(shape, dtype)


def call(body, outs, ins, out_specs=None, scratch=(), room=6, aliases=None):
    out_specs = out_specs or [VMEM] * len(outs)
    placed = [
        pltpu.VMEM(out.shape, out.dtype) if spec is VMEM else out for out, spec in zip(outs, out_specs)
    ]
    kernel = pl.pallas_call(
        body,
        out_shape=placed,
        in_specs=[VMEM if spec is FREE else spec for spec in ins],
        out_specs=[VMEM if spec is FREE else spec for spec in out_specs],
        scratch_shapes=list(scratch),
        input_output_aliases=aliases or {},
        cost_estimate=pl.CostEstimate(flops=COST, bytes_accessed=COST, transcendentals=0),
        compiler_params=pltpu.CompilerParams(vmem_limit_bytes=room * 2**20),
    )

    def pinned(*operands):
        spaces = {id(VMEM): pltpu.VMEM, id(HBM): pltpu.HBM}
        fixed = [
            pltpu.with_memory_space_constraint(operand, spaces[id(spec)]) if id(spec) in spaces else operand
            for operand, spec in zip(operands, ins, strict=True)
        ]
        return kernel(*fixed)

    return pinned


def head_slices(place, per_quarter, quarters=range(QUAD)):
    for j in quarters:
        for i in range(per_quarter):
            start = (((place & (QUAD - 1)) ^ j) * per_quarter + i) * DH
            yield j, i, pl.ds(pl.multiple_of(start, DH), DH)


def state_kernel(per_quarter, place_ref, key_hbm, value_hbm, *rest):
    out_refs, key_ref, value_ref, sems = rest[:QUAD], rest[QUAD], rest[QUAD + 1], rest[QUAD + 2]
    copies = [
        pltpu.make_async_copy(key_hbm, key_ref, sems.at[0]),
        pltpu.make_async_copy(value_hbm, value_ref, sems.at[1]),
    ]
    for copy in copies:
        copy.start()
    for copy in copies:
        copy.wait()
    for j, i, head in head_slices(place_ref[0], per_quarter):
        state = dot(key_ref[:, head], value_ref[:, head], (0, 0))
        out_refs[j][i * DH : (i + 1) * DH, :] = state.astype(low)


def causal(tokens):
    rows = lax.broadcasted_iota(jnp.int32, (tokens, tokens), 0)
    columns = lax.broadcasted_iota(jnp.int32, (tokens, tokens), 1)
    return rows >= columns


def local_kernel(heads, query_hbm, key_ref, value_ref, local_ref, query_ref, score_ref, sems):
    copy = pltpu.make_async_copy(query_hbm, query_ref, sems.at[0])
    copy.start()
    keep = causal(query_ref.shape[0])
    copy.wait()
    for h in range(heads):
        head = slice(h * DH, (h + 1) * DH)
        scores = dot(query_ref[:, head], key_ref[:, head], (1, 1))
        scores = jnp.where(keep, scores, 0.0).astype(low)
        score_ref[h] = scores
        local_ref[:, head] = dot(scores, value_ref[:, head], (1, 0))


def norm_kernel(
    per_quarter, j, place_ref, query_ref, local_ref, grad_ref, gain_ref, prefix_ref,
    normed_ref, low_ref, out_ref
):
    for _, i, head in head_slices(place_ref[0], per_quarter, (j,)):
        rows = slice(i * DH, (i + 1) * DH)
        query = query_ref[:, head]
        attention = local_ref[:, head] + dot(query, prefix_ref[rows, :], (1, 0))
        inverse = lax.rsqrt(jnp.mean(attention * attention, axis=-1, keepdims=True) + EPSILON)
        scaled = attention * inverse
        gain = gain_ref[:, head]
        normed_ref[:, rows] = (scaled * gain).astype(low)
        grad = grad_ref[:, head]
        gain_term = jnp.sum(grad * scaled, axis=0, keepdims=True)
        gained = grad * gain
        inner = jnp.mean(gained * scaled, axis=-1, keepdims=True)
        grad_low = (inverse * (gained - scaled * inner)).astype(low)
        low_ref[:, rows] = grad_low
        out_ref[rows, :] = dot(query, grad_low, (0, 0)).astype(low)
        if i == 0:
            out_ref[per_quarter * DH :, :] = jnp.zeros((EXTRA, DH), low)
        put_pair(out_ref, per_quarter, i, gain_term)


def times_weight(place, side, normed, weight_ref, start, count):
    width = normed[0].shape[1]
    half = weight_ref.shape[1] // 2
    columns = pl.ds(pl.multiple_of(side * half + start, DH), count)
    total = None
    for j in range(QUAD):
        rows = pl.ds(pl.multiple_of(((place & (QUAD - 1)) ^ j) * width, DH), width)
        part = dot(normed[j][...], weight_ref[rows, columns], (1, 0))
        total = part if total is None else total + part
    return total


def query_kernel(per_quarter, place_ref, side_ref, key_ref, value_ref, weight_ref, *rest):
    lows, normed, prefix = rest[:QUAD], rest[QUAD : 2 * QUAD], rest[2 * QUAD : 3 * QUAD]
    grad_query_hbm, sent_ref, grad_score_ref, grad_query_ref, sems = rest[3 * QUAD :]
    keep = causal(key_ref.shape[0])
    for j, i, head in head_slices(place_ref[0], per_quarter):
        rows = slice(i * DH, (i + 1) * DH)
        raw = dot(lows[j][:, rows], value_ref[:, head], (1, 1))
        grad_scores = jnp.where(keep, raw, 0.0).astype(low)
        grad_score_ref[j * per_quarter + i] = grad_scores
        grad_query = dot(grad_scores, key_ref[:, head], (1, 0))
        grad_query = grad_query + dot(lows[j][:, rows], prefix[j][rows, :], (1, 1))
        grad_query_ref[:, head] = grad_query.astype(low)
    store = pltpu.make_async_copy(grad_query_ref, grad_query_hbm, sems.at[0])
    store.start()
    for start in range(0, sent_ref.shape[1], CHUNK):
        total = times_weight(place_ref[0], 1 - side_ref[0], normed, weight_ref, start, CHUNK)
        sent_ref[:, start : start + CHUNK] = total.astype(low)
    store.wait()


def mixed_kernel(per_quarter, place_ref, side_ref, query_ref, score_ref, grad_score_ref, weight_ref, other_ref, *rest):
    lows, normed, rest = rest[:QUAD], rest[QUAD : 2 * QUAD], rest[2 * QUAD :]
    mixed_hbm, grad_key_ref, grad_value_ref, mixed_ref, sems = rest
    for start in range(0, other_ref.shape[1], CHUNK):
        columns = slice(start, start + CHUNK)
        total = times_weight(place_ref[0], side_ref[0], normed, weight_ref, start, CHUNK)
        mixed_ref[:, columns] = (total + other_ref[:, columns].astype(wide)).astype(low)
    store = pltpu.make_async_copy(mixed_ref, mixed_hbm, sems.at[0])
    store.start()
    for j, i, head in head_slices(place_ref[0], per_quarter):
        n = j * per_quarter + i
        columns = slice(n * DH, (n + 1) * DH)
        scores = score_ref[((place_ref[0] & (QUAD - 1)) ^ j) * per_quarter + i]
        grad_key_ref[:, columns] = dot(grad_score_ref[n], query_ref[:, head], (0, 0))
        grad_value_ref[:, columns] = dot(scores, lows[j][:, i * DH : (i + 1) * DH], (0, 0))
    store.wait()


def finish_kernel(per_quarter, quarters, place_ref, key_ref, value_ref, local_key_ref, local_value_ref, *rest):
    suffix, rest = rest[: len(quarters)], rest[len(quarters) :]
    grad_key_hbm, grad_value_hbm, gain_ref, key_out, value_out, sems = rest[-6:]
    gain_ref[...] = rest[0][...] if len(rest) > 6 else jnp.zeros_like(gain_ref)
    copies = []
    for n, (j, i, head) in enumerate(head_slices(place_ref[0], per_quarter, quarters)):
        rows = slice(i * DH, (i + 1) * DH)
        columns = slice(n * DH, (n + 1) * DH)
        own = slice((j * per_quarter + i) * DH, (j * per_quarter + i + 1) * DH)
        state_ref = suffix[n // per_quarter]
        state = state_ref[rows, :]
        grad_key = local_key_ref[:, own] + dot(value_ref[:, head], state, (1, 1))
        key_out[:, columns] = grad_key.astype(low)
        grad_value = local_value_ref[:, own] + dot(key_ref[:, head], state, (1, 0))
        value_out[:, columns] = grad_value.astype(low)
        copies.append(pltpu.make_async_copy(key_out.at[:, columns], grad_key_hbm.at[:, head], sems.at[0, n]))
        copies.append(pltpu.make_async_copy(value_out.at[:, columns], grad_value_hbm.at[:, head], sems.at[1, n]))
        for copy in copies[-2:]:
            copy.start()
        gain_ref[:, head] = pair_sum(state_ref, per_quarter, i)
    for copy in copies:
        copy.wait()


def pair_sum(ref, per_quarter, i):
    base = per_quarter * DH + 2 * i
    return ref[base : base + 1, :].astype(wide) + ref[base + 1 : base + 2, :].astype(wide)


def put_pair(ref, per_quarter, i, gain):
    base = per_quarter * DH + 2 * i
    upper = gain.astype(low)
    ref[base : base + 1, :] = upper
    ref[base + 1 : base + 2, :] = (gain - upper.astype(wide)).astype(low)


def back_kernel(side_ref, own_hbm, other_ref, weight_hbm, out_ref, weight_ref, own_ref, own_sem, sems):
    width = own_ref.shape[1]
    own = pl.ds(pl.multiple_of(side_ref[0] * width, DH), width)
    other = pl.ds(pl.multiple_of((1 - side_ref[0]) * width, DH), width)
    own_copy = pltpu.make_async_copy(own_hbm, own_ref, own_sem.at[0])
    own_copy.start()
    chunks = [slice(start, start + CHUNK) for start in range(0, weight_ref.shape[0], CHUNK)]
    copies = [
        pltpu.make_async_copy(weight_hbm.at[rows, :], weight_ref.at[rows, :], sems.at[c])
        for c, rows in enumerate(chunks)
    ]
    for copy in copies:
        copy.start()
    own_copy.wait()
    for copy, rows in zip(copies, chunks):
        copy.wait()
        total = dot(own_ref[...], weight_ref[rows, own], (1, 1))
        out_ref[:, rows] = total + dot(other_ref[...], weight_ref[rows, other], (1, 1))


def first_kernel(gains, keep, b0, b1, b2, b3, send_ref, *refs):
    rows = send_ref.shape[0] - (EXTRA if gains else 0)
    blocks = (b0, b1, b2, b3)
    total = sum(block[:rows, :].astype(wide) for block in blocks)
    send_ref[:rows, :] = total.astype(low)
    gain_refs = refs[keep:]
    if keep:
        refs[0][...] = total
    spread_gain(gains, send_ref, gain_refs, blocks, None)


def spread_gain(gains, send_ref, gain_refs, blocks, earlier):
    if not gains:
        return
    send_ref[gains * DH :, :] = jnp.zeros((EXTRA, DH), low)
    for i in range(gains):
        gain = sum(pair_sum(block, gains, i) for block in blocks)
        if earlier is not None:
            gain = gain + earlier[i : i + 1, :]
        gain_refs[0][i : i + 1, :] = gain
        put_pair(send_ref, gains, i, gain)


def is_beyond(place_ref, step, backward):
    return (place_ref[0] & step) == (0 if backward else step)


def step_kernel(gains, past, step, backward, place_ref, total_ref, got_ref, *refs):
    refs = list(refs)
    outside_ref = refs.pop(0) if past else None
    earlier = refs.pop(0) if gains else None
    total_out, outside_out, send_ref = refs[:3]
    rows = total_ref.shape[0]
    state = got_ref[:rows, :].astype(wide)
    outside = jnp.where(is_beyond(place_ref, step, backward), state, 0.0)
    outside_out[...] = outside + outside_ref[...] if past else outside
    total = total_ref[...] + state
    total_out[...] = total
    send_ref[:rows, :] = total.astype(low)
    spread_gain(gains, send_ref, refs[3:], (got_ref,), earlier)


def last_kernel(gains, past, step, backward, place_ref, b0, b1, b2, b3, got_ref, *refs):
    refs = list(refs)
    outside_ref = refs.pop(0) if past else None
    earlier = refs.pop(0) if gains else None
    blocks = (b0, b1, b2, b3)
    rows = got_ref.shape[0] - (EXTRA if gains else 0)
    quarter = place_ref[0] & (QUAD - 1)
    outside = jnp.where(is_beyond(place_ref, step, backward), got_ref[:rows, :].astype(wide), 0.0)
    if past:
        outside = outside + outside_ref[...]
    states = [block[:rows, :].astype(wide) for block in blocks]
    for j in range(QUAD):
        result = outside
        for i in range(QUAD):
            if i == j:
                continue
            source, target = quarter ^ i, quarter ^ j
            counts = (source > target) if backward else (source < target)
            result = result + jnp.where(counts, states[i], 0.0)
        refs[j][:rows, :] = result.astype(low)
        if gains:
            refs[j][rows:, :] = jnp.zeros((EXTRA, DH), low)
    for i in range(gains):
        gain = earlier[i : i + 1, :] + pair_sum(got_ref, gains, i)
        for j in range(QUAD):
            put_pair(refs[j], gains, i, gain)


def swap(array, flip):
    count = lax.axis_size("seq")
    return lax.ppermute(array, "seq", [(i, i ^ flip) for i in range(count)])


def trade(array):
    return lax.ppermute(array, "tensor", [(0, 1), (1, 0)])


def scan(where, parts, backward, rows, gains, before_first, before_last):
    blocks, before_first = begin(parts, before_first)
    back, before_last = end(where, blocks, backward, rows, gains, before_last)
    return back, before_first, before_last


def begin(parts, before_first):
    blocks = [parts[0]] + [swap(parts[j], j) for j in range(1, QUAD)]
    return lax.optimization_barrier((blocks, before_first))


def end(where, blocks, backward, rows, gains, before_last):
    count = lax.axis_size("seq")
    total_shape = [shaped((rows, DH), wide)]
    part_shape = [shaped(blocks[0].shape, low)]
    gain_shape = [shaped((gains, DH), wide)] if gains else []
    keep = int(count > 2 * QUAD)
    send, *rest = call(
        functools.partial(first_kernel, gains, keep),
        part_shape + total_shape * keep + gain_shape,
        [VMEM] * QUAD,
    )(*blocks)
    total, gain = rest[:keep], rest[keep:]
    outside = []
    step = QUAD
    while True:
        got = swap(send, step)
        if 2 * step >= count:
            break
        new_total, new_outside, send, *gain = call(
            functools.partial(step_kernel, gains, len(outside), step, backward),
            total_shape * 2 + part_shape + gain_shape,
            [SMEM] + [VMEM] * (2 + len(outside) + len(gain)),
        )(where, *total, got, *outside, *gain)
        total, outside = [new_total], [new_outside]
        step *= 2
    got, before_last = lax.optimization_barrier((got, before_last))
    results = call(
        functools.partial(last_kernel, gains, len(outside), step, backward),
        part_shape * QUAD,
        [SMEM] + [VMEM] * (QUAD + 1 + len(outside) + len(gain)),
    )(where, *blocks, got, *outside, *gain)
    back = [results[0]] + [swap(results[j], j) for j in range(1, QUAD)]
    return back, before_last


def on_device(queries, key_vectors, values, out_weight, norm_gain, grad_output):
    tokens, width = queries.shape
    model = out_weight.shape[1]
    heads = width // DH
    per_quarter = heads // QUAD
    rows = per_quarter * DH
    place = lax.axis_index("seq")
    where = place.astype(jnp.int32).reshape(1)
    side = lax.axis_index("tensor").astype(jnp.int32).reshape(1)
    gain_row = norm_gain.reshape(1, width)
    whole = shaped((tokens, width), wide)
    whole_low = shaped((tokens, width), low)
    half = model // 2
    result_whole = pltpu.VMEM((tokens, width), low)
    one_sem = pltpu.SemaphoreType.DMA((1,))
    two_sems = pltpu.SemaphoreType.DMA((2,))

    other_grad = trade(grad_output)
    *parts, key_near, value_near = call(
        functools.partial(state_kernel, per_quarter),
        [shaped((rows, DH), low)] * QUAD + [whole_low, whole_low],
        [SMEM, HBM, HBM],
        scratch=[two_sems],
    )(where, key_vectors, values)
    squares = shaped((heads, tokens, tokens), low)
    local, query_near, scores = call(
        functools.partial(local_kernel, heads),
        [whole, whole_low, squares],
        [HBM, VMEM, VMEM],
        scratch=[one_sem],
    )(queries, key_near, value_near)
    grad_normed, weight_near = call(
        back_kernel,
        [whole, shaped(out_weight.shape, low)],
        [SMEM, HBM, VMEM, HBM],
        scratch=[
            pltpu.VMEM((tokens, half), low),
            one_sem,
            pltpu.SemaphoreType.DMA((width // CHUNK,)),
        ],
    )(side, grad_output, other_grad, out_weight)
    prefix, grad_normed, local = scan(where, parts, False, rows, 0, grad_normed, local)

    part_low = shaped((tokens, rows), low)
    normed, lows, terms = zip(
        *(
            call(
                functools.partial(norm_kernel, per_quarter, j),
                [part_low, part_low, shaped((rows + EXTRA, DH), low)],
                [SMEM, VMEM, VMEM, VMEM, FREE, VMEM],
            )(where, query_near, local, grad_normed, gain_row, prefix[j])
            for j in range(QUAD)
        )
    )
    grad_queries, sent, grad_scores = call(
        functools.partial(query_kernel, per_quarter),
        [whole_low, whole_low, squares],
        [SMEM, SMEM] + [VMEM] * (3 + 3 * QUAD),
        out_specs=[HBM, VMEM, VMEM],
        scratch=[result_whole, one_sem],
    )(where, side, key_near, value_near, weight_near, *lows, *normed, *prefix)
    blocks, sent = begin(terms, sent)
    other_part = trade(sent)
    mixed, *local_pair = call(
        functools.partial(mixed_kernel, per_quarter),
        [whole_low, whole, whole],
        [SMEM, SMEM] + [VMEM] * (5 + 2 * QUAD),
        out_specs=[HBM, VMEM, VMEM],
        scratch=[result_whole, one_sem],
    )(where, side, query_near, scores, grad_scores, weight_near, other_part, *lows, *normed)
    suffix, local_pair = end(where, blocks, True, rows, per_quarter, local_pair)

    done = []
    for quarters in FINISH:
        count = len(quarters)
        result = pltpu.VMEM((tokens, count * rows), low)
        grad_keys, grad_values, gain = call(
            functools.partial(finish_kernel, per_quarter, quarters),
            [whole_low, whole_low, shaped((1, width), wide)],
            [SMEM] + [VMEM] * (4 + count) + [VMEM, HBM, HBM][: len(done)],
            out_specs=[HBM, HBM, VMEM if not done else FREE],
            scratch=[result, result, pltpu.SemaphoreType.DMA((2, count * per_quarter))],
            aliases={6 + count: 0, 7 + count: 1} if done else {},
        )(where, key_near, value_near, *local_pair, *(suffix[j] for j in quarters), *done)
        done = [gain, grad_keys, grad_values]
    return mixed, grad_queries, grad_keys, grad_values, gain.reshape(width)


def solution(mesh):
    placed = (
        P(("parts", "seq"), "tensor"),
        P(("parts", "seq"), "tensor"),
        P(("parts", "seq"), "tensor"),
        P("tensor", None),
        P("tensor"),
        P(("parts", "seq"), "tensor"),
    )
    return jax.shard_map(
        on_device,
        mesh=mesh,
        in_specs=placed,
        out_specs=(
            P(("parts", "seq"), "tensor"),
            P(("parts", "seq"), "tensor"),
            P(("parts", "seq"), "tensor"),
            P(("parts", "seq"), "tensor"),
            P(("parts", "tensor")),
        ),
        check_vma=False,
    )
```

time: 49.9 us -> 47.3 us (0.948)
  Pallas kernels: 19 us -> 15.8 us
  starting transfers between devices: 19.8 us -> 20.9 us
  waiting for transfers between devices: 10.2 us -> 9.6 us
    pallas_call x12 -> x15, Pallas kernels: 19 us -> 15.8 us  [pinned(): return kernel(*fixed)]
    ppermute x14, starting transfers between devices: 19.3 us -> 20.4 us  [swap(): return lax.ppermute(array, 'seq', [(i, i ^ flip) for i in range(count)])]
    ppermute x14, waiting for transfers between devices: 10.1 us -> 9.59 us  [swap(): return lax.ppermute(array, 'seq', [(i, i ^ flip) for i in range(count)])]
  transfers between devices with their start and end apart: 16 -> 16, of which waited for: 8 -> 7; matrix products, arithmetic and copies ran while one was open for 0% -> 0% of each run, Pallas kernels for 31% -> 29%
where the time goes in v3:
time: 47.3 us; the launch traced here: 47.1 us
  starting transfers between devices  20.9 us (44%)
  Pallas kernels  15.8 us (33%)
  waiting for transfers between devices  9.6 us (20%)
  between operations  0.78 us (2%)
    ppermute x14, starting transfers between devices, swap(): return lax.ppermute(array, 'seq', [(i, i ^ flip) for i in range(count)])  20.4 us
    pallas_call x15, Pallas kernels, pinned(): return kernel(*fixed)  15.8 us
    ppermute x14, waiting for transfers between devices, swap(): return lax.ppermute(array, 'seq', [(i, i ^ flip) for i in range(count)])  9.59 us
  transfers between devices with their start and end apart: 16, of which 7 were waited for; matrix products, arithmetic and copies ran while one was open for 0% of the time, Pallas kernels for 29%

profile of v3, /device:TPU:0, one launch (start us, length us, event | category | flops | bytes accessed | tf_op | source)
XLA Modules:
  0.0 47.1 jit_solution(1909474822046703461)
XLA Ops:
  1.2 1.6 %shard_map.101 = (bf16[256,128]{1,0:T(8,128)(2,1)S(1)}, bf16[256,128]{1,0:T(8,128)(2,1)S(1)}, bf16[256,128]{1,0:T(8,128)(2,1)S(1)}, bf16[256,128]{1,0:T(8,128)(2...) custom-call(s32[1]{0:T(128)} %bitcast.place_ref, bf16[192,1024]{1,0:T(8,128)(2,1)} %key_hbm.1, ...), custom_call_target="tpu_custom_call" | custom-call | flops 1000 | bytes 1000 | tf_op jit(solution)/shard_map/pallas_call | solution.py:55
  2.7 2.6 %collective-permute-start.1 = (bf16[256,128]{1,0:T(8,128)(2,1)S(1)}, bf16[256,128]{1,0:T(8,128)(2,1)S(1)}, u32[]{:S(2)}, u32[]{:S(2)}) collective-permute-start(bf16[256,128]{1,0:T(8,128)(2,1)S(1)} %get-tuple-element.71), channel_id=1, source_target_pairs={{0,2},{2,0},{4,6},{6,4},{8,10},{10,8},{12,14},{14,12},{1,3},{3,1},... | collective-permute-start | bytes 196616 | tf_op jit(solution)/shard_map/ppermute | solution.py:303
  5.3 1.6 %collective-permute-start.2 = (bf16[256,128]{1,0:T(8,128)(2,1)S(1)}, bf16[256,128]{1,0:T(8,128)(2,1)S(1)}, u32[]{:S(2)}, u32[]{:S(2)}) collective-permute-start(bf16[256,128]{1,0:T(8,128)(2,1)S(1)} %get-tuple-element.72), channel_id=1, source_target_pairs={{0,4},{2,6},{4,0},{6,2},{8,12},{10,14},{12,8},{14,10},{1,5},{3,7},... | collective-permute-start | bytes 196616 | tf_op jit(solution)/shard_map/ppermute | solution.py:303
  6.9 3.4 %shard_map.103 = (f32[192,1024]{1,0:T(8,128)S(1)}, bf16[1024,2048]{1,0:T(8,128)(2,1)S(1)}) custom-call(s32[1]{0:T(128)} %bitcast.1.side_ref, bf16[192,1024]{1,0:T(8,128)(2,1)} %own_hbm.1, bf16[192,1024]{1,0:T(8,128)(2,1)S(1)} %collective-permute-done.other_ref, bf16[1024,2048]{1,0:T(8,128)(2,1)} %weight_hbm.1), custom_call_target="tpu_custom_call" | custom-call | flops 1000 | bytes 1000 | tf_op jit(solution)/shard_map/pallas_call | solution.py:55
  10.3 1.8 %collective-permute-done.3.b3 = bf16[256,128]{1,0:T(8,128)(2,1)S(1)} collective-permute-done((bf16[256,128]{1,0:T(8,128)(2,1)S(1)}, bf16[256,128]{1,0:T(8,128)(2,1)S(1)}, u32[]{:S(2)}, u32[]{:S(2)}) %collective-permute-start.3) | collective-permute-done | bytes 65568 | tf_op jit(solution)/shard_map/ppermute | solution.py:303
  12.1 2.7 %collective-permute-start.4 = (bf16[256,128]{1,0:T(8,128)(2,1)S(1)}, bf16[256,128]{1,0:T(8,128)(2,1)S(1)}, u32[]{:S(2)}, u32[]{:S(2)}) collective-permute-start(bf16[256,128]{1,0:T(8,128)(2,1)S(1)} %shard_map.104), channel_id=1, source_target_pairs={{0,8},{2,10},{4,12},{6,14},{8,0},{10,2},{12,4},{14,6},{1,9},{3,11}... | collective-permute-start | bytes 196616 | tf_op jit(solution)/shard_map/ppermute | solution.py:303
  14.8 1.8 %shard_map.102 = (f32[192,1024]{1,0:T(8,128)S(1)}, bf16[192,1024]{1,0:T(8,128)(2,1)S(1)}, bf16[8,192,192]{2,1,0:T(8,128)(2,1)S(1)}) custom-call(bf16[192,1024]{1,0:T(8,128)(2,1)} %query_hbm.1, bf16[192,1024]{1,0:T(8,128)(2,1)S(1)} %get-tuple-element.65.key_ref, bf16[192,1024]{1,0:T(8,128)(2,1)S(1)} %get-tuple-element.66.value_ref), custom_call_target="tpu_custom_call" | custom-call | flops 1000 | bytes 1000 | tf_op jit(solution)/shard_map/pallas_call | solution.py:55
  16.6 1.3 %collective-permute-done.4.got_ref = bf16[256,128]{1,0:T(8,128)(2,1)S(1)} collective-permute-done((bf16[256,128]{1,0:T(8,128)(2,1)S(1)}, bf16[256,128]{1,0:T(8,128)(2,1)S(1)}, u32[]{:S(2)}, u32[]{:S(2)}) %collective-permute-start.4) | collective-permute-done | bytes 65568 | tf_op jit(solution)/shard_map/ppermute | solution.py:303
  18.1 1.3 %collective-permute-start.6 = (bf16[256,128]{1,0:T(8,128)(2,1)S(1)}, bf16[256,128]{1,0:T(8,128)(2,1)S(1)}, u32[]{:S(2)}, u32[]{:S(2)}) collective-permute-start(bf16[256,128]{1,0:T(8,128)(2,1)S(1)} %get-tuple-element.87), channel_id=1, source_target_pairs={{0,4},{2,6},{4,0},{6,2},{8,12},{10,14},{12,8},{14,10},{1,5},{3,7},... | collective-permute-start | bytes 196616 | tf_op jit(solution)/shard_map/ppermute | solution.py:303
  19.4 2.2 %collective-permute-start.7 = (bf16[256,128]{1,0:T(8,128)(2,1)S(1)}, bf16[256,128]{1,0:T(8,128)(2,1)S(1)}, u32[]{:S(2)}, u32[]{:S(2)}) collective-permute-start(bf16[256,128]{1,0:T(8,128)(2,1)S(1)} %get-tuple-element.89), channel_id=1, source_target_pairs={{0,6},{2,4},{4,2},{6,0},{8,14},{10,12},{12,10},{14,8},{1,7},{3,5},... | collective-permute-start | bytes 196616 | tf_op jit(solution)/shard_map/ppermute | solution.py:303
  21.6 1.0 %collective-permute-done.5.prefix_ref.rest_9_ = bf16[256,128]{1,0:T(8,128)(2,1)S(1)} collective-permute-done((bf16[256,128]{1,0:T(8,128)(2,1)S(1)}, bf16[256,128]{1,0:T(8,128)(2,1)S(1)}, u32[]{:S(2)}, u32[]{:S(2)}) %collective-permute-start.5) | collective-permute-done | bytes 65568 | tf_op jit(solution)/shard_map/ppermute | solution.py:303
  24.2 1.4 %collective-permute-start.9 = (bf16[272,128]{1,0:T(8,128)(2,1)S(1)}, bf16[272,128]{1,0:T(8,128)(2,1)S(1)}, u32[]{:S(2)}, u32[]{:S(2)}) collective-permute-start(bf16[272,128]{1,0:T(8,128)(2,1)S(1)} %get-tuple-element.98), channel_id=1, source_target_pairs={{0,4},{2,6},{4,0},{6,2},{8,12},{10,14},{12,8},{14,10},{1,5},{3,7},... | collective-permute-start | bytes 208904 | tf_op jit(solution)/shard_map/ppermute | solution.py:303
  26.2 1.9 %collective-permute-start.10 = (bf16[272,128]{1,0:T(8,128)(2,1)S(1)}, bf16[272,128]{1,0:T(8,128)(2,1)S(1)}, u32[]{:S(2)}, u32[]{:S(2)}) collective-permute-start(bf16[272,128]{1,0:T(8,128)(2,1)S(1)} %get-tuple-element.99), channel_id=1, source_target_pairs={{0,6},{2,4},{4,2},{6,0},{8,14},{10,12},{12,10},{14,8},{1,7},{3,5},... | collective-permute-start | bytes 208904 | tf_op jit(solution)/shard_map/ppermute | solution.py:303
  28.7 2.1 %shard_map.110 = (bf16[192,1024]{1,0:T(8,128)(2,1)}, bf16[192,1024]{1,0:T(8,128)(2,1)S(1)}, bf16[8,192,192]{2,1,0:T(8,128)(2,1)S(1)}) custom-call(s32[1]{0:T(128)} %bitcast.place_ref, s32[1]{0:T(128)} %bitcast.1.side_ref, bf16[192,1024]{1,0:T(8,128)(2,1)S(1)} %get-tuple-element.65.key_ref, bf16[192,1024]{1,0:T(8,128)(2,1)S(1)} %get-tuple-element.66.value_ref, ...), custom_call_target="tpu_custom_call" | custom-call | flops 1000 | bytes 1000 | tf_op jit(solution)/shard_map/pallas_call | solution.py:55
  30.8 0.6 %collective-permute-done.10.b3 = bf16[272,128]{1,0:T(8,128)(2,1)S(1)} collective-permute-done((bf16[272,128]{1,0:T(8,128)(2,1)S(1)}, bf16[272,128]{1,0:T(8,128)(2,1)S(1)}, u32[]{:S(2)}, u32[]{:S(2)}) %collective-permute-start.10) | collective-permute-done | bytes 69664 | tf_op jit(solution)/shard_map/ppermute | solution.py:303
  31.5 2.8 %collective-permute-start.12 = (bf16[272,128]{1,0:T(8,128)(2,1)S(1)}, bf16[272,128]{1,0:T(8,128)(2,1)S(1)}, u32[]{:S(2)}, u32[]{:S(2)}) collective-permute-start(bf16[272,128]{1,0:T(8,128)(2,1)S(1)} %get-tuple-element.108), channel_id=1, source_target_pairs={{0,8},{2,10},{4,12},{6,14},{8,0},{10,2},{12,4},{14,6},{1,9},{3,11}... | collective-permute-start | bytes 208904 | tf_op jit(solution)/shard_map/ppermute | solution.py:303
  34.3 1.6 %shard_map.111 = (bf16[192,1024]{1,0:T(8,128)(2,1)}, f32[192,1024]{1,0:T(8,128)S(1)}, f32[192,1024]{1,0:T(8,128)S(1)}) custom-call(s32[1]{0:T(128)} %bitcast.place_ref, s32[1]{0:T(128)} %bitcast.1.side_ref, bf16[192,1024]{1,0:T(8,128)(2,1)S(1)} %get-tuple-element.67.query_ref, bf16[8,192,192]{2,1,0:T(8,128)(2,1)S(1)} %get-tuple-element.68.score_ref, ...), custom_call_target="tpu_custom_call" | custom-call | flops 1000 | bytes 1000 | tf_op jit(solution)/shard_map/pallas_call | solution.py:55
  36.0 2.7 %collective-permute-done.12.got_ref = bf16[272,128]{1,0:T(8,128)(2,1)S(1)} collective-permute-done((bf16[272,128]{1,0:T(8,128)(2,1)S(1)}, bf16[272,128]{1,0:T(8,128)(2,1)S(1)}, u32[]{:S(2)}, u32[]{:S(2)}) %collective-permute-start.12) | collective-permute-done | bytes 69664 | tf_op jit(solution)/shard_map/ppermute | solution.py:303
  38.9 1.3 %collective-permute-start.13 = (bf16[272,128]{1,0:T(8,128)(2,1)S(1)}, bf16[272,128]{1,0:T(8,128)(2,1)S(1)}, u32[]{:S(2)}, u32[]{:S(2)}) collective-permute-start(bf16[272,128]{1,0:T(8,128)(2,1)S(1)} %get-tuple-element.115), channel_id=1, source_target_pairs={{0,4},{2,6},{4,0},{6,2},{8,12},{10,14},{12,8},{14,10},{1,5},{3,7},... | collective-permute-start | bytes 208904 | tf_op jit(solution)/shard_map/ppermute | solution.py:303
  40.3 2.2 %collective-permute-start.14 = (bf16[272,128]{1,0:T(8,128)(2,1)S(1)}, bf16[272,128]{1,0:T(8,128)(2,1)S(1)}, u32[]{:S(2)}, u32[]{:S(2)}) collective-permute-start(bf16[272,128]{1,0:T(8,128)(2,1)S(1)} %get-tuple-element.116), channel_id=1, source_target_pairs={{0,6},{2,4},{4,2},{6,0},{8,14},{10,12},{12,10},{14,8},{1,7},{3,5},... | collective-permute-start | bytes 208904 | tf_op jit(solution)/shard_map/ppermute | solution.py:303
  42.4 0.8 %collective-permute-done.15.rest_1_ = bf16[272,128]{1,0:T(8,128)(2,1)S(1)} collective-permute-done((bf16[272,128]{1,0:T(8,128)(2,1)S(1)}, bf16[272,128]{1,0:T(8,128)(2,1)S(1)}, u32[]{:S(2)}, u32[]{:S(2)}) %collective-permute-start.15) | collective-permute-done | bytes 69664 | tf_op jit(solution)/shard_map/ppermute | solution.py:303
  43.2 1.0 %shard_map.114 = (bf16[192,1024]{1,0:T(8,128)(2,1)}, bf16[192,1024]{1,0:T(8,128)(2,1)}, f32[1,1024]{1,0:T(1,128)S(1)}) custom-call(s32[1]{0:T(128)} %bitcast.place_ref, bf16[192,1024]{1,0:T(8,128)(2,1)S(1)} %get-tuple-element.65.key_ref, bf16[192,1024]{1,0:T(8,128)(2,1)S(1)} %get-tuple-element.66.value_ref, ...), custom_call_target="tpu_custom_call" | custom-call | flops 1000 | bytes 1000 | tf_op jit(solution)/shard_map/pallas_call | solution.py:55
  44.2 1.3 %collective-permute-done.14.rest_1_ = bf16[272,128]{1,0:T(8,128)(2,1)S(1)} collective-permute-done((bf16[272,128]{1,0:T(8,128)(2,1)S(1)}, bf16[272,128]{1,0:T(8,128)(2,1)S(1)}, u32[]{:S(2)}, u32[]{:S(2)}) %collective-permute-start.14) | collective-permute-done | bytes 69664 | tf_op jit(solution)/shard_map/ppermute | solution.py:303
  45.5 1.6 %shard_map.115 = (bf16[192,1024]{1,0:T(8,128)(2,1)}, bf16[192,1024]{1,0:T(8,128)(2,1)}, f32[1,1024]{1,0:T(1,128)}) custom-call(s32[1]{0:T(128)} %bitcast.place_ref, bf16[192,1024]{1,0:T(8,128)(2,1)S(1)} %get-tuple-element.65.key_ref, bf16[192,1024]{1,0:T(8,128)(2,1)S(1)} %get-tuple-element.66.value_ref, ...), custom_call_target="tpu_custom_call", output_to_operand_aliasing={{0}: (8, {}), {1}: (9, {})} | custom-call | flops 1000 | bytes 1000 | tf_op jit(solution)/shard_map/pallas_call | solution.py:55
  (25 shorter events, 3.9 us)
Async XLA Ops:
  0.6 22.0 %copy-start = (f32[1024]{0:T(1024)S(1)}, f32[1024]{0:T(1024)}, u32[]{:S(2)}) copy-start(f32[1024]{0:T(1024)} %param.10) | copy-start | bytes 12292
  0.6 6.3 %collective-permute-start = (bf16[192,1024]{1,0:T(8,128)(2,1)}, bf16[192,1024]{1,0:T(8,128)(2,1)S(1)}, u32[]{:S(2)}, u32[]{:S(2)}) collective-permute-start(bf16[192,1024]{1,0:T(8,128)(2,1)} %own_hbm.1), channel_id=1, source_target_pairs={{0,1},{1,0},{2,3},{3,2},{4,5},{5,4},{6,7},{7,6},{8,9},{9,8},{10,11... | collective-permute-start | bytes 1179656 | tf_op jit(solution)/shard_map/ppermute | solution.py:307
  2.7 7.6 %collective-permute-start.1 = (bf16[256,128]{1,0:T(8,128)(2,1)S(1)}, bf16[256,128]{1,0:T(8,128)(2,1)S(1)}, u32[]{:S(2)}, u32[]{:S(2)}) collective-permute-start(bf16[256,128]{1,0:T(8,128)(2,1)S(1)} %get-tuple-element.71), channel_id=1, source_target_pairs={{0,2},{2,0},{4,6},{6,4},{8,10},{10,8},{12,14},{14,12},{1,3},{3,1},... | collective-permute-start | bytes 196616 | tf_op jit(solution)/shard_map/ppermute | solution.py:303
  5.3 5.0 %collective-permute-start.2 = (bf16[256,128]{1,0:T(8,128)(2,1)S(1)}, bf16[256,128]{1,0:T(8,128)(2,1)S(1)}, u32[]{:S(2)}, u32[]{:S(2)}) collective-permute-start(bf16[256,128]{1,0:T(8,128)(2,1)S(1)} %get-tuple-element.72), channel_id=1, source_target_pairs={{0,4},{2,6},{4,0},{6,2},{8,12},{10,14},{12,8},{14,10},{1,5},{3,7},... | collective-permute-start | bytes 196616 | tf_op jit(solution)/shard_map/ppermute | solution.py:303
  6.9 5.2 %collective-permute-start.3 = (bf16[256,128]{1,0:T(8,128)(2,1)S(1)}, bf16[256,128]{1,0:T(8,128)(2,1)S(1)}, u32[]{:S(2)}, u32[]{:S(2)}) collective-permute-start(bf16[256,128]{1,0:T(8,128)(2,1)S(1)} %get-tuple-element.73), channel_id=1, source_target_pairs={{0,6},{2,4},{4,2},{6,0},{8,14},{10,12},{12,10},{14,8},{1,7},{3,5},... | collective-permute-start | bytes 196616 | tf_op jit(solution)/shard_map/ppermute | solution.py:303
  12.1 5.8 %collective-permute-start.4 = (bf16[256,128]{1,0:T(8,128)(2,1)S(1)}, bf16[256,128]{1,0:T(8,128)(2,1)S(1)}, u32[]{:S(2)}, u32[]{:S(2)}) collective-permute-start(bf16[256,128]{1,0:T(8,128)(2,1)S(1)} %shard_map.104), channel_id=1, source_target_pairs={{0,8},{2,10},{4,12},{6,14},{8,0},{10,2},{12,4},{14,6},{1,9},{3,11}... | collective-permute-start | bytes 196616 | tf_op jit(solution)/shard_map/ppermute | solution.py:303
  18.1 4.6 %collective-permute-start.5 = (bf16[256,128]{1,0:T(8,128)(2,1)S(1)}, bf16[256,128]{1,0:T(8,128)(2,1)S(1)}, u32[]{:S(2)}, u32[]{:S(2)}) collective-permute-start(bf16[256,128]{1,0:T(8,128)(2,1)S(1)} %get-tuple-element.85), channel_id=1, source_target_pairs={{0,2},{2,0},{4,6},{6,4},{8,10},{10,8},{12,14},{14,12},{1,3},{3,1},... | collective-permute-start | bytes 196616 | tf_op jit(solution)/shard_map/ppermute | solution.py:303
  18.1 5.5 %collective-permute-start.6 = (bf16[256,128]{1,0:T(8,128)(2,1)S(1)}, bf16[256,128]{1,0:T(8,128)(2,1)S(1)}, u32[]{:S(2)}, u32[]{:S(2)}) collective-permute-start(bf16[256,128]{1,0:T(8,128)(2,1)S(1)} %get-tuple-element.87), channel_id=1, source_target_pairs={{0,4},{2,6},{4,0},{6,2},{8,12},{10,14},{12,8},{14,10},{1,5},{3,7},... | collective-permute-start | bytes 196616 | tf_op jit(solution)/shard_map/ppermute | solution.py:303
  19.4 6.1 %collective-permute-start.7 = (bf16[256,128]{1,0:T(8,128)(2,1)S(1)}, bf16[256,128]{1,0:T(8,128)(2,1)S(1)}, u32[]{:S(2)}, u32[]{:S(2)}) collective-permute-start(bf16[256,128]{1,0:T(8,128)(2,1)S(1)} %get-tuple-element.89), channel_id=1, source_target_pairs={{0,6},{2,4},{4,2},{6,0},{8,14},{10,12},{12,10},{14,8},{1,7},{3,5},... | collective-permute-start | bytes 196616 | tf_op jit(solution)/shard_map/ppermute | solution.py:303
  23.2 7.6 %collective-permute-start.8 = (bf16[272,128]{1,0:T(8,128)(2,1)S(1)}, bf16[272,128]{1,0:T(8,128)(2,1)S(1)}, u32[]{:S(2)}, u32[]{:S(2)}) collective-permute-start(bf16[272,128]{1,0:T(8,128)(2,1)S(1)} %get-tuple-element.97), channel_id=1, source_target_pairs={{0,2},{2,0},{4,6},{6,4},{8,10},{10,8},{12,14},{14,12},{1,3},{3,1},... | collective-permute-start | bytes 208904 | tf_op jit(solution)/shard_map/ppermute | solution.py:303
  24.2 6.6 %collective-permute-start.9 = (bf16[272,128]{1,0:T(8,128)(2,1)S(1)}, bf16[272,128]{1,0:T(8,128)(2,1)S(1)}, u32[]{:S(2)}, u32[]{:S(2)}) collective-permute-start(bf16[272,128]{1,0:T(8,128)(2,1)S(1)} %get-tuple-element.98), channel_id=1, source_target_pairs={{0,4},{2,6},{4,0},{6,2},{8,12},{10,14},{12,8},{14,10},{1,5},{3,7},... | collective-permute-start | bytes 208904 | tf_op jit(solution)/shard_map/ppermute | solution.py:303
  26.2 5.3 %collective-permute-start.10 = (bf16[272,128]{1,0:T(8,128)(2,1)S(1)}, bf16[272,128]{1,0:T(8,128)(2,1)S(1)}, u32[]{:S(2)}, u32[]{:S(2)}) collective-permute-start(bf16[272,128]{1,0:T(8,128)(2,1)S(1)} %get-tuple-element.99), channel_id=1, source_target_pairs={{0,6},{2,4},{4,2},{6,0},{8,14},{10,12},{12,10},{14,8},{1,7},{3,5},... | collective-permute-start | bytes 208904 | tf_op jit(solution)/shard_map/ppermute | solution.py:303
  31.5 2.9 %collective-permute-start.11 = (bf16[192,1024]{1,0:T(8,128)(2,1)S(1)}, bf16[192,1024]{1,0:T(8,128)(2,1)S(1)}, u32[]{:S(2)}, u32[]{:S(2)}) collective-permute-start(bf16[192,1024]{1,0:T(8,128)(2,1)S(1)} %get-tuple-element.101), channel_id=1, source_target_pairs={{0,1},{1,0},{2,3},{3,2},{4,5},{5,4},{6,7},{7,6},{8,9},{9,8},{10,11... | collective-permute-start | bytes 1179656 | tf_op jit(solution)/shard_map/ppermute | solution.py:307
  31.5 7.2 %collective-permute-start.12 = (bf16[272,128]{1,0:T(8,128)(2,1)S(1)}, bf16[272,128]{1,0:T(8,128)(2,1)S(1)}, u32[]{:S(2)}, u32[]{:S(2)}) collective-permute-start(bf16[272,128]{1,0:T(8,128)(2,1)S(1)} %get-tuple-element.108), channel_id=1, source_target_pairs={{0,8},{2,10},{4,12},{6,14},{8,0},{10,2},{12,4},{14,6},{1,9},{3,11}... | collective-permute-start | bytes 208904 | tf_op jit(solution)/shard_map/ppermute | solution.py:303
  38.9 4.4 %collective-permute-start.15 = (bf16[272,128]{1,0:T(8,128)(2,1)S(1)}, bf16[272,128]{1,0:T(8,128)(2,1)S(1)}, u32[]{:S(2)}, u32[]{:S(2)}) collective-permute-start(bf16[272,128]{1,0:T(8,128)(2,1)S(1)} %get-tuple-element.118), channel_id=1, source_target_pairs={{0,2},{2,0},{4,6},{6,4},{8,10},{10,8},{12,14},{14,12},{1,3},{3,1},... | collective-permute-start | bytes 208904 | tf_op jit(solution)/shard_map/ppermute | solution.py:303
  38.9 5.3 %collective-permute-start.13 = (bf16[272,128]{1,0:T(8,128)(2,1)S(1)}, bf16[272,128]{1,0:T(8,128)(2,1)S(1)}, u32[]{:S(2)}, u32[]{:S(2)}) collective-permute-start(bf16[272,128]{1,0:T(8,128)(2,1)S(1)} %get-tuple-element.115), channel_id=1, source_target_pairs={{0,4},{2,6},{4,0},{6,2},{8,12},{10,14},{12,8},{14,10},{1,5},{3,7},... | collective-permute-start | bytes 208904 | tf_op jit(solution)/shard_map/ppermute | solution.py:303
  40.3 5.3 %collective-permute-start.14 = (bf16[272,128]{1,0:T(8,128)(2,1)S(1)}, bf16[272,128]{1,0:T(8,128)(2,1)S(1)}, u32[]{:S(2)}, u32[]{:S(2)}) collective-permute-start(bf16[272,128]{1,0:T(8,128)(2,1)S(1)} %get-tuple-element.116), channel_id=1, source_target_pairs={{0,6},{2,4},{4,2},{6,0},{8,14},{10,12},{12,10},{14,8},{1,7},{3,5},... | collective-permute-start | bytes 208904 | tf_op jit(solution)/shard_map/ppermute | solution.py:303

commit v4 on v3

--- a/solution.py
+++ b/solution.py
@@ -12,7 +12,7 @@
 EXTRA = 16
 CHUNK = 512
 COST = 1000
-FINISH = ((0, 1), (2, 3))
+FINISH = ((0,), (1, 2, 3))
 EPSILON = 1e-05
 wide = jnp.float32
 low = jnp.bfloat16
@@ -154,22 +154,27 @@
     store.wait()
 
 
-def mixed_kernel(per_quarter, place_ref, side_ref, query_ref, score_ref, grad_score_ref, weight_ref, other_ref, *rest):
-    lows, normed, rest = rest[:QUAD], rest[QUAD : 2 * QUAD], rest[2 * QUAD :]
-    mixed_hbm, grad_key_ref, grad_value_ref, mixed_ref, sems = rest
-    for start in range(0, other_ref.shape[1], CHUNK):
-        columns = slice(start, start + CHUNK)
-        total = times_weight(place_ref[0], side_ref[0], normed, weight_ref, start, CHUNK)
-        mixed_ref[:, columns] = (total + other_ref[:, columns].astype(wide)).astype(low)
-    store = pltpu.make_async_copy(mixed_ref, mixed_hbm, sems.at[0])
-    store.start()
+def pair_kernel(per_quarter, place_ref, query_ref, score_ref, grad_score_ref, *rest):
+    lows, (grad_key_ref, grad_value_ref) = rest[:QUAD], rest[QUAD:]
     for j, i, head in head_slices(place_ref[0], per_quarter):
         n = j * per_quarter + i
         columns = slice(n * DH, (n + 1) * DH)
         scores = score_ref[((place_ref[0] & (QUAD - 1)) ^ j) * per_quarter + i]
         grad_key_ref[:, columns] = dot(grad_score_ref[n], query_ref[:, head], (0, 0))
         grad_value_ref[:, columns] = dot(scores, lows[j][:, i * DH : (i + 1) * DH], (0, 0))
-    store.wait()
+
+
+def mixed_kernel(place_ref, side_ref, weight_ref, other_ref, *rest):
+    normed, (mixed_hbm, mixed_ref, sems) = rest[:QUAD], rest[QUAD:]
+    copies = []
+    for n, start in enumerate(range(0, other_ref.shape[1], CHUNK)):
+        columns = slice(start, start + CHUNK)
+        total = times_weight(place_ref[0], side_ref[0], normed, weight_ref, start, CHUNK)
+        mixed_ref[:, columns] = (total + other_ref[:, columns].astype(wide)).astype(low)
+        copies.append(pltpu.make_async_copy(mixed_ref.at[:, columns], mixed_hbm.at[:, columns], sems.at[n]))
+        copies[n].start()
+    for copy in copies:
+        copy.wait()
 
 
 def finish_kernel(per_quarter, quarters, place_ref, key_ref, value_ref, local_key_ref, local_value_ref, *rest):
@@ -415,15 +420,22 @@
         scratch=[result_whole, one_sem],
     )(where, side, key_near, value_near, weight_near, *lows, *normed, *prefix)
     blocks, sent = begin(terms, sent)
+    local_pair = call(
+        functools.partial(pair_kernel, per_quarter),
+        [whole, whole],
+        [SMEM] + [VMEM] * (3 + QUAD),
+    )(where, query_near, scores, grad_scores, *lows)
+    suffix, local_pair = end(where, blocks, True, rows, per_quarter, (local_pair, sent))
+    local_pair, sent = local_pair
     other_part = trade(sent)
-    mixed, *local_pair = call(
-        functools.partial(mixed_kernel, per_quarter),
-        [whole_low, whole, whole],
-        [SMEM, SMEM] + [VMEM] * (5 + 2 * QUAD),
-        out_specs=[HBM, VMEM, VMEM],
-        scratch=[result_whole, one_sem],
-    )(where, side, query_near, scores, grad_scores, weight_near, other_part, *lows, *normed)
-    suffix, local_pair = end(where, blocks, True, rows, per_quarter, local_pair)
+    (mixed,) = call(
+        mixed_kernel,
+        [whole_low],
+        [SMEM, SMEM] + [VMEM] * (2 + QUAD),
+        out_specs=[HBM],
+        scratch=[result_whole, pltpu.SemaphoreType.DMA((half // CHUNK,))],
+    )(where, side, weight_near, other_part, *normed)
+    mixed, local_pair = lax.optimization_barrier((mixed, local_pair))
 
     done = []
     for quarters in FINISH:
@@ -433,7 +445,7 @@
             functools.partial(finish_kernel, per_quarter, quarters),
             [whole_low, whole_low, shaped((1, width), wide)],
             [SMEM] + [VMEM] * (4 + count) + [VMEM, HBM, HBM][: len(done)],
-            out_specs=[HBM, HBM, VMEM if not done else FREE],
+            out_specs=[HBM, HBM, FREE if quarters is FINISH[-1] else VMEM],
             scratch=[result, result, pltpu.SemaphoreType.DMA((2, count * per_quarter))],
             aliases={6 + count: 0, 7 + count: 1} if done else {},
         )(where, key_near, value_near, *local_pair, *(suffix[j] for j in quarters), *done)

time: 47.3 us -> 46.4 us (0.981)
  waiting for transfers between devices: 9.6 us -> 8.91 us
  starting transfers between devices: 20.9 us -> 20.4 us
    ppermute x14, waiting for transfers between devices: 9.59 us -> 8.91 us  [swap(): return lax.ppermute(array, 'seq', [(i, i ^ flip) for i in range(count)])]
    ppermute x14, starting transfers between devices: 20.4 us -> 19.9 us  [swap(): return lax.ppermute(array, 'seq', [(i, i ^ flip) for i in range(count)])]
    pallas_call x15 -> x16, Pallas kernels: 15.8 us -> 16.2 us  [pinned(): return kernel(*fixed)]
  transfers between devices with their start and end apart: 16 -> 16, of which waited for: 7 -> 6; matrix products, arithmetic and copies ran while one was open for 0% -> 0% of each run, Pallas kernels for 29% -> 31%
where the time goes in v4:
time: 46.4 us; the launch traced here: 46.3 us
  starting transfers between devices  20.4 us (44%)
  Pallas kernels  16.2 us (35%)
  waiting for transfers between devices  8.91 us (19%)
  between operations  0.77 us (2%)
    ppermute x14, starting transfers between devices, swap(): return lax.ppermute(array, 'seq', [(i, i ^ flip) for i in range(count)])  19.9 us
    pallas_call x16, Pallas kernels, pinned(): return kernel(*fixed)  16.2 us
    ppermute x14, waiting for transfers between devices, swap(): return lax.ppermute(array, 'seq', [(i, i ^ flip) for i in range(count)])  8.91 us
  transfers between devices with their start and end apart: 16, of which 6 were waited for; matrix products, arithmetic and copies ran while one was open for 0% of the time, Pallas kernels for 31%

profile of v4, /device:TPU:0, one launch (start us, length us, event | category | flops | bytes accessed | tf_op | source)
XLA Modules:
  0.0 46.3 jit_solution(12092619782406813738)
XLA Ops:
  1.2 1.6 %shard_map.102 = (bf16[256,128]{1,0:T(8,128)(2,1)S(1)}, bf16[256,128]{1,0:T(8,128)(2,1)S(1)}, bf16[256,128]{1,0:T(8,128)(2,1)S(1)}, bf16[256,128]{1,0:T(8,128)(2...) custom-call(s32[1]{0:T(128)} %bitcast.place_ref, bf16[192,1024]{1,0:T(8,128)(2,1)} %key_hbm.1, ...), custom_call_target="tpu_custom_call" | custom-call | flops 1000 | bytes 1000 | tf_op jit(solution)/shard_map/pallas_call | solution.py:55
  2.7 2.6 %collective-permute-start.1 = (bf16[256,128]{1,0:T(8,128)(2,1)S(1)}, bf16[256,128]{1,0:T(8,128)(2,1)S(1)}, u32[]{:S(2)}, u32[]{:S(2)}) collective-permute-start(bf16[256,128]{1,0:T(8,128)(2,1)S(1)} %get-tuple-element.73), channel_id=1, source_target_pairs={{0,2},{2,0},{4,6},{6,4},{8,10},{10,8},{12,14},{14,12},{1,3},{3,1},... | collective-permute-start | bytes 196616 | tf_op jit(solution)/shard_map/ppermute | solution.py:308
  5.3 1.6 %collective-permute-start.2 = (bf16[256,128]{1,0:T(8,128)(2,1)S(1)}, bf16[256,128]{1,0:T(8,128)(2,1)S(1)}, u32[]{:S(2)}, u32[]{:S(2)}) collective-permute-start(bf16[256,128]{1,0:T(8,128)(2,1)S(1)} %get-tuple-element.74), channel_id=1, source_target_pairs={{0,4},{2,6},{4,0},{6,2},{8,12},{10,14},{12,8},{14,10},{1,5},{3,7},... | collective-permute-start | bytes 196616 | tf_op jit(solution)/shard_map/ppermute | solution.py:308
  6.9 3.4 %shard_map.101 = (f32[192,1024]{1,0:T(8,128)S(1)}, bf16[1024,2048]{1,0:T(8,128)(2,1)S(1)}) custom-call(s32[1]{0:T(128)} %bitcast.1.side_ref, bf16[192,1024]{1,0:T(8,128)(2,1)} %own_hbm.1, bf16[192,1024]{1,0:T(8,128)(2,1)S(1)} %collective-permute-done.other_ref, bf16[1024,2048]{1,0:T(8,128)(2,1)} %weight_hbm.1), custom_call_target="tpu_custom_call" | custom-call | flops 1000 | bytes 1000 | tf_op jit(solution)/shard_map/pallas_call | solution.py:55
  10.3 1.8 %collective-permute-done.3.b3 = bf16[256,128]{1,0:T(8,128)(2,1)S(1)} collective-permute-done((bf16[256,128]{1,0:T(8,128)(2,1)S(1)}, bf16[256,128]{1,0:T(8,128)(2,1)S(1)}, u32[]{:S(2)}, u32[]{:S(2)}) %collective-permute-start.3) | collective-permute-done | bytes 65568 | tf_op jit(solution)/shard_map/ppermute | solution.py:308
  12.1 2.7 %collective-permute-start.4 = (bf16[256,128]{1,0:T(8,128)(2,1)S(1)}, bf16[256,128]{1,0:T(8,128)(2,1)S(1)}, u32[]{:S(2)}, u32[]{:S(2)}) collective-permute-start(bf16[256,128]{1,0:T(8,128)(2,1)S(1)} %shard_map.104), channel_id=1, source_target_pairs={{0,8},{2,10},{4,12},{6,14},{8,0},{10,2},{12,4},{14,6},{1,9},{3,11}... | collective-permute-start | bytes 196616 | tf_op jit(solution)/shard_map/ppermute | solution.py:308
  14.8 1.8 %shard_map.103 = (f32[192,1024]{1,0:T(8,128)S(1)}, bf16[192,1024]{1,0:T(8,128)(2,1)S(1)}, bf16[8,192,192]{2,1,0:T(8,128)(2,1)S(1)}) custom-call(bf16[192,1024]{1,0:T(8,128)(2,1)} %query_hbm.1, bf16[192,1024]{1,0:T(8,128)(2,1)S(1)} %get-tuple-element.69.key_ref, bf16[192,1024]{1,0:T(8,128)(2,1)S(1)} %get-tuple-element.70.value_ref), custom_call_target="tpu_custom_call" | custom-call | flops 1000 | bytes 1000 | tf_op jit(solution)/shard_map/pallas_call | solution.py:55
  16.6 1.3 %collective-permute-done.4.got_ref = bf16[256,128]{1,0:T(8,128)(2,1)S(1)} collective-permute-done((bf16[256,128]{1,0:T(8,128)(2,1)S(1)}, bf16[256,128]{1,0:T(8,128)(2,1)S(1)}, u32[]{:S(2)}, u32[]{:S(2)}) %collective-permute-start.4) | collective-permute-done | bytes 65568 | tf_op jit(solution)/shard_map/ppermute | solution.py:308
  18.1 0.8 %collective-permute-start.9 = (bf16[256,128]{1,0:T(8,128)(2,1)S(1)}, bf16[256,128]{1,0:T(8,128)(2,1)S(1)}, u32[]{:S(2)}, u32[]{:S(2)}) collective-permute-start(bf16[256,128]{1,0:T(8,128)(2,1)S(1)} %get-tuple-element.91), channel_id=1, source_target_pairs={{0,6},{2,4},{4,2},{6,0},{8,14},{10,12},{12,10},{14,8},{1,7},{3,5},... | collective-permute-start | bytes 196616 | tf_op jit(solution)/shard_map/ppermute | solution.py:308
  19.5 2.1 %collective-permute-start.5 = (bf16[256,128]{1,0:T(8,128)(2,1)S(1)}, bf16[256,128]{1,0:T(8,128)(2,1)S(1)}, u32[]{:S(2)}, u32[]{:S(2)}) collective-permute-start(bf16[256,128]{1,0:T(8,128)(2,1)S(1)} %get-tuple-element.87), channel_id=1, source_target_pairs={{0,2},{2,0},{4,6},{6,4},{8,10},{10,8},{12,14},{14,12},{1,3},{3,1},... | collective-permute-start | bytes 196616 | tf_op jit(solution)/shard_map/ppermute | solution.py:308
  21.6 1.7 %collective-permute-done.9.prefix_ref.rest_11_ = bf16[256,128]{1,0:T(8,128)(2,1)S(1)} collective-permute-done((bf16[256,128]{1,0:T(8,128)(2,1)S(1)}, bf16[256,128]{1,0:T(8,128)(2,1)S(1)}, u32[]{:S(2)}, u32[]{:S(2)}) %collective-permute-start.9) | collective-permute-done | bytes 65568 | tf_op jit(solution)/shard_map/ppermute | solution.py:308
  23.9 0.8 %collective-permute-start.10 = (bf16[272,128]{1,0:T(8,128)(2,1)S(1)}, bf16[272,128]{1,0:T(8,128)(2,1)S(1)}, u32[]{:S(2)}, u32[]{:S(2)}) collective-permute-start(bf16[272,128]{1,0:T(8,128)(2,1)S(1)} %get-tuple-element.92), channel_id=1, source_target_pairs={{0,6},{2,4},{4,2},{6,0},{8,14},{10,12},{12,10},{14,8},{1,7},{3,5},... | collective-permute-start | bytes 208904 | tf_op jit(solution)/shard_map/ppermute | solution.py:308
  25.3 0.7 %collective-permute-start.8 = (bf16[272,128]{1,0:T(8,128)(2,1)S(1)}, bf16[272,128]{1,0:T(8,128)(2,1)S(1)}, u32[]{:S(2)}, u32[]{:S(2)}) collective-permute-start(bf16[272,128]{1,0:T(8,128)(2,1)S(1)} %get-tuple-element.90), channel_id=1, source_target_pairs={{0,4},{2,6},{4,0},{6,2},{8,12},{10,14},{12,8},{14,10},{1,5},{3,7},... | collective-permute-start | bytes 208904 | tf_op jit(solution)/shard_map/ppermute | solution.py:308
  26.6 2.1 %collective-permute-start.6 = (bf16[272,128]{1,0:T(8,128)(2,1)S(1)}, bf16[272,128]{1,0:T(8,128)(2,1)S(1)}, u32[]{:S(2)}, u32[]{:S(2)}) collective-permute-start(bf16[272,128]{1,0:T(8,128)(2,1)S(1)} %get-tuple-element.88), channel_id=1, source_target_pairs={{0,2},{2,0},{4,6},{6,4},{8,10},{10,8},{12,14},{14,12},{1,3},{3,1},... | collective-permute-start | bytes 208904 | tf_op jit(solution)/shard_map/ppermute | solution.py:308
  29.4 2.1 %shard_map.110 = (bf16[192,1024]{1,0:T(8,128)(2,1)}, bf16[192,1024]{1,0:T(8,128)(2,1)S(1)}, bf16[8,192,192]{2,1,0:T(8,128)(2,1)S(1)}) custom-call(s32[1]{0:T(128)} %bitcast.place_ref, s32[1]{0:T(128)} %bitcast.1.side_ref, bf16[192,1024]{1,0:T(8,128)(2,1)S(1)} %get-tuple-element.69.key_ref, bf16[192,1024]{1,0:T(8,128)(2,1)S(1)} %get-tuple-element.70.value_ref, ...), custom_call_target="tpu_custom_call" | custom-call | flops 1000 | bytes 1000 | tf_op jit(solution)/shard_map/pallas_call | solution.py:55
  31.6 2.2 %collective-permute-start.11 = (bf16[272,128]{1,0:T(8,128)(2,1)S(1)}, bf16[272,128]{1,0:T(8,128)(2,1)S(1)}, u32[]{:S(2)}, u32[]{:S(2)}) collective-permute-start(bf16[272,128]{1,0:T(8,128)(2,1)S(1)} %get-tuple-element.106), channel_id=1, source_target_pairs={{0,8},{2,10},{4,12},{6,14},{8,0},{10,2},{12,4},{14,6},{1,9},{3,11}... | collective-permute-start | bytes 208904 | tf_op jit(solution)/shard_map/ppermute | solution.py:308
  33.8 0.7 %shard_map.112 = (f32[192,1024]{1,0:T(8,128)S(1)}, f32[192,1024]{1,0:T(8,128)S(1)}) custom-call(s32[1]{0:T(128)} %bitcast.place_ref, bf16[192,1024]{1,0:T(8,128)(2,1)S(1)} %get-tuple-element.71.query_ref, bf16[8,192,192]{2,1,0:T(8,128)(2,1)S(1)} %get-tuple-element.107.score_ref, bf16[8,192,192]{2,1,0:T(8,128)(2,1)S(1)} %get-tuple-element.108.grad_score_ref, ...), custom_call_target="tpu_custom_call" | custom-call | flops 1000 | bytes 1000 | tf_op jit(solution)/shard_map/pallas_call | solution.py:55
  34.5 2.3 %collective-permute-done.11.got_ref = bf16[272,128]{1,0:T(8,128)(2,1)S(1)} collective-permute-done((bf16[272,128]{1,0:T(8,128)(2,1)S(1)}, bf16[272,128]{1,0:T(8,128)(2,1)S(1)}, u32[]{:S(2)}, u32[]{:S(2)}) %collective-permute-start.11) | collective-permute-done | bytes 69664 | tf_op jit(solution)/shard_map/ppermute | solution.py:308
  37.0 1.9 %collective-permute-start.13 = (bf16[272,128]{1,0:T(8,128)(2,1)S(1)}, bf16[272,128]{1,0:T(8,128)(2,1)S(1)}, u32[]{:S(2)}, u32[]{:S(2)}) collective-permute-start(bf16[272,128]{1,0:T(8,128)(2,1)S(1)} %get-tuple-element.121), channel_id=1, source_target_pairs={{0,2},{2,0},{4,6},{6,4},{8,10},{10,8},{12,14},{14,12},{1,3},{3,1},... | collective-permute-start | bytes 208904 | tf_op jit(solution)/shard_map/ppermute | solution.py:308
  39.1 1.5 %collective-permute-start.15 = (bf16[272,128]{1,0:T(8,128)(2,1)S(1)}, bf16[272,128]{1,0:T(8,128)(2,1)S(1)}, u32[]{:S(2)}, u32[]{:S(2)}) collective-permute-start(bf16[272,128]{1,0:T(8,128)(2,1)S(1)} %get-tuple-element.123), channel_id=1, source_target_pairs={{0,6},{2,4},{4,2},{6,0},{8,14},{10,12},{12,10},{14,8},{1,7},{3,5},... | collective-permute-start | bytes 208904 | tf_op jit(solution)/shard_map/ppermute | solution.py:308
  40.6 1.3 %shard_map.113 = bf16[192,1024]{1,0:T(8,128)(2,1)} custom-call(s32[1]{0:T(128)} %bitcast.place_ref, s32[1]{0:T(128)} %bitcast.1.side_ref, bf16[1024,2048]{1,0:T(8,128)(2,1)S(1)} %get-tuple-element.68.weight_ref, bf16[192,1024]{1,0:T(8,128)(2,1)S(1)} %collective-permute-done.12.other_ref, bf16[192,256]{1,0:T(8,128)(2,1)S(1)} %get-tuple-element.97.rest_4_.rest_0_, ...), custom_call_target="tpu_custom_call" | custom-call | flops 1000 | bytes 1000 | tf_op jit(solution)/shard_map/pallas_call | solution.py:55
  41.9 0.9 %shard_map.115 = (bf16[192,1024]{1,0:T(8,128)(2,1)}, bf16[192,1024]{1,0:T(8,128)(2,1)}, f32[1,1024]{1,0:T(1,128)S(1)}) custom-call(s32[1]{0:T(128)} %bitcast.place_ref, bf16[192,1024]{1,0:T(8,128)(2,1)S(1)} %get-tuple-element.69.key_ref, bf16[192,1024]{1,0:T(8,128)(2,1)S(1)} %get-tuple-element.70.value_ref, ...), custom_call_target="tpu_custom_call" | custom-call | flops 1000 | bytes 1000 | tf_op jit(solution)/shard_map/pallas_call | solution.py:55
  42.8 1.2 %collective-permute-done.14.rest_1_ = bf16[272,128]{1,0:T(8,128)(2,1)S(1)} collective-permute-done((bf16[272,128]{1,0:T(8,128)(2,1)S(1)}, bf16[272,128]{1,0:T(8,128)(2,1)S(1)}, u32[]{:S(2)}, u32[]{:S(2)}) %collective-permute-start.14) | collective-permute-done | bytes 69664 | tf_op jit(solution)/shard_map/ppermute | solution.py:308
  44.6 1.7 %shard_map.116 = (bf16[192,1024]{1,0:T(8,128)(2,1)}, bf16[192,1024]{1,0:T(8,128)(2,1)}, f32[1,1024]{1,0:T(1,128)}) custom-call(s32[1]{0:T(128)} %bitcast.place_ref, bf16[192,1024]{1,0:T(8,128)(2,1)S(1)} %get-tuple-element.69.key_ref, bf16[192,1024]{1,0:T(8,128)(2,1)S(1)} %get-tuple-element.70.value_ref, ...), custom_call_target="tpu_custom_call", output_to_operand_aliasing={{0}: (9, {}), {1}: (10, {})} | custom-call | flops 1000 | bytes 1000 | tf_op jit(solution)/shard_map/pallas_call | solution.py:55
  (26 shorter events, 4.7 us)
Async XLA Ops:
  0.6 22.7 %copy-start = (f32[1024]{0:T(1024)S(1)}, f32[1024]{0:T(1024)}, u32[]{:S(2)}) copy-start(f32[1024]{0:T(1024)} %param.10) | copy-start | bytes 12292
  0.6 6.3 %collective-permute-start = (bf16[192,1024]{1,0:T(8,128)(2,1)}, bf16[192,1024]{1,0:T(8,128)(2,1)S(1)}, u32[]{:S(2)}, u32[]{:S(2)}) collective-permute-start(bf16[192,1024]{1,0:T(8,128)(2,1)} %own_hbm.1), channel_id=1, source_target_pairs={{0,1},{1,0},{2,3},{3,2},{4,5},{5,4},{6,7},{7,6},{8,9},{9,8},{10,11... | collective-permute-start | bytes 1179656 | tf_op jit(solution)/shard_map/ppermute | solution.py:312
  2.7 7.6 %collective-permute-start.1 = (bf16[256,128]{1,0:T(8,128)(2,1)S(1)}, bf16[256,128]{1,0:T(8,128)(2,1)S(1)}, u32[]{:S(2)}, u32[]{:S(2)}) collective-permute-start(bf16[256,128]{1,0:T(8,128)(2,1)S(1)} %get-tuple-element.73), channel_id=1, source_target_pairs={{0,2},{2,0},{4,6},{6,4},{8,10},{10,8},{12,14},{14,12},{1,3},{3,1},... | collective-permute-start | bytes 196616 | tf_op jit(solution)/shard_map/ppermute | solution.py:308
  5.3 5.0 %collective-permute-start.2 = (bf16[256,128]{1,0:T(8,128)(2,1)S(1)}, bf16[256,128]{1,0:T(8,128)(2,1)S(1)}, u32[]{:S(2)}, u32[]{:S(2)}) collective-permute-start(bf16[256,128]{1,0:T(8,128)(2,1)S(1)} %get-tuple-element.74), channel_id=1, source_target_pairs={{0,4},{2,6},{4,0},{6,2},{8,12},{10,14},{12,8},{14,10},{1,5},{3,7},... | collective-permute-start | bytes 196616 | tf_op jit(solution)/shard_map/ppermute | solution.py:308
  6.9 5.2 %collective-permute-start.3 = (bf16[256,128]{1,0:T(8,128)(2,1)S(1)}, bf16[256,128]{1,0:T(8,128)(2,1)S(1)}, u32[]{:S(2)}, u32[]{:S(2)}) collective-permute-start(bf16[256,128]{1,0:T(8,128)(2,1)S(1)} %get-tuple-element.75), channel_id=1, source_target_pairs={{0,6},{2,4},{4,2},{6,0},{8,14},{10,12},{12,10},{14,8},{1,7},{3,5},... | collective-permute-start | bytes 196616 | tf_op jit(solution)/shard_map/ppermute | solution.py:308
  12.1 5.8 %collective-permute-start.4 = (bf16[256,128]{1,0:T(8,128)(2,1)S(1)}, bf16[256,128]{1,0:T(8,128)(2,1)S(1)}, u32[]{:S(2)}, u32[]{:S(2)}) collective-permute-start(bf16[256,128]{1,0:T(8,128)(2,1)S(1)} %shard_map.104), channel_id=1, source_target_pairs={{0,8},{2,10},{4,12},{6,14},{8,0},{10,2},{12,4},{14,6},{1,9},{3,11}... | collective-permute-start | bytes 196616 | tf_op jit(solution)/shard_map/ppermute | solution.py:308
  18.1 5.2 %collective-permute-start.9 = (bf16[256,128]{1,0:T(8,128)(2,1)S(1)}, bf16[256,128]{1,0:T(8,128)(2,1)S(1)}, u32[]{:S(2)}, u32[]{:S(2)}) collective-permute-start(bf16[256,128]{1,0:T(8,128)(2,1)S(1)} %get-tuple-element.91), channel_id=1, source_target_pairs={{0,6},{2,4},{4,2},{6,0},{8,14},{10,12},{12,10},{14,8},{1,7},{3,5},... | collective-permute-start | bytes 196616 | tf_op jit(solution)/shard_map/ppermute | solution.py:308
  18.9 5.8 %collective-permute-start.7 = (bf16[256,128]{1,0:T(8,128)(2,1)S(1)}, bf16[256,128]{1,0:T(8,128)(2,1)S(1)}, u32[]{:S(2)}, u32[]{:S(2)}) collective-permute-start(bf16[256,128]{1,0:T(8,128)(2,1)S(1)} %get-tuple-element.89), channel_id=1, source_target_pairs={{0,4},{2,6},{4,0},{6,2},{8,12},{10,14},{12,8},{14,10},{1,5},{3,7},... | collective-permute-start | bytes 196616 | tf_op jit(solution)/shard_map/ppermute | solution.py:308
  19.5 6.5 %collective-permute-start.5 = (bf16[256,128]{1,0:T(8,128)(2,1)S(1)}, bf16[256,128]{1,0:T(8,128)(2,1)S(1)}, u32[]{:S(2)}, u32[]{:S(2)}) collective-permute-start(bf16[256,128]{1,0:T(8,128)(2,1)S(1)} %get-tuple-element.87), channel_id=1, source_target_pairs={{0,2},{2,0},{4,6},{6,4},{8,10},{10,8},{12,14},{14,12},{1,3},{3,1},... | collective-permute-start | bytes 196616 | tf_op jit(solution)/shard_map/ppermute | solution.py:308
  23.9 7.6 %collective-permute-start.10 = (bf16[272,128]{1,0:T(8,128)(2,1)S(1)}, bf16[272,128]{1,0:T(8,128)(2,1)S(1)}, u32[]{:S(2)}, u32[]{:S(2)}) collective-permute-start(bf16[272,128]{1,0:T(8,128)(2,1)S(1)} %get-tuple-element.92), channel_id=1, source_target_pairs={{0,6},{2,4},{4,2},{6,0},{8,14},{10,12},{12,10},{14,8},{1,7},{3,5},... | collective-permute-start | bytes 208904 | tf_op jit(solution)/shard_map/ppermute | solution.py:308
  25.3 6.2 %collective-permute-start.8 = (bf16[272,128]{1,0:T(8,128)(2,1)S(1)}, bf16[272,128]{1,0:T(8,128)(2,1)S(1)}, u32[]{:S(2)}, u32[]{:S(2)}) collective-permute-start(bf16[272,128]{1,0:T(8,128)(2,1)S(1)} %get-tuple-element.90), channel_id=1, source_target_pairs={{0,4},{2,6},{4,0},{6,2},{8,12},{10,14},{12,8},{14,10},{1,5},{3,7},... | collective-permute-start | bytes 208904 | tf_op jit(solution)/shard_map/ppermute | solution.py:308
  26.6 4.9 %collective-permute-start.6 = (bf16[272,128]{1,0:T(8,128)(2,1)S(1)}, bf16[272,128]{1,0:T(8,128)(2,1)S(1)}, u32[]{:S(2)}, u32[]{:S(2)}) collective-permute-start(bf16[272,128]{1,0:T(8,128)(2,1)S(1)} %get-tuple-element.88), channel_id=1, source_target_pairs={{0,2},{2,0},{4,6},{6,4},{8,10},{10,8},{12,14},{14,12},{1,3},{3,1},... | collective-permute-start | bytes 208904 | tf_op jit(solution)/shard_map/ppermute | solution.py:308
  31.6 5.3 %collective-permute-start.11 = (bf16[272,128]{1,0:T(8,128)(2,1)S(1)}, bf16[272,128]{1,0:T(8,128)(2,1)S(1)}, u32[]{:S(2)}, u32[]{:S(2)}) collective-permute-start(bf16[272,128]{1,0:T(8,128)(2,1)S(1)} %get-tuple-element.106), channel_id=1, source_target_pairs={{0,8},{2,10},{4,12},{6,14},{8,0},{10,2},{12,4},{14,6},{1,9},{3,11}... | collective-permute-start | bytes 208904 | tf_op jit(solution)/shard_map/ppermute | solution.py:308
  36.8 3.8 %collective-permute-start.12 = (bf16[192,1024]{1,0:T(8,128)(2,1)S(1)}, bf16[192,1024]{1,0:T(8,128)(2,1)S(1)}, u32[]{:S(2)}, u32[]{:S(2)}) collective-permute-start(bf16[192,1024]{1,0:T(8,128)(2,1)S(1)} %get-tuple-element.112), channel_id=1, source_target_pairs={{0,1},{1,0},{2,3},{3,2},{4,5},{5,4},{6,7},{7,6},{8,9},{9,8},{10,11... | collective-permute-start | bytes 1179656 | tf_op jit(solution)/shard_map/ppermute | solution.py:312
  37.0 5.8 %collective-permute-start.13 = (bf16[272,128]{1,0:T(8,128)(2,1)S(1)}, bf16[272,128]{1,0:T(8,128)(2,1)S(1)}, u32[]{:S(2)}, u32[]{:S(2)}) collective-permute-start(bf16[272,128]{1,0:T(8,128)(2,1)S(1)} %get-tuple-element.121), channel_id=1, source_target_pairs={{0,2},{2,0},{4,6},{6,4},{8,10},{10,8},{12,14},{14,12},{1,3},{3,1},... | collective-permute-start | bytes 208904 | tf_op jit(solution)/shard_map/ppermute | solution.py:308
  39.0 5.0 %collective-permute-start.14 = (bf16[272,128]{1,0:T(8,128)(2,1)S(1)}, bf16[272,128]{1,0:T(8,128)(2,1)S(1)}, u32[]{:S(2)}, u32[]{:S(2)}) collective-permute-start(bf16[272,128]{1,0:T(8,128)(2,1)S(1)} %get-tuple-element.122), channel_id=1, source_target_pairs={{0,4},{2,6},{4,0},{6,2},{8,12},{10,14},{12,8},{14,10},{1,5},{3,7},... | collective-permute-start | bytes 208904 | tf_op jit(solution)/shard_map/ppermute | solution.py:308
  39.1 5.5 %collective-permute-start.15 = (bf16[272,128]{1,0:T(8,128)(2,1)S(1)}, bf16[272,128]{1,0:T(8,128)(2,1)S(1)}, u32[]{:S(2)}, u32[]{:S(2)}) collective-permute-start(bf16[272,128]{1,0:T(8,128)(2,1)S(1)} %get-tuple-element.123), channel_id=1, source_target_pairs={{0,6},{2,4},{4,2},{6,0},{8,14},{10,12},{12,10},{14,8},{1,7},{3,5},... | collective-permute-start | bytes 208904 | tf_op jit(solution)/shard_map/ppermute | solution.py:308

commit v5 on v4

--- a/solution.py
+++ b/solution.py
@@ -12,7 +12,7 @@
 EXTRA = 16
 CHUNK = 512
 COST = 1000
-FINISH = ((0,), (1, 2, 3))
+FINISH = (0, 1, 2, 3)
 EPSILON = 1e-05
 wide = jnp.float32
 low = jnp.bfloat16
@@ -107,14 +107,15 @@
         query = query_ref[:, head]
         attention = local_ref[:, head] + dot(query, prefix_ref[rows, :], (1, 0))
         inverse = lax.rsqrt(jnp.mean(attention * attention, axis=-1, keepdims=True) + EPSILON)
+        grad = grad_ref[:, head]
+        gain = gain_ref[:, head]
+        gained = grad * gain
+        inner = jnp.mean(gained * attention, axis=-1, keepdims=True)
+        cubed = inverse * inverse * inverse
+        grad_low = (inverse * gained - attention * (cubed * inner)).astype(low)
         scaled = attention * inverse
-        gain = gain_ref[:, head]
         normed_ref[:, rows] = (scaled * gain).astype(low)
-        grad = grad_ref[:, head]
         gain_term = jnp.sum(grad * scaled, axis=0, keepdims=True)
-        gained = grad * gain
-        inner = jnp.mean(gained * scaled, axis=-1, keepdims=True)
-        grad_low = (inverse * (gained - scaled * inner)).astype(low)
         low_ref[:, rows] = grad_low
         out_ref[rows, :] = dot(query, grad_low, (0, 0)).astype(low)
         if i == 0:
@@ -164,40 +165,64 @@
         grad_value_ref[:, columns] = dot(scores, lows[j][:, i * DH : (i + 1) * DH], (0, 0))
 
 
-def mixed_kernel(place_ref, side_ref, weight_ref, other_ref, *rest):
-    normed, (mixed_hbm, mixed_ref, sems) = rest[:QUAD], rest[QUAD:]
+def finish_part(per_quarter, j, place, key_ref, value_ref, local_key_ref, local_value_ref, state_ref, grad_key_ref, grad_value_ref):
+    for _, i, head in head_slices(place, per_quarter, (j,)):
+        rows = slice(i * DH, (i + 1) * DH)
+        own = slice((j * per_quarter + i) * DH, (j * per_quarter + i + 1) * DH)
+        state = state_ref[rows, :]
+        grad_key = local_key_ref[:, own] + dot(value_ref[:, head], state, (1, 1))
+        grad_key_ref[:, rows] = grad_key.astype(low)
+        grad_value = local_value_ref[:, own] + dot(key_ref[:, head], state, (1, 0))
+        grad_value_ref[:, rows] = grad_value.astype(low)
+
+
+def finish_kernel(per_quarter, j, place_ref, *refs):
+    finish_part(per_quarter, j, place_ref[0], *refs)
+
+
+def stores(per_quarter, place, quarters, parts, outs, sems):
+    width = per_quarter * DH
     copies = []
-    for n, start in enumerate(range(0, other_ref.shape[1], CHUNK)):
+    for n, part in enumerate(parts):
+        start = ((place & (QUAD - 1)) ^ quarters[n // 2]) * width
+        columns = pl.ds(pl.multiple_of(start, DH), width)
+        copies.append(pltpu.make_async_copy(part, outs[n % 2].at[:, columns], sems.at[n]))
+    return copies
+
+
+def mixed_kernel(per_quarter, quarters, place_ref, side_ref, weight_ref, other_ref, *rest):
+    count = 2 * len(quarters)
+    normed, parts, rest = rest[:QUAD], rest[QUAD : QUAD + count], rest[QUAD + count :]
+    mixed_hbm, grad_key_hbm, grad_value_hbm, mixed_ref, sems = rest
+    copies = stores(per_quarter, place_ref[0], quarters, parts, (grad_key_hbm, grad_value_hbm), sems)
+    for copy in copies:
+        copy.start()
+    for start in range(0, other_ref.shape[1], CHUNK):
         columns = slice(start, start + CHUNK)
         total = times_weight(place_ref[0], side_ref[0], normed, weight_ref, start, CHUNK)
         mixed_ref[:, columns] = (total + other_ref[:, columns].astype(wide)).astype(low)
-        copies.append(pltpu.make_async_copy(mixed_ref.at[:, columns], mixed_hbm.at[:, columns], sems.at[n]))
-        copies[n].start()
+    copies.append(pltpu.make_async_copy(mixed_ref, mixed_hbm, sems.at[count]))
+    copies[-1].start()
     for copy in copies:
         copy.wait()
 
 
-def finish_kernel(per_quarter, quarters, place_ref, key_ref, value_ref, local_key_ref, local_value_ref, *rest):
-    suffix, rest = rest[: len(quarters)], rest[len(quarters) :]
-    grad_key_hbm, grad_value_hbm, gain_ref, key_out, value_out, sems = rest[-6:]
-    gain_ref[...] = rest[0][...] if len(rest) > 6 else jnp.zeros_like(gain_ref)
-    copies = []
-    for n, (j, i, head) in enumerate(head_slices(place_ref[0], per_quarter, quarters)):
-        rows = slice(i * DH, (i + 1) * DH)
-        columns = slice(n * DH, (n + 1) * DH)
-        own = slice((j * per_quarter + i) * DH, (j * per_quarter + i + 1) * DH)
-        state_ref = suffix[n // per_quarter]
-        state = state_ref[rows, :]
-        grad_key = local_key_ref[:, own] + dot(value_ref[:, head], state, (1, 1))
-        key_out[:, columns] = grad_key.astype(low)
-        grad_value = local_value_ref[:, own] + dot(key_ref[:, head], state, (1, 0))
-        value_out[:, columns] = grad_value.astype(low)
-        copies.append(pltpu.make_async_copy(key_out.at[:, columns], grad_key_hbm.at[:, head], sems.at[0, n]))
-        copies.append(pltpu.make_async_copy(value_out.at[:, columns], grad_value_hbm.at[:, head], sems.at[1, n]))
-        for copy in copies[-2:]:
-            copy.start()
-        gain_ref[:, head] = pair_sum(state_ref, per_quarter, i)
+def store_kernel(per_quarter, quarter, place_ref, key_ref, value_ref, local_key_ref, local_value_ref, *rest):
+    suffix, rest = rest[:QUAD], rest[QUAD + 2 :]
+    grad_key_hbm, grad_value_hbm, gain_hbm, key_part, value_part, gain_ref, sems = rest
+    place = place_ref[0]
+    for j, i, head in head_slices(place, per_quarter):
+        gain_ref[:, head] = pair_sum(suffix[j], per_quarter, i)
+    gain_copy = pltpu.make_async_copy(gain_ref, gain_hbm, sems.at[2])
+    gain_copy.start()
+    finish_part(
+        per_quarter, quarter, place, key_ref, value_ref, local_key_ref, local_value_ref, suffix[quarter],
+        key_part, value_part,
+    )
+    copies = stores(per_quarter, place, (quarter,), (key_part, value_part), (grad_key_hbm, grad_value_hbm), sems)
     for copy in copies:
+        copy.start()
+    for copy in (gain_copy, *copies):
         copy.wait()
 
 
@@ -428,28 +453,30 @@
     suffix, local_pair = end(where, blocks, True, rows, per_quarter, (local_pair, sent))
     local_pair, sent = local_pair
     other_part = trade(sent)
-    (mixed,) = call(
-        mixed_kernel,
-        [whole_low],
-        [SMEM, SMEM] + [VMEM] * (2 + QUAD),
-        out_specs=[HBM],
-        scratch=[result_whole, pltpu.SemaphoreType.DMA((half // CHUNK,))],
-    )(where, side, weight_near, other_part, *normed)
-    mixed, local_pair = lax.optimization_barrier((mixed, local_pair))
-
-    done = []
-    for quarters in FINISH:
-        count = len(quarters)
-        result = pltpu.VMEM((tokens, count * rows), low)
-        grad_keys, grad_values, gain = call(
-            functools.partial(finish_kernel, per_quarter, quarters),
-            [whole_low, whole_low, shaped((1, width), wide)],
-            [SMEM] + [VMEM] * (4 + count) + [VMEM, HBM, HBM][: len(done)],
-            out_specs=[HBM, HBM, FREE if quarters is FINISH[-1] else VMEM],
-            scratch=[result, result, pltpu.SemaphoreType.DMA((2, count * per_quarter))],
-            aliases={6 + count: 0, 7 + count: 1} if done else {},
-        )(where, key_near, value_near, *local_pair, *(suffix[j] for j in quarters), *done)
-        done = [gain, grad_keys, grad_values]
+    *early, last = FINISH
+    finished = []
+    for j in early:
+        finished += call(
+            functools.partial(finish_kernel, per_quarter, j),
+            [part_low, part_low],
+            [SMEM] + [VMEM] * 5,
+        )(where, key_near, value_near, *local_pair, suffix[j])
+    mixed, grad_keys, grad_values = call(
+        functools.partial(mixed_kernel, per_quarter, early),
+        [whole_low, whole_low, whole_low],
+        [SMEM, SMEM] + [VMEM] * (2 + QUAD + len(finished)),
+        out_specs=[HBM] * 3,
+        scratch=[result_whole, pltpu.SemaphoreType.DMA((len(finished) + 1,))],
+    )(where, side, weight_near, other_part, *normed, *finished)
+    part = pltpu.VMEM((tokens, rows), low)
+    grad_keys, grad_values, gain = call(
+        functools.partial(store_kernel, per_quarter, last),
+        [whole_low, whole_low, shaped((1, width), wide)],
+        [SMEM] + [VMEM] * (4 + QUAD) + [HBM, HBM],
+        out_specs=[HBM, HBM, HBM],
+        scratch=[part, part, pltpu.VMEM((1, width), wide), pltpu.SemaphoreType.DMA((3,))],
+        aliases={5 + QUAD: 0, 6 + QUAD: 1},
+    )(where, key_near, value_near, *local_pair, *suffix, grad_keys, grad_values)
     return mixed, grad_queries, grad_keys, grad_values, gain.reshape(width)
 
 

time: 46.4 us -> 45.1 us (0.972)
  Pallas kernels: 16.2 us -> 14.8 us
    pallas_call x16 -> x18, Pallas kernels: 16.2 us -> 14.8 us  [pinned(): return kernel(*fixed)]
  transfers between devices with their start and end apart: 16 -> 16, of which waited for: 6 -> 7; matrix products, arithmetic and copies ran while one was open for 0% -> 0% of each run, Pallas kernels for 31% -> 30%
where the time goes in v5:
time: 45.1 us; the launch traced here: 45 us
  starting transfers between devices  20.5 us (45%)
  Pallas kernels  14.8 us (33%)
  waiting for transfers between devices  8.88 us (20%)
  between operations  0.81 us (2%)
    ppermute x14, starting transfers between devices, swap(): return lax.ppermute(array, 'seq', [(i, i ^ flip) for i in range(count)])  20 us
    pallas_call x18, Pallas kernels, pinned(): return kernel(*fixed)  14.8 us
    ppermute x14, waiting for transfers between devices, swap(): return lax.ppermute(array, 'seq', [(i, i ^ flip) for i in range(count)])  8.87 us
  transfers between devices with their start and end apart: 16, of which 7 were waited for; matrix products, arithmetic and copies ran while one was open for 0% of the time, Pallas kernels for 30%

profile of v5, /device:TPU:0, one launch (start us, length us, event | category | flops | bytes accessed | tf_op | source)
XLA Modules:
  0.0 45.0 jit_solution(13246721195944037564)
XLA Ops:
  1.2 1.6 %shard_map.102 = (bf16[256,128]{1,0:T(8,128)(2,1)S(1)}, bf16[256,128]{1,0:T(8,128)(2,1)S(1)}, bf16[256,128]{1,0:T(8,128)(2,1)S(1)}, bf16[256,128]{1,0:T(8,128)(2...) custom-call(s32[1]{0:T(128)} %bitcast.place_ref, bf16[192,1024]{1,0:T(8,128)(2,1)} %key_hbm.1, ...), custom_call_target="tpu_custom_call" | custom-call | flops 1000 | bytes 1000 | tf_op jit(solution)/shard_map/pallas_call | solution.py:55
  2.7 2.6 %collective-permute-start.1 = (bf16[256,128]{1,0:T(8,128)(2,1)S(1)}, bf16[256,128]{1,0:T(8,128)(2,1)S(1)}, u32[]{:S(2)}, u32[]{:S(2)}) collective-permute-start(bf16[256,128]{1,0:T(8,128)(2,1)S(1)} %get-tuple-element.76), channel_id=1, source_target_pairs={{0,2},{2,0},{4,6},{6,4},{8,10},{10,8},{12,14},{14,12},{1,3},{3,1},... | collective-permute-start | bytes 196616 | tf_op jit(solution)/shard_map/ppermute | solution.py:333
  5.3 1.6 %collective-permute-start.2 = (bf16[256,128]{1,0:T(8,128)(2,1)S(1)}, bf16[256,128]{1,0:T(8,128)(2,1)S(1)}, u32[]{:S(2)}, u32[]{:S(2)}) collective-permute-start(bf16[256,128]{1,0:T(8,128)(2,1)S(1)} %get-tuple-element.77), channel_id=1, source_target_pairs={{0,4},{2,6},{4,0},{6,2},{8,12},{10,14},{12,8},{14,10},{1,5},{3,7},... | collective-permute-start | bytes 196616 | tf_op jit(solution)/shard_map/ppermute | solution.py:333
  6.9 3.4 %shard_map.101 = (f32[192,1024]{1,0:T(8,128)S(1)}, bf16[1024,2048]{1,0:T(8,128)(2,1)S(1)}) custom-call(s32[1]{0:T(128)} %bitcast.1.side_ref, bf16[192,1024]{1,0:T(8,128)(2,1)} %own_hbm.1, bf16[192,1024]{1,0:T(8,128)(2,1)S(1)} %collective-permute-done.other_ref, bf16[1024,2048]{1,0:T(8,128)(2,1)} %weight_hbm.1), custom_call_target="tpu_custom_call" | custom-call | flops 1000 | bytes 1000 | tf_op jit(solution)/shard_map/pallas_call | solution.py:55
  10.3 1.8 %collective-permute-done.3.b3 = bf16[256,128]{1,0:T(8,128)(2,1)S(1)} collective-permute-done((bf16[256,128]{1,0:T(8,128)(2,1)S(1)}, bf16[256,128]{1,0:T(8,128)(2,1)S(1)}, u32[]{:S(2)}, u32[]{:S(2)}) %collective-permute-start.3) | collective-permute-done | bytes 65568 | tf_op jit(solution)/shard_map/ppermute | solution.py:333
  12.1 2.7 %collective-permute-start.4 = (bf16[256,128]{1,0:T(8,128)(2,1)S(1)}, bf16[256,128]{1,0:T(8,128)(2,1)S(1)}, u32[]{:S(2)}, u32[]{:S(2)}) collective-permute-start(bf16[256,128]{1,0:T(8,128)(2,1)S(1)} %shard_map.104), channel_id=1, source_target_pairs={{0,8},{2,10},{4,12},{6,14},{8,0},{10,2},{12,4},{14,6},{1,9},{3,11}... | collective-permute-start | bytes 196616 | tf_op jit(solution)/shard_map/ppermute | solution.py:333
  14.8 1.8 %shard_map.103 = (f32[192,1024]{1,0:T(8,128)S(1)}, bf16[192,1024]{1,0:T(8,128)(2,1)S(1)}, bf16[8,192,192]{2,1,0:T(8,128)(2,1)S(1)}) custom-call(bf16[192,1024]{1,0:T(8,128)(2,1)} %query_hbm.1, bf16[192,1024]{1,0:T(8,128)(2,1)S(1)} %get-tuple-element.72.key_ref.refs_0_, bf16[192,1024]{1,0:T(8,128)(2,1)S(1)} %get-tuple-element.73.value_ref.refs_1_), custom_call_target="tpu_custom_call" | custom-call | flops 1000 | bytes 1000 | tf_op jit(solution)/shard_map/pallas_call | solution.py:55
  16.6 1.3 %collective-permute-done.4.got_ref = bf16[256,128]{1,0:T(8,128)(2,1)S(1)} collective-permute-done((bf16[256,128]{1,0:T(8,128)(2,1)S(1)}, bf16[256,128]{1,0:T(8,128)(2,1)S(1)}, u32[]{:S(2)}, u32[]{:S(2)}) %collective-permute-start.4) | collective-permute-done | bytes 65568 | tf_op jit(solution)/shard_map/ppermute | solution.py:333
  18.1 0.8 %collective-permute-start.9 = (bf16[256,128]{1,0:T(8,128)(2,1)S(1)}, bf16[256,128]{1,0:T(8,128)(2,1)S(1)}, u32[]{:S(2)}, u32[]{:S(2)}) collective-permute-start(bf16[256,128]{1,0:T(8,128)(2,1)S(1)} %get-tuple-element.94), channel_id=1, source_target_pairs={{0,6},{2,4},{4,2},{6,0},{8,14},{10,12},{12,10},{14,8},{1,7},{3,5},... | collective-permute-start | bytes 196616 | tf_op jit(solution)/shard_map/ppermute | solution.py:333
  19.5 2.1 %collective-permute-start.5 = (bf16[256,128]{1,0:T(8,128)(2,1)S(1)}, bf16[256,128]{1,0:T(8,128)(2,1)S(1)}, u32[]{:S(2)}, u32[]{:S(2)}) collective-permute-start(bf16[256,128]{1,0:T(8,128)(2,1)S(1)} %get-tuple-element.90), channel_id=1, source_target_pairs={{0,2},{2,0},{4,6},{6,4},{8,10},{10,8},{12,14},{14,12},{1,3},{3,1},... | collective-permute-start | bytes 196616 | tf_op jit(solution)/shard_map/ppermute | solution.py:333
  21.6 1.7 %collective-permute-done.9.prefix_ref.rest_11_ = bf16[256,128]{1,0:T(8,128)(2,1)S(1)} collective-permute-done((bf16[256,128]{1,0:T(8,128)(2,1)S(1)}, bf16[256,128]{1,0:T(8,128)(2,1)S(1)}, u32[]{:S(2)}, u32[]{:S(2)}) %collective-permute-start.9) | collective-permute-done | bytes 65568 | tf_op jit(solution)/shard_map/ppermute | solution.py:333
  23.8 0.8 %collective-permute-start.10 = (bf16[272,128]{1,0:T(8,128)(2,1)S(1)}, bf16[272,128]{1,0:T(8,128)(2,1)S(1)}, u32[]{:S(2)}, u32[]{:S(2)}) collective-permute-start(bf16[272,128]{1,0:T(8,128)(2,1)S(1)} %get-tuple-element.95), channel_id=1, source_target_pairs={{0,6},{2,4},{4,2},{6,0},{8,14},{10,12},{12,10},{14,8},{1,7},{3,5},... | collective-permute-start | bytes 208904 | tf_op jit(solution)/shard_map/ppermute | solution.py:333
  25.1 0.7 %collective-permute-start.8 = (bf16[272,128]{1,0:T(8,128)(2,1)S(1)}, bf16[272,128]{1,0:T(8,128)(2,1)S(1)}, u32[]{:S(2)}, u32[]{:S(2)}) collective-permute-start(bf16[272,128]{1,0:T(8,128)(2,1)S(1)} %get-tuple-element.93), channel_id=1, source_target_pairs={{0,4},{2,6},{4,0},{6,2},{8,12},{10,14},{12,8},{14,10},{1,5},{3,7},... | collective-permute-start | bytes 208904 | tf_op jit(solution)/shard_map/ppermute | solution.py:333
  26.3 2.1 %collective-permute-start.6 = (bf16[272,128]{1,0:T(8,128)(2,1)S(1)}, bf16[272,128]{1,0:T(8,128)(2,1)S(1)}, u32[]{:S(2)}, u32[]{:S(2)}) collective-permute-start(bf16[272,128]{1,0:T(8,128)(2,1)S(1)} %get-tuple-element.91), channel_id=1, source_target_pairs={{0,2},{2,0},{4,6},{6,4},{8,10},{10,8},{12,14},{14,12},{1,3},{3,1},... | collective-permute-start | bytes 208904 | tf_op jit(solution)/shard_map/ppermute | solution.py:333
  28.9 2.1 %shard_map.110 = (bf16[192,1024]{1,0:T(8,128)(2,1)}, bf16[192,1024]{1,0:T(8,128)(2,1)S(1)}, bf16[8,192,192]{2,1,0:T(8,128)(2,1)S(1)}) custom-call(s32[1]{0:T(128)} %bitcast.place_ref, s32[1]{0:T(128)} %bitcast.1.side_ref, bf16[192,1024]{1,0:T(8,128)(2,1)S(1)} %get-tuple-element.72.key_ref.refs_0_, bf16[192,1024]{1,0:T(8,128)(2,1)S(1)} %get-tuple-element.73.value_ref.refs_1_, ...), custom_call_target="tpu_custom_call" | custom-call | flops 1000 | bytes 1000 | tf_op jit(solution)/shard_map/pallas_call | solution.py:55
  31.1 2.3 %collective-permute-start.11 = (bf16[272,128]{1,0:T(8,128)(2,1)S(1)}, bf16[272,128]{1,0:T(8,128)(2,1)S(1)}, u32[]{:S(2)}, u32[]{:S(2)}) collective-permute-start(bf16[272,128]{1,0:T(8,128)(2,1)S(1)} %get-tuple-element.109), channel_id=1, source_target_pairs={{0,8},{2,10},{4,12},{6,14},{8,0},{10,2},{12,4},{14,6},{1,9},{3,11}... | collective-permute-start | bytes 208904 | tf_op jit(solution)/shard_map/ppermute | solution.py:333
  33.4 0.7 %shard_map.112 = (f32[192,1024]{1,0:T(8,128)S(1)}, f32[192,1024]{1,0:T(8,128)S(1)}) custom-call(s32[1]{0:T(128)} %bitcast.place_ref, bf16[192,1024]{1,0:T(8,128)(2,1)S(1)} %get-tuple-element.74.query_ref, bf16[8,192,192]{2,1,0:T(8,128)(2,1)S(1)} %get-tuple-element.110.score_ref, bf16[8,192,192]{2,1,0:T(8,128)(2,1)S(1)} %get-tuple-element.111.grad_score_ref, ...), custom_call_target="tpu_custom_call" | custom-call | flops 1000 | bytes 1000 | tf_op jit(solution)/shard_map/pallas_call | solution.py:55
  34.2 2.2 %collective-permute-done.11.got_ref = bf16[272,128]{1,0:T(8,128)(2,1)S(1)} collective-permute-done((bf16[272,128]{1,0:T(8,128)(2,1)S(1)}, bf16[272,128]{1,0:T(8,128)(2,1)S(1)}, u32[]{:S(2)}, u32[]{:S(2)}) %collective-permute-start.11) | collective-permute-done | bytes 69664 | tf_op jit(solution)/shard_map/ppermute | solution.py:333
  36.6 1.4 %collective-permute-start.14 = (bf16[272,128]{1,0:T(8,128)(2,1)S(1)}, bf16[272,128]{1,0:T(8,128)(2,1)S(1)}, u32[]{:S(2)}, u32[]{:S(2)}) collective-permute-start(bf16[272,128]{1,0:T(8,128)(2,1)S(1)} %get-tuple-element.126), channel_id=1, source_target_pairs={{0,4},{2,6},{4,0},{6,2},{8,12},{10,14},{12,8},{14,10},{1,5},{3,7},... | collective-permute-start | bytes 208904 | tf_op jit(solution)/shard_map/ppermute | solution.py:333
  38.6 1.5 %collective-permute-start.15 = (bf16[272,128]{1,0:T(8,128)(2,1)S(1)}, bf16[272,128]{1,0:T(8,128)(2,1)S(1)}, u32[]{:S(2)}, u32[]{:S(2)}) collective-permute-start(bf16[272,128]{1,0:T(8,128)(2,1)S(1)} %get-tuple-element.131), channel_id=1, source_target_pairs={{0,6},{2,4},{4,2},{6,0},{8,14},{10,12},{12,10},{14,8},{1,7},{3,5},... | collective-permute-start | bytes 208904 | tf_op jit(solution)/shard_map/ppermute | solution.py:333
  40.3 0.9 %collective-permute-done.14.refs_4_.rest_2_ = bf16[272,128]{1,0:T(8,128)(2,1)S(1)} collective-permute-done((bf16[272,128]{1,0:T(8,128)(2,1)S(1)}, bf16[272,128]{1,0:T(8,128)(2,1)S(1)}, u32[]{:S(2)}, u32[]{:S(2)}) %collective-permute-start.14) | collective-permute-done | bytes 69664 | tf_op jit(solution)/shard_map/ppermute | solution.py:333
  41.4 0.9 %collective-permute-done.13.refs_4_.rest_1_ = bf16[272,128]{1,0:T(8,128)(2,1)S(1)} collective-permute-done((bf16[272,128]{1,0:T(8,128)(2,1)S(1)}, bf16[272,128]{1,0:T(8,128)(2,1)S(1)}, u32[]{:S(2)}, u32[]{:S(2)}) %collective-permute-start.13) | collective-permute-done | bytes 69664 | tf_op jit(solution)/shard_map/ppermute | solution.py:333
  42.5 1.4 %shard_map.117 = (bf16[192,1024]{1,0:T(8,128)(2,1)}, bf16[192,1024]{1,0:T(8,128)(2,1)}, bf16[192,1024]{1,0:T(8,128)(2,1)}) custom-call(s32[1]{0:T(128)} %bitcast.place_ref, s32[1]{0:T(128)} %bitcast.1.side_ref, bf16[1024,2048]{1,0:T(8,128)(2,1)S(1)} %get-tuple-element.71.weight_ref, bf16[192,1024]{1,0:T(8,128)(2,1)S(1)} %collective-permute-done.12.other_ref, ...), custom_call_target="tpu_custom_call" | custom-call | flops 1000 | bytes 1000 | tf_op jit(solution)/shard_map/pallas_call | solution.py:55
  44.1 0.9 %shard_map.118 = (bf16[192,1024]{1,0:T(8,128)(2,1)}, bf16[192,1024]{1,0:T(8,128)(2,1)}, f32[1,1024]{1,0:T(1,128)}) custom-call(s32[1]{0:T(128)} %bitcast.place_ref, bf16[192,1024]{1,0:T(8,128)(2,1)S(1)} %get-tuple-element.72.key_ref.refs_0_, ...), custom_call_target="tpu_custom_call", output_to_operand_aliasing={{0}: (9, {}), {1}: (10, {})} | custom-call | flops 1000 | bytes 1000 | tf_op jit(solution)/shard_map/pallas_call | solution.py:55
  (28 shorter events, 4.8 us)
Async XLA Ops:
  0.6 22.7 %copy-start = (f32[1024]{0:T(1024)S(1)}, f32[1024]{0:T(1024)}, u32[]{:S(2)}) copy-start(f32[1024]{0:T(1024)} %param.10) | copy-start | bytes 12292
  0.6 6.3 %collective-permute-start = (bf16[192,1024]{1,0:T(8,128)(2,1)}, bf16[192,1024]{1,0:T(8,128)(2,1)S(1)}, u32[]{:S(2)}, u32[]{:S(2)}) collective-permute-start(bf16[192,1024]{1,0:T(8,128)(2,1)} %own_hbm.1), channel_id=1, source_target_pairs={{0,1},{1,0},{2,3},{3,2},{4,5},{5,4},{6,7},{7,6},{8,9},{9,8},{10,11... | collective-permute-start | bytes 1179656 | tf_op jit(solution)/shard_map/ppermute | solution.py:337
  2.7 7.6 %collective-permute-start.1 = (bf16[256,128]{1,0:T(8,128)(2,1)S(1)}, bf16[256,128]{1,0:T(8,128)(2,1)S(1)}, u32[]{:S(2)}, u32[]{:S(2)}) collective-permute-start(bf16[256,128]{1,0:T(8,128)(2,1)S(1)} %get-tuple-element.76), channel_id=1, source_target_pairs={{0,2},{2,0},{4,6},{6,4},{8,10},{10,8},{12,14},{14,12},{1,3},{3,1},... | collective-permute-start | bytes 196616 | tf_op jit(solution)/shard_map/ppermute | solution.py:333
  5.3 5.0 %collective-permute-start.2 = (bf16[256,128]{1,0:T(8,128)(2,1)S(1)}, bf16[256,128]{1,0:T(8,128)(2,1)S(1)}, u32[]{:S(2)}, u32[]{:S(2)}) collective-permute-start(bf16[256,128]{1,0:T(8,128)(2,1)S(1)} %get-tuple-element.77), channel_id=1, source_target_pairs={{0,4},{2,6},{4,0},{6,2},{8,12},{10,14},{12,8},{14,10},{1,5},{3,7},... | collective-permute-start | bytes 196616 | tf_op jit(solution)/shard_map/ppermute | solution.py:333
  6.9 5.2 %collective-permute-start.3 = (bf16[256,128]{1,0:T(8,128)(2,1)S(1)}, bf16[256,128]{1,0:T(8,128)(2,1)S(1)}, u32[]{:S(2)}, u32[]{:S(2)}) collective-permute-start(bf16[256,128]{1,0:T(8,128)(2,1)S(1)} %get-tuple-element.78), channel_id=1, source_target_pairs={{0,6},{2,4},{4,2},{6,0},{8,14},{10,12},{12,10},{14,8},{1,7},{3,5},... | collective-permute-start | bytes 196616 | tf_op jit(solution)/shard_map/ppermute | solution.py:333
  12.1 5.8 %collective-permute-start.4 = (bf16[256,128]{1,0:T(8,128)(2,1)S(1)}, bf16[256,128]{1,0:T(8,128)(2,1)S(1)}, u32[]{:S(2)}, u32[]{:S(2)}) collective-permute-start(bf16[256,128]{1,0:T(8,128)(2,1)S(1)} %shard_map.104), channel_id=1, source_target_pairs={{0,8},{2,10},{4,12},{6,14},{8,0},{10,2},{12,4},{14,6},{1,9},{3,11}... | collective-permute-start | bytes 196616 | tf_op jit(solution)/shard_map/ppermute | solution.py:333
  18.1 5.2 %collective-permute-start.9 = (bf16[256,128]{1,0:T(8,128)(2,1)S(1)}, bf16[256,128]{1,0:T(8,128)(2,1)S(1)}, u32[]{:S(2)}, u32[]{:S(2)}) collective-permute-start(bf16[256,128]{1,0:T(8,128)(2,1)S(1)} %get-tuple-element.94), channel_id=1, source_target_pairs={{0,6},{2,4},{4,2},{6,0},{8,14},{10,12},{12,10},{14,8},{1,7},{3,5},... | collective-permute-start | bytes 196616 | tf_op jit(solution)/shard_map/ppermute | solution.py:333
  18.9 5.7 %collective-permute-start.7 = (bf16[256,128]{1,0:T(8,128)(2,1)S(1)}, bf16[256,128]{1,0:T(8,128)(2,1)S(1)}, u32[]{:S(2)}, u32[]{:S(2)}) collective-permute-start(bf16[256,128]{1,0:T(8,128)(2,1)S(1)} %get-tuple-element.92), channel_id=1, source_target_pairs={{0,4},{2,6},{4,0},{6,2},{8,12},{10,14},{12,8},{14,10},{1,5},{3,7},... | collective-permute-start | bytes 196616 | tf_op jit(solution)/shard_map/ppermute | solution.py:333
  19.5 6.3 %collective-permute-start.5 = (bf16[256,128]{1,0:T(8,128)(2,1)S(1)}, bf16[256,128]{1,0:T(8,128)(2,1)S(1)}, u32[]{:S(2)}, u32[]{:S(2)}) collective-permute-start(bf16[256,128]{1,0:T(8,128)(2,1)S(1)} %get-tuple-element.90), channel_id=1, source_target_pairs={{0,2},{2,0},{4,6},{6,4},{8,10},{10,8},{12,14},{14,12},{1,3},{3,1},... | collective-permute-start | bytes 196616 | tf_op jit(solution)/shard_map/ppermute | solution.py:333
  23.8 7.2 %collective-permute-start.10 = (bf16[272,128]{1,0:T(8,128)(2,1)S(1)}, bf16[272,128]{1,0:T(8,128)(2,1)S(1)}, u32[]{:S(2)}, u32[]{:S(2)}) collective-permute-start(bf16[272,128]{1,0:T(8,128)(2,1)S(1)} %get-tuple-element.95), channel_id=1, source_target_pairs={{0,6},{2,4},{4,2},{6,0},{8,14},{10,12},{12,10},{14,8},{1,7},{3,5},... | collective-permute-start | bytes 208904 | tf_op jit(solution)/shard_map/ppermute | solution.py:333
  25.1 5.9 %collective-permute-start.8 = (bf16[272,128]{1,0:T(8,128)(2,1)S(1)}, bf16[272,128]{1,0:T(8,128)(2,1)S(1)}, u32[]{:S(2)}, u32[]{:S(2)}) collective-permute-start(bf16[272,128]{1,0:T(8,128)(2,1)S(1)} %get-tuple-element.93), channel_id=1, source_target_pairs={{0,4},{2,6},{4,0},{6,2},{8,12},{10,14},{12,8},{14,10},{1,5},{3,7},... | collective-permute-start | bytes 208904 | tf_op jit(solution)/shard_map/ppermute | solution.py:333
  26.3 4.7 %collective-permute-start.6 = (bf16[272,128]{1,0:T(8,128)(2,1)S(1)}, bf16[272,128]{1,0:T(8,128)(2,1)S(1)}, u32[]{:S(2)}, u32[]{:S(2)}) collective-permute-start(bf16[272,128]{1,0:T(8,128)(2,1)S(1)} %get-tuple-element.91), channel_id=1, source_target_pairs={{0,2},{2,0},{4,6},{6,4},{8,10},{10,8},{12,14},{14,12},{1,3},{3,1},... | collective-permute-start | bytes 208904 | tf_op jit(solution)/shard_map/ppermute | solution.py:333
  31.1 5.3 %collective-permute-start.11 = (bf16[272,128]{1,0:T(8,128)(2,1)S(1)}, bf16[272,128]{1,0:T(8,128)(2,1)S(1)}, u32[]{:S(2)}, u32[]{:S(2)}) collective-permute-start(bf16[272,128]{1,0:T(8,128)(2,1)S(1)} %get-tuple-element.109), channel_id=1, source_target_pairs={{0,8},{2,10},{4,12},{6,14},{8,0},{10,2},{12,4},{14,6},{1,9},{3,11}... | collective-permute-start | bytes 208904 | tf_op jit(solution)/shard_map/ppermute | solution.py:333
  36.4 6.2 %collective-permute-start.12 = (bf16[192,1024]{1,0:T(8,128)(2,1)S(1)}, bf16[192,1024]{1,0:T(8,128)(2,1)S(1)}, u32[]{:S(2)}, u32[]{:S(2)}) collective-permute-start(bf16[192,1024]{1,0:T(8,128)(2,1)S(1)} %get-tuple-element.115), channel_id=1, source_target_pairs={{0,1},{1,0},{2,3},{3,2},{4,5},{5,4},{6,7},{7,6},{8,9},{9,8},{10,11... | collective-permute-start | bytes 1179656 | tf_op jit(solution)/shard_map/ppermute | solution.py:337
  36.6 4.7 %collective-permute-start.14 = (bf16[272,128]{1,0:T(8,128)(2,1)S(1)}, bf16[272,128]{1,0:T(8,128)(2,1)S(1)}, u32[]{:S(2)}, u32[]{:S(2)}) collective-permute-start(bf16[272,128]{1,0:T(8,128)(2,1)S(1)} %get-tuple-element.126), channel_id=1, source_target_pairs={{0,4},{2,6},{4,0},{6,2},{8,12},{10,14},{12,8},{14,10},{1,5},{3,7},... | collective-permute-start | bytes 208904 | tf_op jit(solution)/shard_map/ppermute | solution.py:333
  38.0 4.3 %collective-permute-start.13 = (bf16[272,128]{1,0:T(8,128)(2,1)S(1)}, bf16[272,128]{1,0:T(8,128)(2,1)S(1)}, u32[]{:S(2)}, u32[]{:S(2)}) collective-permute-start(bf16[272,128]{1,0:T(8,128)(2,1)S(1)} %get-tuple-element.123), channel_id=1, source_target_pairs={{0,2},{2,0},{4,6},{6,4},{8,10},{10,8},{12,14},{14,12},{1,3},{3,1},... | collective-permute-start | bytes 208904 | tf_op jit(solution)/shard_map/ppermute | solution.py:333
  38.6 5.4 %collective-permute-start.15 = (bf16[272,128]{1,0:T(8,128)(2,1)S(1)}, bf16[272,128]{1,0:T(8,128)(2,1)S(1)}, u32[]{:S(2)}, u32[]{:S(2)}) collective-permute-start(bf16[272,128]{1,0:T(8,128)(2,1)S(1)} %get-tuple-element.131), channel_id=1, source_target_pairs={{0,6},{2,4},{4,2},{6,0},{8,14},{10,12},{12,10},{14,8},{1,7},{3,5},... | collective-permute-start | bytes 208904 | tf_op jit(solution)/shard_map/ppermute | solution.py:333

commit v6 on v5

--- a/solution.py
+++ b/solution.py
@@ -64,8 +64,18 @@
             yield j, i, pl.ds(pl.multiple_of(start, DH), DH)
 
 
+def states(per_quarter, quarters, place, key_ref, value_ref, out_refs):
+    for j, i, head in head_slices(place, per_quarter, quarters):
+        state = dot(key_ref[:, head], value_ref[:, head], (0, 0))
+        out_refs[j - quarters[0]][i * DH : (i + 1) * DH, :] = state.astype(low)
+
+
+def own_state_kernel(per_quarter, place_ref, key_ref, value_ref, *out_refs):
+    states(per_quarter, range(1), place_ref[0], key_ref, value_ref, out_refs)
+
+
 def state_kernel(per_quarter, place_ref, key_hbm, value_hbm, *rest):
-    out_refs, key_ref, value_ref, sems = rest[:QUAD], rest[QUAD], rest[QUAD + 1], rest[QUAD + 2]
+    out_refs, (key_ref, value_ref, sems) = rest[: QUAD - 1], rest[QUAD - 1 :]
     copies = [
         pltpu.make_async_copy(key_hbm, key_ref, sems.at[0]),
         pltpu.make_async_copy(value_hbm, value_ref, sems.at[1]),
@@ -74,9 +84,7 @@
         copy.start()
     for copy in copies:
         copy.wait()
-    for j, i, head in head_slices(place_ref[0], per_quarter):
-        state = dot(key_ref[:, head], value_ref[:, head], (0, 0))
-        out_refs[j][i * DH : (i + 1) * DH, :] = state.astype(low)
+    states(per_quarter, range(1, QUAD), place_ref[0], key_ref, value_ref, out_refs)
 
 
 def causal(tokens):
@@ -306,19 +314,21 @@
     earlier = refs.pop(0) if gains else None
     blocks = (b0, b1, b2, b3)
     rows = got_ref.shape[0] - (EXTRA if gains else 0)
-    quarter = place_ref[0] & (QUAD - 1)
     outside = jnp.where(is_beyond(place_ref, step, backward), got_ref[:rows, :].astype(wide), 0.0)
     if past:
         outside = outside + outside_ref[...]
     states = [block[:rows, :].astype(wide) for block in blocks]
+    pairs = (states[0] + states[1], states[2] + states[3])
+    near = ((place_ref[0] & 1) != 0) != backward
+    far = ((place_ref[0] & 2) != 0) != backward
+    bases = (
+        outside + jnp.where(far, pairs[1], 0.0),
+        outside + jnp.where(far, 0.0, pairs[0]),
+    )
     for j in range(QUAD):
-        result = outside
-        for i in range(QUAD):
-            if i == j:
-                continue
-            source, target = quarter ^ i, quarter ^ j
-            counts = (source > target) if backward else (source < target)
-            result = result + jnp.where(counts, states[i], 0.0)
+        neighbour = states[j ^ 1]
+        own = jnp.where(near, 0.0, neighbour) if j & 1 else jnp.where(near, neighbour, 0.0)
+        result = bases[j >> 1] + own
         refs[j][:rows, :] = result.astype(low)
         if gains:
             refs[j][rows:, :] = jnp.zeros((EXTRA, DH), low)
@@ -403,10 +413,16 @@
     other_grad = trade(grad_output)
     *parts, key_near, value_near = call(
         functools.partial(state_kernel, per_quarter),
-        [shaped((rows, DH), low)] * QUAD + [whole_low, whole_low],
+        [shaped((rows, DH), low)] * (QUAD - 1) + [whole_low, whole_low],
         [SMEM, HBM, HBM],
         scratch=[two_sems],
     )(where, key_vectors, values)
+    (own_part,) = call(
+        functools.partial(own_state_kernel, per_quarter),
+        [shaped((rows, DH), low)],
+        [SMEM, VMEM, VMEM],
+    )(where, key_near, value_near)
+    parts = [own_part, *parts]
     squares = shaped((heads, tokens, tokens), low)
     local, query_near, scores = call(
         functools.partial(local_kernel, heads),

time: 45.1 us -> 45 us (level)
    pallas_call x18 -> x19, Pallas kernels: 14.8 us -> 14.9 us  [pinned(): return kernel(*fixed)]
  transfers between devices with their start and end apart: 16 -> 16, of which waited for: 7 -> 7; matrix products, arithmetic and copies ran while one was open for 0% -> 0% of each run, Pallas kernels for 30% -> 31%
where the time goes in v6:
time: 45 us; the launch traced here: 44.9 us
  starting transfers between devices  20.5 us (46%)
  Pallas kernels  14.9 us (33%)
  waiting for transfers between devices  8.59 us (19%)
  between operations  0.82 us (2%)
    ppermute x14, starting transfers between devices, swap(): return lax.ppermute(array, 'seq', [(i, i ^ flip) for i in range(count)])  20 us
    pallas_call x19, Pallas kernels, pinned(): return kernel(*fixed)  14.9 us
    ppermute x14, waiting for transfers between devices, swap(): return lax.ppermute(array, 'seq', [(i, i ^ flip) for i in range(count)])  8.59 us
  transfers between devices with their start and end apart: 16, of which 7 were waited for; matrix products, arithmetic and copies ran while one was open for 0% of the time, Pallas kernels for 31%

profile of v6, /device:TPU:0, one launch (start us, length us, event | category | flops | bytes accessed | tf_op | source)
XLA Modules:
  0.0 44.9 jit_solution(473580031493057015)
XLA Ops:
  1.2 1.5 %shard_map.102 = (bf16[256,128]{1,0:T(8,128)(2,1)S(1)}, bf16[256,128]{1,0:T(8,128)(2,1)S(1)}, bf16[256,128]{1,0:T(8,128)(2,1)S(1)}, bf16[192,1024]{1,0:T(8,128)(2,1)S(1)}, bf16[192,1024]{1,0:T(8,128)(2,1)S(1)}) custom-call(s32[1]{0:T(128)} %bitcast.place_ref, bf16[192,1024]{1,0:T(8,128)(2,1)} %key_hbm.1, bf16[192,1024]{1,0:T(8,128)(2,1)} %value_hbm.1), custom_call_target="tpu_custom_call" | custom-call | flops 1000 | bytes 1000 | tf_op jit(solution)/shard_map/pallas_call | solution.py:55
  2.7 2.6 %collective-permute-start.1 = (bf16[256,128]{1,0:T(8,128)(2,1)S(1)}, bf16[256,128]{1,0:T(8,128)(2,1)S(1)}, u32[]{:S(2)}, u32[]{:S(2)}) collective-permute-start(bf16[256,128]{1,0:T(8,128)(2,1)S(1)} %get-tuple-element.74), channel_id=1, source_target_pairs={{0,2},{2,0},{4,6},{6,4},{8,10},{10,8},{12,14},{14,12},{1,3},{3,1},... | collective-permute-start | bytes 196616 | tf_op jit(solution)/shard_map/ppermute | solution.py:343
  5.3 1.6 %collective-permute-start.2 = (bf16[256,128]{1,0:T(8,128)(2,1)S(1)}, bf16[256,128]{1,0:T(8,128)(2,1)S(1)}, u32[]{:S(2)}, u32[]{:S(2)}) collective-permute-start(bf16[256,128]{1,0:T(8,128)(2,1)S(1)} %get-tuple-element.75), channel_id=1, source_target_pairs={{0,4},{2,6},{4,0},{6,2},{8,12},{10,14},{12,8},{14,10},{1,5},{3,7},... | collective-permute-start | bytes 196616 | tf_op jit(solution)/shard_map/ppermute | solution.py:343
  7.1 3.4 %shard_map.101 = (f32[192,1024]{1,0:T(8,128)S(1)}, bf16[1024,2048]{1,0:T(8,128)(2,1)S(1)}) custom-call(s32[1]{0:T(128)} %bitcast.1.side_ref, bf16[192,1024]{1,0:T(8,128)(2,1)} %own_hbm.1, bf16[192,1024]{1,0:T(8,128)(2,1)S(1)} %collective-permute-done.other_ref, bf16[1024,2048]{1,0:T(8,128)(2,1)} %weight_hbm.1), custom_call_target="tpu_custom_call" | custom-call | flops 1000 | bytes 1000 | tf_op jit(solution)/shard_map/pallas_call | solution.py:55
  10.5 1.5 %collective-permute-done.3.b3 = bf16[256,128]{1,0:T(8,128)(2,1)S(1)} collective-permute-done((bf16[256,128]{1,0:T(8,128)(2,1)S(1)}, bf16[256,128]{1,0:T(8,128)(2,1)S(1)}, u32[]{:S(2)}, u32[]{:S(2)}) %collective-permute-start.3) | collective-permute-done | bytes 65568 | tf_op jit(solution)/shard_map/ppermute | solution.py:343
  12.0 2.7 %collective-permute-start.4 = (bf16[256,128]{1,0:T(8,128)(2,1)S(1)}, bf16[256,128]{1,0:T(8,128)(2,1)S(1)}, u32[]{:S(2)}, u32[]{:S(2)}) collective-permute-start(bf16[256,128]{1,0:T(8,128)(2,1)S(1)} %shard_map.105), channel_id=1, source_target_pairs={{0,8},{2,10},{4,12},{6,14},{8,0},{10,2},{12,4},{14,6},{1,9},{3,11}... | collective-permute-start | bytes 196616 | tf_op jit(solution)/shard_map/ppermute | solution.py:343
  14.7 1.8 %shard_map.103 = (f32[192,1024]{1,0:T(8,128)S(1)}, bf16[192,1024]{1,0:T(8,128)(2,1)S(1)}, bf16[8,192,192]{2,1,0:T(8,128)(2,1)S(1)}) custom-call(bf16[192,1024]{1,0:T(8,128)(2,1)} %query_hbm.1, bf16[192,1024]{1,0:T(8,128)(2,1)S(1)} %get-tuple-element.71.key_ref.refs_0_, bf16[192,1024]{1,0:T(8,128)(2,1)S(1)} %get-tuple-element.72.value_ref.refs_1_), custom_call_target="tpu_custom_call" | custom-call | flops 1000 | bytes 1000 | tf_op jit(solution)/shard_map/pallas_call | solution.py:55
  16.5 1.4 %collective-permute-done.4.got_ref = bf16[256,128]{1,0:T(8,128)(2,1)S(1)} collective-permute-done((bf16[256,128]{1,0:T(8,128)(2,1)S(1)}, bf16[256,128]{1,0:T(8,128)(2,1)S(1)}, u32[]{:S(2)}, u32[]{:S(2)}) %collective-permute-start.4) | collective-permute-done | bytes 65568 | tf_op jit(solution)/shard_map/ppermute | solution.py:343
  18.0 1.0 %collective-permute-start.9 = (bf16[256,128]{1,0:T(8,128)(2,1)S(1)}, bf16[256,128]{1,0:T(8,128)(2,1)S(1)}, u32[]{:S(2)}, u32[]{:S(2)}) collective-permute-start(bf16[256,128]{1,0:T(8,128)(2,1)S(1)} %get-tuple-element.92), channel_id=1, source_target_pairs={{0,6},{2,4},{4,2},{6,0},{8,14},{10,12},{12,10},{14,8},{1,7},{3,5},... | collective-permute-start | bytes 196616 | tf_op jit(solution)/shard_map/ppermute | solution.py:343
  19.0 0.8 %collective-permute-start.7 = (bf16[256,128]{1,0:T(8,128)(2,1)S(1)}, bf16[256,128]{1,0:T(8,128)(2,1)S(1)}, u32[]{:S(2)}, u32[]{:S(2)}) collective-permute-start(bf16[256,128]{1,0:T(8,128)(2,1)S(1)} %get-tuple-element.90), channel_id=1, source_target_pairs={{0,4},{2,6},{4,0},{6,2},{8,12},{10,14},{12,8},{14,10},{1,5},{3,7},... | collective-permute-start | bytes 196616 | tf_op jit(solution)/shard_map/ppermute | solution.py:343
  19.7 1.8 %collective-permute-start.5 = (bf16[256,128]{1,0:T(8,128)(2,1)S(1)}, bf16[256,128]{1,0:T(8,128)(2,1)S(1)}, u32[]{:S(2)}, u32[]{:S(2)}) collective-permute-start(bf16[256,128]{1,0:T(8,128)(2,1)S(1)} %get-tuple-element.88), channel_id=1, source_target_pairs={{0,2},{2,0},{4,6},{6,4},{8,10},{10,8},{12,14},{14,12},{1,3},{3,1},... | collective-permute-start | bytes 196616 | tf_op jit(solution)/shard_map/ppermute | solution.py:343
  21.6 1.7 %collective-permute-done.9.prefix_ref.rest_11_ = bf16[256,128]{1,0:T(8,128)(2,1)S(1)} collective-permute-done((bf16[256,128]{1,0:T(8,128)(2,1)S(1)}, bf16[256,128]{1,0:T(8,128)(2,1)S(1)}, u32[]{:S(2)}, u32[]{:S(2)}) %collective-permute-start.9) | collective-permute-done | bytes 65568 | tf_op jit(solution)/shard_map/ppermute | solution.py:343
  23.7 1.0 %collective-permute-start.10 = (bf16[272,128]{1,0:T(8,128)(2,1)S(1)}, bf16[272,128]{1,0:T(8,128)(2,1)S(1)}, u32[]{:S(2)}, u32[]{:S(2)}) collective-permute-start(bf16[272,128]{1,0:T(8,128)(2,1)S(1)} %get-tuple-element.93), channel_id=1, source_target_pairs={{0,6},{2,4},{4,2},{6,0},{8,14},{10,12},{12,10},{14,8},{1,7},{3,5},... | collective-permute-start | bytes 208904 | tf_op jit(solution)/shard_map/ppermute | solution.py:343
  25.1 0.8 %collective-permute-start.8 = (bf16[272,128]{1,0:T(8,128)(2,1)S(1)}, bf16[272,128]{1,0:T(8,128)(2,1)S(1)}, u32[]{:S(2)}, u32[]{:S(2)}) collective-permute-start(bf16[272,128]{1,0:T(8,128)(2,1)S(1)} %get-tuple-element.91), channel_id=1, source_target_pairs={{0,4},{2,6},{4,0},{6,2},{8,12},{10,14},{12,8},{14,10},{1,5},{3,7},... | collective-permute-start | bytes 208904 | tf_op jit(solution)/shard_map/ppermute | solution.py:343
  26.5 1.9 %collective-permute-start.6 = (bf16[272,128]{1,0:T(8,128)(2,1)S(1)}, bf16[272,128]{1,0:T(8,128)(2,1)S(1)}, u32[]{:S(2)}, u32[]{:S(2)}) collective-permute-start(bf16[272,128]{1,0:T(8,128)(2,1)S(1)} %get-tuple-element.89), channel_id=1, source_target_pairs={{0,2},{2,0},{4,6},{6,4},{8,10},{10,8},{12,14},{14,12},{1,3},{3,1},... | collective-permute-start | bytes 208904 | tf_op jit(solution)/shard_map/ppermute | solution.py:343
  28.8 2.1 %shard_map.111 = (bf16[192,1024]{1,0:T(8,128)(2,1)}, bf16[192,1024]{1,0:T(8,128)(2,1)S(1)}, bf16[8,192,192]{2,1,0:T(8,128)(2,1)S(1)}) custom-call(s32[1]{0:T(128)} %bitcast.place_ref, s32[1]{0:T(128)} %bitcast.1.side_ref, bf16[192,1024]{1,0:T(8,128)(2,1)S(1)} %get-tuple-element.71.key_ref.refs_0_, bf16[192,1024]{1,0:T(8,128)(2,1)S(1)} %get-tuple-element.72.value_ref.refs_1_, ...), custom_call_target="tpu_custom_call" | custom-call | flops 1000 | bytes 1000 | tf_op jit(solution)/shard_map/pallas_call | solution.py:55
  31.0 2.4 %collective-permute-start.11 = (bf16[272,128]{1,0:T(8,128)(2,1)S(1)}, bf16[272,128]{1,0:T(8,128)(2,1)S(1)}, u32[]{:S(2)}, u32[]{:S(2)}) collective-permute-start(bf16[272,128]{1,0:T(8,128)(2,1)S(1)} %get-tuple-element.107), channel_id=1, source_target_pairs={{0,8},{2,10},{4,12},{6,14},{8,0},{10,2},{12,4},{14,6},{1,9},{3,11}... | collective-permute-start | bytes 208904 | tf_op jit(solution)/shard_map/ppermute | solution.py:343
  34.1 2.1 %collective-permute-done.11.got_ref = bf16[272,128]{1,0:T(8,128)(2,1)S(1)} collective-permute-done((bf16[272,128]{1,0:T(8,128)(2,1)S(1)}, bf16[272,128]{1,0:T(8,128)(2,1)S(1)}, u32[]{:S(2)}, u32[]{:S(2)}) %collective-permute-start.11) | collective-permute-done | bytes 69664 | tf_op jit(solution)/shard_map/ppermute | solution.py:343
  36.4 1.5 %collective-permute-start.14 = (bf16[272,128]{1,0:T(8,128)(2,1)S(1)}, bf16[272,128]{1,0:T(8,128)(2,1)S(1)}, u32[]{:S(2)}, u32[]{:S(2)}) collective-permute-start(bf16[272,128]{1,0:T(8,128)(2,1)S(1)} %get-tuple-element.124), channel_id=1, source_target_pairs={{0,4},{2,6},{4,0},{6,2},{8,12},{10,14},{12,8},{14,10},{1,5},{3,7},... | collective-permute-start | bytes 208904 | tf_op jit(solution)/shard_map/ppermute | solution.py:343
  38.5 1.5 %collective-permute-start.15 = (bf16[272,128]{1,0:T(8,128)(2,1)S(1)}, bf16[272,128]{1,0:T(8,128)(2,1)S(1)}, u32[]{:S(2)}, u32[]{:S(2)}) collective-permute-start(bf16[272,128]{1,0:T(8,128)(2,1)S(1)} %get-tuple-element.129), channel_id=1, source_target_pairs={{0,6},{2,4},{4,2},{6,0},{8,14},{10,12},{12,10},{14,8},{1,7},{3,5},... | collective-permute-start | bytes 208904 | tf_op jit(solution)/shard_map/ppermute | solution.py:343
  40.2 0.9 %collective-permute-done.14.refs_4_.rest_2_ = bf16[272,128]{1,0:T(8,128)(2,1)S(1)} collective-permute-done((bf16[272,128]{1,0:T(8,128)(2,1)S(1)}, bf16[272,128]{1,0:T(8,128)(2,1)S(1)}, u32[]{:S(2)}, u32[]{:S(2)}) %collective-permute-start.14) | collective-permute-done | bytes 69664 | tf_op jit(solution)/shard_map/ppermute | solution.py:343
  41.3 0.9 %collective-permute-done.13.refs_4_.rest_1_ = bf16[272,128]{1,0:T(8,128)(2,1)S(1)} collective-permute-done((bf16[272,128]{1,0:T(8,128)(2,1)S(1)}, bf16[272,128]{1,0:T(8,128)(2,1)S(1)}, u32[]{:S(2)}, u32[]{:S(2)}) %collective-permute-start.13) | collective-permute-done | bytes 69664 | tf_op jit(solution)/shard_map/ppermute | solution.py:343
  42.4 1.4 %shard_map.118 = (bf16[192,1024]{1,0:T(8,128)(2,1)}, bf16[192,1024]{1,0:T(8,128)(2,1)}, bf16[192,1024]{1,0:T(8,128)(2,1)}) custom-call(s32[1]{0:T(128)} %bitcast.place_ref, s32[1]{0:T(128)} %bitcast.1.side_ref, bf16[1024,2048]{1,0:T(8,128)(2,1)S(1)} %get-tuple-element.70.weight_ref, bf16[192,1024]{1,0:T(8,128)(2,1)S(1)} %collective-permute-done.12.other_ref, ...), custom_call_target="tpu_custom_call" | custom-call | flops 1000 | bytes 1000 | tf_op jit(solution)/shard_map/pallas_call | solution.py:55
  43.9 0.9 %shard_map.119 = (bf16[192,1024]{1,0:T(8,128)(2,1)}, bf16[192,1024]{1,0:T(8,128)(2,1)}, f32[1,1024]{1,0:T(1,128)}) custom-call(s32[1]{0:T(128)} %bitcast.place_ref, bf16[192,1024]{1,0:T(8,128)(2,1)S(1)} %get-tuple-element.71.key_ref.refs_0_, ...), custom_call_target="tpu_custom_call", output_to_operand_aliasing={{0}: (9, {}), {1}: (10, {})} | custom-call | flops 1000 | bytes 1000 | tf_op jit(solution)/shard_map/pallas_call | solution.py:55
  (29 shorter events, 5.0 us)
Async XLA Ops:
  0.6 6.5 %collective-permute-start = (bf16[192,1024]{1,0:T(8,128)(2,1)}, bf16[192,1024]{1,0:T(8,128)(2,1)S(1)}, u32[]{:S(2)}, u32[]{:S(2)}) collective-permute-start(bf16[192,1024]{1,0:T(8,128)(2,1)} %own_hbm.1), channel_id=1, source_target_pairs={{0,1},{1,0},{2,3},{3,2},{4,5},{5,4},{6,7},{7,6},{8,9},{9,8},{10,11... | collective-permute-start | bytes 1179656 | tf_op jit(solution)/shard_map/ppermute | solution.py:347
  1.1 22.1 %copy-start = (f32[1024]{0:T(1024)S(1)}, f32[1024]{0:T(1024)}, u32[]{:S(2)}) copy-start(f32[1024]{0:T(1024)} %param.10) | copy-start | bytes 12292
  2.7 7.8 %collective-permute-start.1 = (bf16[256,128]{1,0:T(8,128)(2,1)S(1)}, bf16[256,128]{1,0:T(8,128)(2,1)S(1)}, u32[]{:S(2)}, u32[]{:S(2)}) collective-permute-start(bf16[256,128]{1,0:T(8,128)(2,1)S(1)} %get-tuple-element.74), channel_id=1, source_target_pairs={{0,2},{2,0},{4,6},{6,4},{8,10},{10,8},{12,14},{14,12},{1,3},{3,1},... | collective-permute-start | bytes 196616 | tf_op jit(solution)/shard_map/ppermute | solution.py:343
  5.3 5.2 %collective-permute-start.2 = (bf16[256,128]{1,0:T(8,128)(2,1)S(1)}, bf16[256,128]{1,0:T(8,128)(2,1)S(1)}, u32[]{:S(2)}, u32[]{:S(2)}) collective-permute-start(bf16[256,128]{1,0:T(8,128)(2,1)S(1)} %get-tuple-element.75), channel_id=1, source_target_pairs={{0,4},{2,6},{4,0},{6,2},{8,12},{10,14},{12,8},{14,10},{1,5},{3,7},... | collective-permute-start | bytes 196616 | tf_op jit(solution)/shard_map/ppermute | solution.py:343
  6.8 5.2 %collective-permute-start.3 = (bf16[256,128]{1,0:T(8,128)(2,1)S(1)}, bf16[256,128]{1,0:T(8,128)(2,1)S(1)}, u32[]{:S(2)}, u32[]{:S(2)}) collective-permute-start(bf16[256,128]{1,0:T(8,128)(2,1)S(1)} %get-tuple-element.76), channel_id=1, source_target_pairs={{0,6},{2,4},{4,2},{6,0},{8,14},{10,12},{12,10},{14,8},{1,7},{3,5},... | collective-permute-start | bytes 196616 | tf_op jit(solution)/shard_map/ppermute | solution.py:343
  12.0 5.8 %collective-permute-start.4 = (bf16[256,128]{1,0:T(8,128)(2,1)S(1)}, bf16[256,128]{1,0:T(8,128)(2,1)S(1)}, u32[]{:S(2)}, u32[]{:S(2)}) collective-permute-start(bf16[256,128]{1,0:T(8,128)(2,1)S(1)} %shard_map.105), channel_id=1, source_target_pairs={{0,8},{2,10},{4,12},{6,14},{8,0},{10,2},{12,4},{14,6},{1,9},{3,11}... | collective-permute-start | bytes 196616 | tf_op jit(solution)/shard_map/ppermute | solution.py:343
  18.0 5.2 %collective-permute-start.9 = (bf16[256,128]{1,0:T(8,128)(2,1)S(1)}, bf16[256,128]{1,0:T(8,128)(2,1)S(1)}, u32[]{:S(2)}, u32[]{:S(2)}) collective-permute-start(bf16[256,128]{1,0:T(8,128)(2,1)S(1)} %get-tuple-element.92), channel_id=1, source_target_pairs={{0,6},{2,4},{4,2},{6,0},{8,14},{10,12},{12,10},{14,8},{1,7},{3,5},... | collective-permute-start | bytes 196616 | tf_op jit(solution)/shard_map/ppermute | solution.py:343
  19.0 5.7 %collective-permute-start.7 = (bf16[256,128]{1,0:T(8,128)(2,1)S(1)}, bf16[256,128]{1,0:T(8,128)(2,1)S(1)}, u32[]{:S(2)}, u32[]{:S(2)}) collective-permute-start(bf16[256,128]{1,0:T(8,128)(2,1)S(1)} %get-tuple-element.90), channel_id=1, source_target_pairs={{0,4},{2,6},{4,0},{6,2},{8,12},{10,14},{12,8},{14,10},{1,5},{3,7},... | collective-permute-start | bytes 196616 | tf_op jit(solution)/shard_map/ppermute | solution.py:343
  19.7 6.3 %collective-permute-start.5 = (bf16[256,128]{1,0:T(8,128)(2,1)S(1)}, bf16[256,128]{1,0:T(8,128)(2,1)S(1)}, u32[]{:S(2)}, u32[]{:S(2)}) collective-permute-start(bf16[256,128]{1,0:T(8,128)(2,1)S(1)} %get-tuple-element.88), channel_id=1, source_target_pairs={{0,2},{2,0},{4,6},{6,4},{8,10},{10,8},{12,14},{14,12},{1,3},{3,1},... | collective-permute-start | bytes 196616 | tf_op jit(solution)/shard_map/ppermute | solution.py:343
  23.7 7.2 %collective-permute-start.10 = (bf16[272,128]{1,0:T(8,128)(2,1)S(1)}, bf16[272,128]{1,0:T(8,128)(2,1)S(1)}, u32[]{:S(2)}, u32[]{:S(2)}) collective-permute-start(bf16[272,128]{1,0:T(8,128)(2,1)S(1)} %get-tuple-element.93), channel_id=1, source_target_pairs={{0,6},{2,4},{4,2},{6,0},{8,14},{10,12},{12,10},{14,8},{1,7},{3,5},... | collective-permute-start | bytes 208904 | tf_op jit(solution)/shard_map/ppermute | solution.py:343
  25.1 5.8 %collective-permute-start.8 = (bf16[272,128]{1,0:T(8,128)(2,1)S(1)}, bf16[272,128]{1,0:T(8,128)(2,1)S(1)}, u32[]{:S(2)}, u32[]{:S(2)}) collective-permute-start(bf16[272,128]{1,0:T(8,128)(2,1)S(1)} %get-tuple-element.91), channel_id=1, source_target_pairs={{0,4},{2,6},{4,0},{6,2},{8,12},{10,14},{12,8},{14,10},{1,5},{3,7},... | collective-permute-start | bytes 208904 | tf_op jit(solution)/shard_map/ppermute | solution.py:343
  26.5 4.5 %collective-permute-start.6 = (bf16[272,128]{1,0:T(8,128)(2,1)S(1)}, bf16[272,128]{1,0:T(8,128)(2,1)S(1)}, u32[]{:S(2)}, u32[]{:S(2)}) collective-permute-start(bf16[272,128]{1,0:T(8,128)(2,1)S(1)} %get-tuple-element.89), channel_id=1, source_target_pairs={{0,2},{2,0},{4,6},{6,4},{8,10},{10,8},{12,14},{14,12},{1,3},{3,1},... | collective-permute-start | bytes 208904 | tf_op jit(solution)/shard_map/ppermute | solution.py:343
  31.0 5.3 %collective-permute-start.11 = (bf16[272,128]{1,0:T(8,128)(2,1)S(1)}, bf16[272,128]{1,0:T(8,128)(2,1)S(1)}, u32[]{:S(2)}, u32[]{:S(2)}) collective-permute-start(bf16[272,128]{1,0:T(8,128)(2,1)S(1)} %get-tuple-element.107), channel_id=1, source_target_pairs={{0,8},{2,10},{4,12},{6,14},{8,0},{10,2},{12,4},{14,6},{1,9},{3,11}... | collective-permute-start | bytes 208904 | tf_op jit(solution)/shard_map/ppermute | solution.py:343
  36.3 6.2 %collective-permute-start.12 = (bf16[192,1024]{1,0:T(8,128)(2,1)S(1)}, bf16[192,1024]{1,0:T(8,128)(2,1)S(1)}, u32[]{:S(2)}, u32[]{:S(2)}) collective-permute-start(bf16[192,1024]{1,0:T(8,128)(2,1)S(1)} %get-tuple-element.113), channel_id=1, source_target_pairs={{0,1},{1,0},{2,3},{3,2},{4,5},{5,4},{6,7},{7,6},{8,9},{9,8},{10,11... | collective-permute-start | bytes 1179656 | tf_op jit(solution)/shard_map/ppermute | solution.py:347
  36.4 4.7 %collective-permute-start.14 = (bf16[272,128]{1,0:T(8,128)(2,1)S(1)}, bf16[272,128]{1,0:T(8,128)(2,1)S(1)}, u32[]{:S(2)}, u32[]{:S(2)}) collective-permute-start(bf16[272,128]{1,0:T(8,128)(2,1)S(1)} %get-tuple-element.124), channel_id=1, source_target_pairs={{0,4},{2,6},{4,0},{6,2},{8,12},{10,14},{12,8},{14,10},{1,5},{3,7},... | collective-permute-start | bytes 208904 | tf_op jit(solution)/shard_map/ppermute | solution.py:343
  37.9 4.3 %collective-permute-start.13 = (bf16[272,128]{1,0:T(8,128)(2,1)S(1)}, bf16[272,128]{1,0:T(8,128)(2,1)S(1)}, u32[]{:S(2)}, u32[]{:S(2)}) collective-permute-start(bf16[272,128]{1,0:T(8,128)(2,1)S(1)} %get-tuple-element.121), channel_id=1, source_target_pairs={{0,2},{2,0},{4,6},{6,4},{8,10},{10,8},{12,14},{14,12},{1,3},{3,1},... | collective-permute-start | bytes 208904 | tf_op jit(solution)/shard_map/ppermute | solution.py:343
  38.5 5.4 %collective-permute-start.15 = (bf16[272,128]{1,0:T(8,128)(2,1)S(1)}, bf16[272,128]{1,0:T(8,128)(2,1)S(1)}, u32[]{:S(2)}, u32[]{:S(2)}) collective-permute-start(bf16[272,128]{1,0:T(8,128)(2,1)S(1)} %get-tuple-element.129), channel_id=1, source_target_pairs={{0,6},{2,4},{4,2},{6,0},{8,14},{10,12},{12,10},{14,8},{1,7},{3,5},... | collective-permute-start | bytes 208904 | tf_op jit(solution)/shard_map/ppermute | solution.py:343

commit v7 on v6

--- a/solution.py
+++ b/solution.py
@@ -68,10 +68,6 @@
     for j, i, head in head_slices(place, per_quarter, quarters):
         state = dot(key_ref[:, head], value_ref[:, head], (0, 0))
         out_refs[j - quarters[0]][i * DH : (i + 1) * DH, :] = state.astype(low)
-
-
-def own_state_kernel(per_quarter, place_ref, key_ref, value_ref, *out_refs):
-    states(per_quarter, range(1), place_ref[0], key_ref, value_ref, out_refs)
 
 
 def state_kernel(per_quarter, place_ref, key_hbm, value_hbm, *rest):
@@ -246,7 +242,10 @@
     ref[base + 1 : base + 2, :] = (gain - upper.astype(wide)).astype(low)
 
 
-def back_kernel(side_ref, own_hbm, other_ref, weight_hbm, out_ref, weight_ref, own_ref, own_sem, sems):
+def back_kernel(
+    per_quarter, side_ref, own_hbm, other_ref, weight_hbm, place_ref, key_ref, value_ref,
+    out_ref, weight_ref, part_ref, own_ref, own_sem, sems
+):
     width = own_ref.shape[1]
     own = pl.ds(pl.multiple_of(side_ref[0] * width, DH), width)
     other = pl.ds(pl.multiple_of((1 - side_ref[0]) * width, DH), width)
@@ -259,6 +258,7 @@
     ]
     for copy in copies:
         copy.start()
+    states(per_quarter, range(1), place_ref[0], key_ref, value_ref, (part_ref,))
     own_copy.wait()
     for copy, rows in zip(copies, chunks):
         copy.wait()
@@ -417,12 +417,6 @@
         [SMEM, HBM, HBM],
         scratch=[two_sems],
     )(where, key_vectors, values)
-    (own_part,) = call(
-        functools.partial(own_state_kernel, per_quarter),
-        [shaped((rows, DH), low)],
-        [SMEM, VMEM, VMEM],
-    )(where, key_near, value_near)
-    parts = [own_part, *parts]
     squares = shaped((heads, tokens, tokens), low)
     local, query_near, scores = call(
         functools.partial(local_kernel, heads),
@@ -430,16 +424,17 @@
         [HBM, VMEM, VMEM],
         scratch=[one_sem],
     )(queries, key_near, value_near)
-    grad_normed, weight_near = call(
-        back_kernel,
-        [whole, shaped(out_weight.shape, low)],
-        [SMEM, HBM, VMEM, HBM],
+    grad_normed, weight_near, own_part = call(
+        functools.partial(back_kernel, per_quarter),
+        [whole, shaped(out_weight.shape, low), shaped((rows, DH), low)],
+        [SMEM, HBM, VMEM, HBM, SMEM, VMEM, VMEM],
         scratch=[
             pltpu.VMEM((tokens, half), low),
             one_sem,
             pltpu.SemaphoreType.DMA((width // CHUNK,)),
         ],
-    )(side, grad_output, other_grad, out_weight)
+    )(side, grad_output, other_grad, out_weight, where, key_near, value_near)
+    parts = [own_part, *parts]
     prefix, grad_normed, local = scan(where, parts, False, rows, 0, grad_normed, local)
 
     part_low = shaped((tokens, rows), low)

time: 45 us -> 45 us (level)
    pallas_call x19 -> x18, Pallas kernels: 14.9 us -> 14.6 us  [pinned(): return kernel(*fixed)]
  transfers between devices with their start and end apart: 16 -> 16, of which waited for: 7 -> 7; matrix products, arithmetic and copies ran while one was open for 0% -> 0% of each run, Pallas kernels for 31% -> 30%
where the time goes in v7:
time: 45 us; the launch traced here: 44.8 us
  starting transfers between devices  20.5 us (46%)
  Pallas kernels  14.6 us (32%)
  waiting for transfers between devices  8.88 us (20%)
  between operations  0.8 us (2%)
    ppermute x14, starting transfers between devices, swap(): return lax.ppermute(array, 'seq', [(i, i ^ flip) for i in range(count)])  20 us
    pallas_call x18, Pallas kernels, pinned(): return kernel(*fixed)  14.6 us
    ppermute x14, waiting for transfers between devices, swap(): return lax.ppermute(array, 'seq', [(i, i ^ flip) for i in range(count)])  8.87 us
  transfers between devices with their start and end apart: 16, of which 7 were waited for; matrix products, arithmetic and copies ran while one was open for 0% of the time, Pallas kernels for 30%

profile of v7, /device:TPU:0, one launch (start us, length us, event | category | flops | bytes accessed | tf_op | source)
XLA Modules:
  0.0 44.8 jit_solution(6572436951717198110)
XLA Ops:
  1.2 1.5 %shard_map.101 = (bf16[256,128]{1,0:T(8,128)(2,1)S(1)}, bf16[256,128]{1,0:T(8,128)(2,1)S(1)}, bf16[256,128]{1,0:T(8,128)(2,1)S(1)}, bf16[192,1024]{1,0:T(8,128)(2,1)S(1)}, bf16[192,1024]{1,0:T(8,128)(2,1)S(1)}) custom-call(s32[1]{0:T(128)} %bitcast.place_ref, bf16[192,1024]{1,0:T(8,128)(2,1)} %key_hbm.1, bf16[192,1024]{1,0:T(8,128)(2,1)} %value_hbm.1), custom_call_target="tpu_custom_call" | custom-call | flops 1000 | bytes 1000 | tf_op jit(solution)/shard_map/pallas_call | solution.py:55
  2.7 2.6 %collective-permute-start.1 = (bf16[256,128]{1,0:T(8,128)(2,1)S(1)}, bf16[256,128]{1,0:T(8,128)(2,1)S(1)}, u32[]{:S(2)}, u32[]{:S(2)}) collective-permute-start(bf16[256,128]{1,0:T(8,128)(2,1)S(1)} %get-tuple-element.76), channel_id=1, source_target_pairs={{0,2},{2,0},{4,6},{6,4},{8,10},{10,8},{12,14},{14,12},{1,3},{3,1},... | collective-permute-start | bytes 196616 | tf_op jit(solution)/shard_map/ppermute | solution.py:343
  5.3 1.6 %collective-permute-start.2 = (bf16[256,128]{1,0:T(8,128)(2,1)S(1)}, bf16[256,128]{1,0:T(8,128)(2,1)S(1)}, u32[]{:S(2)}, u32[]{:S(2)}) collective-permute-start(bf16[256,128]{1,0:T(8,128)(2,1)S(1)} %get-tuple-element.77), channel_id=1, source_target_pairs={{0,4},{2,6},{4,0},{6,2},{8,12},{10,14},{12,8},{14,10},{1,5},{3,7},... | collective-permute-start | bytes 196616 | tf_op jit(solution)/shard_map/ppermute | solution.py:343
  6.8 3.4 %shard_map.102 = (f32[192,1024]{1,0:T(8,128)S(1)}, bf16[1024,2048]{1,0:T(8,128)(2,1)S(1)}, bf16[256,128]{1,0:T(8,128)(2,1)S(1)}) custom-call(s32[1]{0:T(128)} %bitcast.1.side_ref, bf16[192,1024]{1,0:T(8,128)(2,1)} %own_hbm.1, bf16[192,1024]{1,0:T(8,128)(2,1)S(1)} %collective-permute-done.other_ref, bf16[1024,2048]{1,0:T(8,128)(2,1)} %weight_hbm.1, ...), custom_call_target="tpu_custom_call" | custom-call | flops 1000 | bytes 1000 | tf_op jit(solution)/shard_map/pallas_call | solution.py:55
  10.2 1.8 %collective-permute-done.3.b3 = bf16[256,128]{1,0:T(8,128)(2,1)S(1)} collective-permute-done((bf16[256,128]{1,0:T(8,128)(2,1)S(1)}, bf16[256,128]{1,0:T(8,128)(2,1)S(1)}, u32[]{:S(2)}, u32[]{:S(2)}) %collective-permute-start.3) | collective-permute-done | bytes 65568 | tf_op jit(solution)/shard_map/ppermute | solution.py:343
  12.0 2.7 %collective-permute-start.4 = (bf16[256,128]{1,0:T(8,128)(2,1)S(1)}, bf16[256,128]{1,0:T(8,128)(2,1)S(1)}, u32[]{:S(2)}, u32[]{:S(2)}) collective-permute-start(bf16[256,128]{1,0:T(8,128)(2,1)S(1)} %shard_map.104), channel_id=1, source_target_pairs={{0,8},{2,10},{4,12},{6,14},{8,0},{10,2},{12,4},{14,6},{1,9},{3,11}... | collective-permute-start | bytes 196616 | tf_op jit(solution)/shard_map/ppermute | solution.py:343
  14.7 1.8 %shard_map.103 = (f32[192,1024]{1,0:T(8,128)S(1)}, bf16[192,1024]{1,0:T(8,128)(2,1)S(1)}, bf16[8,192,192]{2,1,0:T(8,128)(2,1)S(1)}) custom-call(bf16[192,1024]{1,0:T(8,128)(2,1)} %query_hbm.1, bf16[192,1024]{1,0:T(8,128)(2,1)S(1)} %get-tuple-element.71.key_ref.refs_0_, bf16[192,1024]{1,0:T(8,128)(2,1)S(1)} %get-tuple-element.72.value_ref.refs_1_), custom_call_target="tpu_custom_call" | custom-call | flops 1000 | bytes 1000 | tf_op jit(solution)/shard_map/pallas_call | solution.py:55
  16.5 1.3 %collective-permute-done.4.got_ref = bf16[256,128]{1,0:T(8,128)(2,1)S(1)} collective-permute-done((bf16[256,128]{1,0:T(8,128)(2,1)S(1)}, bf16[256,128]{1,0:T(8,128)(2,1)S(1)}, u32[]{:S(2)}, u32[]{:S(2)}) %collective-permute-start.4) | collective-permute-done | bytes 65568 | tf_op jit(solution)/shard_map/ppermute | solution.py:343
  18.0 0.8 %collective-permute-start.9 = (bf16[256,128]{1,0:T(8,128)(2,1)S(1)}, bf16[256,128]{1,0:T(8,128)(2,1)S(1)}, u32[]{:S(2)}, u32[]{:S(2)}) collective-permute-start(bf16[256,128]{1,0:T(8,128)(2,1)S(1)} %get-tuple-element.94), channel_id=1, source_target_pairs={{0,6},{2,4},{4,2},{6,0},{8,14},{10,12},{12,10},{14,8},{1,7},{3,5},... | collective-permute-start | bytes 196616 | tf_op jit(solution)/shard_map/ppermute | solution.py:343
  19.5 2.1 %collective-permute-start.5 = (bf16[256,128]{1,0:T(8,128)(2,1)S(1)}, bf16[256,128]{1,0:T(8,128)(2,1)S(1)}, u32[]{:S(2)}, u32[]{:S(2)}) collective-permute-start(bf16[256,128]{1,0:T(8,128)(2,1)S(1)} %get-tuple-element.90), channel_id=1, source_target_pairs={{0,2},{2,0},{4,6},{6,4},{8,10},{10,8},{12,14},{14,12},{1,3},{3,1},... | collective-permute-start | bytes 196616 | tf_op jit(solution)/shard_map/ppermute | solution.py:343
  21.5 1.7 %collective-permute-done.9.prefix_ref.rest_11_ = bf16[256,128]{1,0:T(8,128)(2,1)S(1)} collective-permute-done((bf16[256,128]{1,0:T(8,128)(2,1)S(1)}, bf16[256,128]{1,0:T(8,128)(2,1)S(1)}, u32[]{:S(2)}, u32[]{:S(2)}) %collective-permute-start.9) | collective-permute-done | bytes 65568 | tf_op jit(solution)/shard_map/ppermute | solution.py:343
  23.7 0.8 %collective-permute-start.10 = (bf16[272,128]{1,0:T(8,128)(2,1)S(1)}, bf16[272,128]{1,0:T(8,128)(2,1)S(1)}, u32[]{:S(2)}, u32[]{:S(2)}) collective-permute-start(bf16[272,128]{1,0:T(8,128)(2,1)S(1)} %get-tuple-element.95), channel_id=1, source_target_pairs={{0,6},{2,4},{4,2},{6,0},{8,14},{10,12},{12,10},{14,8},{1,7},{3,5},... | collective-permute-start | bytes 208904 | tf_op jit(solution)/shard_map/ppermute | solution.py:343
  25.0 0.7 %collective-permute-start.8 = (bf16[272,128]{1,0:T(8,128)(2,1)S(1)}, bf16[272,128]{1,0:T(8,128)(2,1)S(1)}, u32[]{:S(2)}, u32[]{:S(2)}) collective-permute-start(bf16[272,128]{1,0:T(8,128)(2,1)S(1)} %get-tuple-element.93), channel_id=1, source_target_pairs={{0,4},{2,6},{4,0},{6,2},{8,12},{10,14},{12,8},{14,10},{1,5},{3,7},... | collective-permute-start | bytes 208904 | tf_op jit(solution)/shard_map/ppermute | solution.py:343
  26.2 2.1 %collective-permute-start.6 = (bf16[272,128]{1,0:T(8,128)(2,1)S(1)}, bf16[272,128]{1,0:T(8,128)(2,1)S(1)}, u32[]{:S(2)}, u32[]{:S(2)}) collective-permute-start(bf16[272,128]{1,0:T(8,128)(2,1)S(1)} %get-tuple-element.91), channel_id=1, source_target_pairs={{0,2},{2,0},{4,6},{6,4},{8,10},{10,8},{12,14},{14,12},{1,3},{3,1},... | collective-permute-start | bytes 208904 | tf_op jit(solution)/shard_map/ppermute | solution.py:343
  28.8 2.1 %shard_map.110 = (bf16[192,1024]{1,0:T(8,128)(2,1)}, bf16[192,1024]{1,0:T(8,128)(2,1)S(1)}, bf16[8,192,192]{2,1,0:T(8,128)(2,1)S(1)}) custom-call(s32[1]{0:T(128)} %bitcast.place_ref, s32[1]{0:T(128)} %bitcast.1.side_ref, bf16[192,1024]{1,0:T(8,128)(2,1)S(1)} %get-tuple-element.71.key_ref.refs_0_, bf16[192,1024]{1,0:T(8,128)(2,1)S(1)} %get-tuple-element.72.value_ref.refs_1_, ...), custom_call_target="tpu_custom_call" | custom-call | flops 1000 | bytes 1000 | tf_op jit(solution)/shard_map/pallas_call | solution.py:55
  31.0 2.3 %collective-permute-start.11 = (bf16[272,128]{1,0:T(8,128)(2,1)S(1)}, bf16[272,128]{1,0:T(8,128)(2,1)S(1)}, u32[]{:S(2)}, u32[]{:S(2)}) collective-permute-start(bf16[272,128]{1,0:T(8,128)(2,1)S(1)} %get-tuple-element.109), channel_id=1, source_target_pairs={{0,8},{2,10},{4,12},{6,14},{8,0},{10,2},{12,4},{14,6},{1,9},{3,11}... | collective-permute-start | bytes 208904 | tf_op jit(solution)/shard_map/ppermute | solution.py:343
  33.3 0.7 %shard_map.112 = (f32[192,1024]{1,0:T(8,128)S(1)}, f32[192,1024]{1,0:T(8,128)S(1)}) custom-call(s32[1]{0:T(128)} %bitcast.place_ref, bf16[192,1024]{1,0:T(8,128)(2,1)S(1)} %get-tuple-element.74.query_ref, bf16[8,192,192]{2,1,0:T(8,128)(2,1)S(1)} %get-tuple-element.110.score_ref, bf16[8,192,192]{2,1,0:T(8,128)(2,1)S(1)} %get-tuple-element.111.grad_score_ref, ...), custom_call_target="tpu_custom_call" | custom-call | flops 1000 | bytes 1000 | tf_op jit(solution)/shard_map/pallas_call | solution.py:55
  34.1 2.2 %collective-permute-done.11.got_ref = bf16[272,128]{1,0:T(8,128)(2,1)S(1)} collective-permute-done((bf16[272,128]{1,0:T(8,128)(2,1)S(1)}, bf16[272,128]{1,0:T(8,128)(2,1)S(1)}, u32[]{:S(2)}, u32[]{:S(2)}) %collective-permute-start.11) | collective-permute-done | bytes 69664 | tf_op jit(solution)/shard_map/ppermute | solution.py:343
  36.4 1.4 %collective-permute-start.14 = (bf16[272,128]{1,0:T(8,128)(2,1)S(1)}, bf16[272,128]{1,0:T(8,128)(2,1)S(1)}, u32[]{:S(2)}, u32[]{:S(2)}) collective-permute-start(bf16[272,128]{1,0:T(8,128)(2,1)S(1)} %get-tuple-element.126), channel_id=1, source_target_pairs={{0,4},{2,6},{4,0},{6,2},{8,12},{10,14},{12,8},{14,10},{1,5},{3,7},... | collective-permute-start | bytes 208904 | tf_op jit(solution)/shard_map/ppermute | solution.py:343
  38.5 1.5 %collective-permute-start.15 = (bf16[272,128]{1,0:T(8,128)(2,1)S(1)}, bf16[272,128]{1,0:T(8,128)(2,1)S(1)}, u32[]{:S(2)}, u32[]{:S(2)}) collective-permute-start(bf16[272,128]{1,0:T(8,128)(2,1)S(1)} %get-tuple-element.131), channel_id=1, source_target_pairs={{0,6},{2,4},{4,2},{6,0},{8,14},{10,12},{12,10},{14,8},{1,7},{3,5},... | collective-permute-start | bytes 208904 | tf_op jit(solution)/shard_map/ppermute | solution.py:343
  40.2 0.9 %collective-permute-done.14.refs_4_.rest_2_ = bf16[272,128]{1,0:T(8,128)(2,1)S(1)} collective-permute-done((bf16[272,128]{1,0:T(8,128)(2,1)S(1)}, bf16[272,128]{1,0:T(8,128)(2,1)S(1)}, u32[]{:S(2)}, u32[]{:S(2)}) %collective-permute-start.14) | collective-permute-done | bytes 69664 | tf_op jit(solution)/shard_map/ppermute | solution.py:343
  41.3 0.9 %collective-permute-done.13.refs_4_.rest_1_ = bf16[272,128]{1,0:T(8,128)(2,1)S(1)} collective-permute-done((bf16[272,128]{1,0:T(8,128)(2,1)S(1)}, bf16[272,128]{1,0:T(8,128)(2,1)S(1)}, u32[]{:S(2)}, u32[]{:S(2)}) %collective-permute-start.13) | collective-permute-done | bytes 69664 | tf_op jit(solution)/shard_map/ppermute | solution.py:343
  42.4 1.4 %shard_map.117 = (bf16[192,1024]{1,0:T(8,128)(2,1)}, bf16[192,1024]{1,0:T(8,128)(2,1)}, bf16[192,1024]{1,0:T(8,128)(2,1)}) custom-call(s32[1]{0:T(128)} %bitcast.place_ref, s32[1]{0:T(128)} %bitcast.1.side_ref, bf16[1024,2048]{1,0:T(8,128)(2,1)S(1)} %get-tuple-element.73.weight_ref, bf16[192,1024]{1,0:T(8,128)(2,1)S(1)} %collective-permute-done.12.other_ref, ...), custom_call_target="tpu_custom_call" | custom-call | flops 1000 | bytes 1000 | tf_op jit(solution)/shard_map/pallas_call | solution.py:55
  43.9 0.9 %shard_map.118 = (bf16[192,1024]{1,0:T(8,128)(2,1)}, bf16[192,1024]{1,0:T(8,128)(2,1)}, f32[1,1024]{1,0:T(1,128)}) custom-call(s32[1]{0:T(128)} %bitcast.place_ref, bf16[192,1024]{1,0:T(8,128)(2,1)S(1)} %get-tuple-element.71.key_ref.refs_0_, ...), custom_call_target="tpu_custom_call", output_to_operand_aliasing={{0}: (9, {}), {1}: (10, {})} | custom-call | flops 1000 | bytes 1000 | tf_op jit(solution)/shard_map/pallas_call | solution.py:55
  (28 shorter events, 4.8 us)
Async XLA Ops:
  0.6 6.2 %collective-permute-start = (bf16[192,1024]{1,0:T(8,128)(2,1)}, bf16[192,1024]{1,0:T(8,128)(2,1)S(1)}, u32[]{:S(2)}, u32[]{:S(2)}) collective-permute-start(bf16[192,1024]{1,0:T(8,128)(2,1)} %own_hbm.1), channel_id=1, source_target_pairs={{0,1},{1,0},{2,3},{3,2},{4,5},{5,4},{6,7},{7,6},{8,9},{9,8},{10,11... | collective-permute-start | bytes 1179656 | tf_op jit(solution)/shard_map/ppermute | solution.py:347
  1.1 22.1 %copy-start = (f32[1024]{0:T(1024)S(1)}, f32[1024]{0:T(1024)}, u32[]{:S(2)}) copy-start(f32[1024]{0:T(1024)} %param.10) | copy-start | bytes 12292
  2.7 7.6 %collective-permute-start.1 = (bf16[256,128]{1,0:T(8,128)(2,1)S(1)}, bf16[256,128]{1,0:T(8,128)(2,1)S(1)}, u32[]{:S(2)}, u32[]{:S(2)}) collective-permute-start(bf16[256,128]{1,0:T(8,128)(2,1)S(1)} %get-tuple-element.76), channel_id=1, source_target_pairs={{0,2},{2,0},{4,6},{6,4},{8,10},{10,8},{12,14},{14,12},{1,3},{3,1},... | collective-permute-start | bytes 196616 | tf_op jit(solution)/shard_map/ppermute | solution.py:343
  5.3 5.0 %collective-permute-start.2 = (bf16[256,128]{1,0:T(8,128)(2,1)S(1)}, bf16[256,128]{1,0:T(8,128)(2,1)S(1)}, u32[]{:S(2)}, u32[]{:S(2)}) collective-permute-start(bf16[256,128]{1,0:T(8,128)(2,1)S(1)} %get-tuple-element.77), channel_id=1, source_target_pairs={{0,4},{2,6},{4,0},{6,2},{8,12},{10,14},{12,8},{14,10},{1,5},{3,7},... | collective-permute-start | bytes 196616 | tf_op jit(solution)/shard_map/ppermute | solution.py:343
  6.8 5.2 %collective-permute-start.3 = (bf16[256,128]{1,0:T(8,128)(2,1)S(1)}, bf16[256,128]{1,0:T(8,128)(2,1)S(1)}, u32[]{:S(2)}, u32[]{:S(2)}) collective-permute-start(bf16[256,128]{1,0:T(8,128)(2,1)S(1)} %get-tuple-element.78), channel_id=1, source_target_pairs={{0,6},{2,4},{4,2},{6,0},{8,14},{10,12},{12,10},{14,8},{1,7},{3,5},... | collective-permute-start | bytes 196616 | tf_op jit(solution)/shard_map/ppermute | solution.py:343
  12.0 5.8 %collective-permute-start.4 = (bf16[256,128]{1,0:T(8,128)(2,1)S(1)}, bf16[256,128]{1,0:T(8,128)(2,1)S(1)}, u32[]{:S(2)}, u32[]{:S(2)}) collective-permute-start(bf16[256,128]{1,0:T(8,128)(2,1)S(1)} %shard_map.104), channel_id=1, source_target_pairs={{0,8},{2,10},{4,12},{6,14},{8,0},{10,2},{12,4},{14,6},{1,9},{3,11}... | collective-permute-start | bytes 196616 | tf_op jit(solution)/shard_map/ppermute | solution.py:343
  18.0 5.2 %collective-permute-start.9 = (bf16[256,128]{1,0:T(8,128)(2,1)S(1)}, bf16[256,128]{1,0:T(8,128)(2,1)S(1)}, u32[]{:S(2)}, u32[]{:S(2)}) collective-permute-start(bf16[256,128]{1,0:T(8,128)(2,1)S(1)} %get-tuple-element.94), channel_id=1, source_target_pairs={{0,6},{2,4},{4,2},{6,0},{8,14},{10,12},{12,10},{14,8},{1,7},{3,5},... | collective-permute-start | bytes 196616 | tf_op jit(solution)/shard_map/ppermute | solution.py:343
  18.8 5.7 %collective-permute-start.7 = (bf16[256,128]{1,0:T(8,128)(2,1)S(1)}, bf16[256,128]{1,0:T(8,128)(2,1)S(1)}, u32[]{:S(2)}, u32[]{:S(2)}) collective-permute-start(bf16[256,128]{1,0:T(8,128)(2,1)S(1)} %get-tuple-element.92), channel_id=1, source_target_pairs={{0,4},{2,6},{4,0},{6,2},{8,12},{10,14},{12,8},{14,10},{1,5},{3,7},... | collective-permute-start | bytes 196616 | tf_op jit(solution)/shard_map/ppermute | solution.py:343
  19.5 6.3 %collective-permute-start.5 = (bf16[256,128]{1,0:T(8,128)(2,1)S(1)}, bf16[256,128]{1,0:T(8,128)(2,1)S(1)}, u32[]{:S(2)}, u32[]{:S(2)}) collective-permute-start(bf16[256,128]{1,0:T(8,128)(2,1)S(1)} %get-tuple-element.90), channel_id=1, source_target_pairs={{0,2},{2,0},{4,6},{6,4},{8,10},{10,8},{12,14},{14,12},{1,3},{3,1},... | collective-permute-start | bytes 196616 | tf_op jit(solution)/shard_map/ppermute | solution.py:343
  23.7 7.2 %collective-permute-start.10 = (bf16[272,128]{1,0:T(8,128)(2,1)S(1)}, bf16[272,128]{1,0:T(8,128)(2,1)S(1)}, u32[]{:S(2)}, u32[]{:S(2)}) collective-permute-start(bf16[272,128]{1,0:T(8,128)(2,1)S(1)} %get-tuple-element.95), channel_id=1, source_target_pairs={{0,6},{2,4},{4,2},{6,0},{8,14},{10,12},{12,10},{14,8},{1,7},{3,5},... | collective-permute-start | bytes 208904 | tf_op jit(solution)/shard_map/ppermute | solution.py:343
  25.0 5.9 %collective-permute-start.8 = (bf16[272,128]{1,0:T(8,128)(2,1)S(1)}, bf16[272,128]{1,0:T(8,128)(2,1)S(1)}, u32[]{:S(2)}, u32[]{:S(2)}) collective-permute-start(bf16[272,128]{1,0:T(8,128)(2,1)S(1)} %get-tuple-element.93), channel_id=1, source_target_pairs={{0,4},{2,6},{4,0},{6,2},{8,12},{10,14},{12,8},{14,10},{1,5},{3,7},... | collective-permute-start | bytes 208904 | tf_op jit(solution)/shard_map/ppermute | solution.py:343
  26.2 4.7 %collective-permute-start.6 = (bf16[272,128]{1,0:T(8,128)(2,1)S(1)}, bf16[272,128]{1,0:T(8,128)(2,1)S(1)}, u32[]{:S(2)}, u32[]{:S(2)}) collective-permute-start(bf16[272,128]{1,0:T(8,128)(2,1)S(1)} %get-tuple-element.91), channel_id=1, source_target_pairs={{0,2},{2,0},{4,6},{6,4},{8,10},{10,8},{12,14},{14,12},{1,3},{3,1},... | collective-permute-start | bytes 208904 | tf_op jit(solution)/shard_map/ppermute | solution.py:343
  31.0 5.3 %collective-permute-start.11 = (bf16[272,128]{1,0:T(8,128)(2,1)S(1)}, bf16[272,128]{1,0:T(8,128)(2,1)S(1)}, u32[]{:S(2)}, u32[]{:S(2)}) collective-permute-start(bf16[272,128]{1,0:T(8,128)(2,1)S(1)} %get-tuple-element.109), channel_id=1, source_target_pairs={{0,8},{2,10},{4,12},{6,14},{8,0},{10,2},{12,4},{14,6},{1,9},{3,11}... | collective-permute-start | bytes 208904 | tf_op jit(solution)/shard_map/ppermute | solution.py:343
  36.3 6.1 %collective-permute-start.12 = (bf16[192,1024]{1,0:T(8,128)(2,1)S(1)}, bf16[192,1024]{1,0:T(8,128)(2,1)S(1)}, u32[]{:S(2)}, u32[]{:S(2)}) collective-permute-start(bf16[192,1024]{1,0:T(8,128)(2,1)S(1)} %get-tuple-element.115), channel_id=1, source_target_pairs={{0,1},{1,0},{2,3},{3,2},{4,5},{5,4},{6,7},{7,6},{8,9},{9,8},{10,11... | collective-permute-start | bytes 1179656 | tf_op jit(solution)/shard_map/ppermute | solution.py:347
  36.4 4.7 %collective-permute-start.14 = (bf16[272,128]{1,0:T(8,128)(2,1)S(1)}, bf16[272,128]{1,0:T(8,128)(2,1)S(1)}, u32[]{:S(2)}, u32[]{:S(2)}) collective-permute-start(bf16[272,128]{1,0:T(8,128)(2,1)S(1)} %get-tuple-element.126), channel_id=1, source_target_pairs={{0,4},{2,6},{4,0},{6,2},{8,12},{10,14},{12,8},{14,10},{1,5},{3,7},... | collective-permute-start | bytes 208904 | tf_op jit(solution)/shard_map/ppermute | solution.py:343
  37.9 4.3 %collective-permute-start.13 = (bf16[272,128]{1,0:T(8,128)(2,1)S(1)}, bf16[272,128]{1,0:T(8,128)(2,1)S(1)}, u32[]{:S(2)}, u32[]{:S(2)}) collective-permute-start(bf16[272,128]{1,0:T(8,128)(2,1)S(1)} %get-tuple-element.123), channel_id=1, source_target_pairs={{0,2},{2,0},{4,6},{6,4},{8,10},{10,8},{12,14},{14,12},{1,3},{3,1},... | collective-permute-start | bytes 208904 | tf_op jit(solution)/shard_map/ppermute | solution.py:343
  38.5 5.4 %collective-permute-start.15 = (bf16[272,128]{1,0:T(8,128)(2,1)S(1)}, bf16[272,128]{1,0:T(8,128)(2,1)S(1)}, u32[]{:S(2)}, u32[]{:S(2)}) collective-permute-start(bf16[272,128]{1,0:T(8,128)(2,1)S(1)} %get-tuple-element.131), channel_id=1, source_target_pairs={{0,6},{2,4},{4,2},{6,0},{8,14},{10,12},{12,10},{14,8},{1,7},{3,5},... | collective-permute-start | bytes 208904 | tf_op jit(solution)/shard_map/ppermute | solution.py:343

commit v8 on v5

--- a/solution.py
+++ b/solution.py
@@ -12,7 +12,7 @@
 EXTRA = 16
 CHUNK = 512
 COST = 1000
-FINISH = (0, 1, 2, 3)
+FINISH = ((0, 1), (2, 3))
 EPSILON = 1e-05
 wide = jnp.float32
 low = jnp.bfloat16
@@ -207,20 +207,24 @@
         copy.wait()
 
 
-def store_kernel(per_quarter, quarter, place_ref, key_ref, value_ref, local_key_ref, local_value_ref, *rest):
-    suffix, rest = rest[:QUAD], rest[QUAD + 2 :]
+def store_kernel(per_quarter, quarters, place_ref, key_ref, value_ref, local_key_ref, local_value_ref, *rest):
+    suffix, before, rest = rest[:QUAD], rest[QUAD : QUAD + 2], rest[QUAD + 4 :]
     grad_key_hbm, grad_value_hbm, gain_hbm, key_part, value_part, gain_ref, sems = rest
     place = place_ref[0]
+    outs = (grad_key_hbm, grad_value_hbm)
+    copies = stores(per_quarter, place, quarters[:1], before, outs, sems.at[3:5])
+    for copy in copies:
+        copy.start()
     for j, i, head in head_slices(place, per_quarter):
         gain_ref[:, head] = pair_sum(suffix[j], per_quarter, i)
     gain_copy = pltpu.make_async_copy(gain_ref, gain_hbm, sems.at[2])
     gain_copy.start()
     finish_part(
-        per_quarter, quarter, place, key_ref, value_ref, local_key_ref, local_value_ref, suffix[quarter],
+        per_quarter, quarters[1], place, key_ref, value_ref, local_key_ref, local_value_ref, suffix[quarters[1]],
         key_part, value_part,
     )
-    copies = stores(per_quarter, place, (quarter,), (key_part, value_part), (grad_key_hbm, grad_value_hbm), sems)
-    for copy in copies:
+    copies += stores(per_quarter, place, quarters[1:], (key_part, value_part), outs, sems)
+    for copy in copies[2:]:
         copy.start()
     for copy in (gain_copy, *copies):
         copy.wait()
@@ -306,19 +310,21 @@
     earlier = refs.pop(0) if gains else None
     blocks = (b0, b1, b2, b3)
     rows = got_ref.shape[0] - (EXTRA if gains else 0)
-    quarter = place_ref[0] & (QUAD - 1)
     outside = jnp.where(is_beyond(place_ref, step, backward), got_ref[:rows, :].astype(wide), 0.0)
     if past:
         outside = outside + outside_ref[...]
     states = [block[:rows, :].astype(wide) for block in blocks]
+    pairs = (states[0] + states[1], states[2] + states[3])
+    near = ((place_ref[0] & 1) != 0) != backward
+    far = ((place_ref[0] & 2) != 0) != backward
+    bases = (
+        outside + jnp.where(far, pairs[1], 0.0),
+        outside + jnp.where(far, 0.0, pairs[0]),
+    )
     for j in range(QUAD):
-        result = outside
-        for i in range(QUAD):
-            if i == j:
-                continue
-            source, target = quarter ^ i, quarter ^ j
-            counts = (source > target) if backward else (source < target)
-            result = result + jnp.where(counts, states[i], 0.0)
+        neighbour = states[j ^ 1]
+        own = jnp.where(near, 0.0, neighbour) if j & 1 else jnp.where(near, neighbour, 0.0)
+        result = bases[j >> 1] + own
         refs[j][:rows, :] = result.astype(low)
         if gains:
             refs[j][rows:, :] = jnp.zeros((EXTRA, DH), low)
@@ -453,14 +459,15 @@
     suffix, local_pair = end(where, blocks, True, rows, per_quarter, (local_pair, sent))
     local_pair, sent = local_pair
     other_part = trade(sent)
-    *early, last = FINISH
-    finished = []
-    for j in early:
-        finished += call(
+    def finish(j):
+        return call(
             functools.partial(finish_kernel, per_quarter, j),
             [part_low, part_low],
             [SMEM] + [VMEM] * 5,
         )(where, key_near, value_near, *local_pair, suffix[j])
+
+    early, late = FINISH
+    finished = [part for j in early for part in finish(j)]
     mixed, grad_keys, grad_values = call(
         functools.partial(mixed_kernel, per_quarter, early),
         [whole_low, whole_low, whole_low],
@@ -468,15 +475,18 @@
         out_specs=[HBM] * 3,
         scratch=[result_whole, pltpu.SemaphoreType.DMA((len(finished) + 1,))],
     )(where, side, weight_near, other_part, *normed, *finished)
+    suffix[late[0]], mixed, grad_keys, grad_values = lax.optimization_barrier(
+        (suffix[late[0]], mixed, grad_keys, grad_values)
+    )
     part = pltpu.VMEM((tokens, rows), low)
     grad_keys, grad_values, gain = call(
-        functools.partial(store_kernel, per_quarter, last),
+        functools.partial(store_kernel, per_quarter, late),
         [whole_low, whole_low, shaped((1, width), wide)],
-        [SMEM] + [VMEM] * (4 + QUAD) + [HBM, HBM],
+        [SMEM] + [VMEM] * (6 + QUAD) + [HBM, HBM],
         out_specs=[HBM, HBM, HBM],
-        scratch=[part, part, pltpu.VMEM((1, width), wide), pltpu.SemaphoreType.DMA((3,))],
-        aliases={5 + QUAD: 0, 6 + QUAD: 1},
-    )(where, key_near, value_near, *local_pair, *suffix, grad_keys, grad_values)
+        scratch=[part, part, pltpu.VMEM((1, width), wide), pltpu.SemaphoreType.DMA((5,))],
+        aliases={7 + QUAD: 0, 8 + QUAD: 1},
+    )(where, key_near, value_near, *local_pair, *suffix, *finish(late[0]), grad_keys, grad_values)
     return mixed, grad_queries, grad_keys, grad_values, gain.reshape(width)
 
 

time: 45.1 us -> 45.2 us (level)
  no operation moved by 1% of the time
where the time goes in v8:
time: 45.2 us; the launch traced here: 45 us
  starting transfers between devices  20.5 us (45%)
  Pallas kernels  14.7 us (33%)
  waiting for transfers between devices  8.97 us (20%)
  between operations  0.81 us (2%)
    ppermute x14, starting transfers between devices, swap(): return lax.ppermute(array, 'seq', [(i, i ^ flip) for i in range(count)])  20 us
    pallas_call x18, Pallas kernels, pinned(): return kernel(*fixed)  14.7 us
    ppermute x14, waiting for transfers between devices, swap(): return lax.ppermute(array, 'seq', [(i, i ^ flip) for i in range(count)])  8.96 us
  transfers between devices with their start and end apart: 16, of which 7 were waited for; matrix products, arithmetic and copies ran while one was open for 0% of the time, Pallas kernels for 30%

profile of v8, /device:TPU:0, one launch (start us, length us, event | category | flops | bytes accessed | tf_op | source)
XLA Modules:
  0.0 45.0 jit_solution(4145643160686266461)
XLA Ops:
  1.2 1.6 %shard_map.101 = (bf16[256,128]{1,0:T(8,128)(2,1)S(1)}, bf16[256,128]{1,0:T(8,128)(2,1)S(1)}, bf16[256,128]{1,0:T(8,128)(2,1)S(1)}, bf16[256,128]{1,0:T(8,128)(2...) custom-call(s32[1]{0:T(128)} %bitcast.place_ref, bf16[192,1024]{1,0:T(8,128)(2,1)} %key_hbm.1, ...), custom_call_target="tpu_custom_call" | custom-call | flops 1000 | bytes 1000 | tf_op jit(solution)/shard_map/pallas_call | solution.py:55
  2.7 2.6 %collective-permute-start = (bf16[256,128]{1,0:T(8,128)(2,1)S(1)}, bf16[256,128]{1,0:T(8,128)(2,1)S(1)}, u32[]{:S(2)}, u32[]{:S(2)}) collective-permute-start(bf16[256,128]{1,0:T(8,128)(2,1)S(1)} %get-tuple-element.79), channel_id=1, source_target_pairs={{0,2},{2,0},{4,6},{6,4},{8,10},{10,8},{12,14},{14,12},{1,3},{3,1},... | collective-permute-start | bytes 196616 | tf_op jit(solution)/shard_map/ppermute | solution.py:339
  5.3 1.6 %collective-permute-start.1 = (bf16[256,128]{1,0:T(8,128)(2,1)S(1)}, bf16[256,128]{1,0:T(8,128)(2,1)S(1)}, u32[]{:S(2)}, u32[]{:S(2)}) collective-permute-start(bf16[256,128]{1,0:T(8,128)(2,1)S(1)} %get-tuple-element.80), channel_id=1, source_target_pairs={{0,4},{2,6},{4,0},{6,2},{8,12},{10,14},{12,8},{14,10},{1,5},{3,7},... | collective-permute-start | bytes 196616 | tf_op jit(solution)/shard_map/ppermute | solution.py:339
  6.9 3.4 %shard_map.103 = (f32[192,1024]{1,0:T(8,128)S(1)}, bf16[1024,2048]{1,0:T(8,128)(2,1)S(1)}) custom-call(s32[1]{0:T(128)} %bitcast.1.side_ref, bf16[192,1024]{1,0:T(8,128)(2,1)} %own_hbm.1, bf16[192,1024]{1,0:T(8,128)(2,1)S(1)} %collective-permute-done.3.other_ref, bf16[1024,2048]{1,0:T(8,128)(2,1)} %weight_hbm.1), custom_call_target="tpu_custom_call" | custom-call | flops 1000 | bytes 1000 | tf_op jit(solution)/shard_map/pallas_call | solution.py:55
  10.3 1.8 %collective-permute-done.2.b3 = bf16[256,128]{1,0:T(8,128)(2,1)S(1)} collective-permute-done((bf16[256,128]{1,0:T(8,128)(2,1)S(1)}, bf16[256,128]{1,0:T(8,128)(2,1)S(1)}, u32[]{:S(2)}, u32[]{:S(2)}) %collective-permute-start.2) | collective-permute-done | bytes 65568 | tf_op jit(solution)/shard_map/ppermute | solution.py:339
  12.1 2.7 %collective-permute-start.4 = (bf16[256,128]{1,0:T(8,128)(2,1)S(1)}, bf16[256,128]{1,0:T(8,128)(2,1)S(1)}, u32[]{:S(2)}, u32[]{:S(2)}) collective-permute-start(bf16[256,128]{1,0:T(8,128)(2,1)S(1)} %shard_map.104), channel_id=1, source_target_pairs={{0,8},{2,10},{4,12},{6,14},{8,0},{10,2},{12,4},{14,6},{1,9},{3,11}... | collective-permute-start | bytes 196616 | tf_op jit(solution)/shard_map/ppermute | solution.py:339
  14.8 1.8 %shard_map.102 = (f32[192,1024]{1,0:T(8,128)S(1)}, bf16[192,1024]{1,0:T(8,128)(2,1)S(1)}, bf16[8,192,192]{2,1,0:T(8,128)(2,1)S(1)}) custom-call(bf16[192,1024]{1,0:T(8,128)(2,1)} %query_hbm.1, bf16[192,1024]{1,0:T(8,128)(2,1)S(1)} %get-tuple-element.75.key_ref.refs_0_, bf16[192,1024]{1,0:T(8,128)(2,1)S(1)} %get-tuple-element.76.value_ref.refs_1_), custom_call_target="tpu_custom_call" | custom-call | flops 1000 | bytes 1000 | tf_op jit(solution)/shard_map/pallas_call | solution.py:55
  16.6 1.3 %collective-permute-done.4.got_ref = bf16[256,128]{1,0:T(8,128)(2,1)S(1)} collective-permute-done((bf16[256,128]{1,0:T(8,128)(2,1)S(1)}, bf16[256,128]{1,0:T(8,128)(2,1)S(1)}, u32[]{:S(2)}, u32[]{:S(2)}) %collective-permute-start.4) | collective-permute-done | bytes 65568 | tf_op jit(solution)/shard_map/ppermute | solution.py:339
  18.0 0.8 %collective-permute-start.9 = (bf16[256,128]{1,0:T(8,128)(2,1)S(1)}, bf16[256,128]{1,0:T(8,128)(2,1)S(1)}, u32[]{:S(2)}, u32[]{:S(2)}) collective-permute-start(bf16[256,128]{1,0:T(8,128)(2,1)S(1)} %get-tuple-element.97), channel_id=1, source_target_pairs={{0,6},{2,4},{4,2},{6,0},{8,14},{10,12},{12,10},{14,8},{1,7},{3,5},... | collective-permute-start | bytes 196616 | tf_op jit(solution)/shard_map/ppermute | solution.py:339
  18.9 0.7 %collective-permute-start.7 = (bf16[256,128]{1,0:T(8,128)(2,1)S(1)}, bf16[256,128]{1,0:T(8,128)(2,1)S(1)}, u32[]{:S(2)}, u32[]{:S(2)}) collective-permute-start(bf16[256,128]{1,0:T(8,128)(2,1)S(1)} %get-tuple-element.95), channel_id=1, source_target_pairs={{0,4},{2,6},{4,0},{6,2},{8,12},{10,14},{12,8},{14,10},{1,5},{3,7},... | collective-permute-start | bytes 196616 | tf_op jit(solution)/shard_map/ppermute | solution.py:339
  19.5 2.1 %collective-permute-start.5 = (bf16[256,128]{1,0:T(8,128)(2,1)S(1)}, bf16[256,128]{1,0:T(8,128)(2,1)S(1)}, u32[]{:S(2)}, u32[]{:S(2)}) collective-permute-start(bf16[256,128]{1,0:T(8,128)(2,1)S(1)} %get-tuple-element.93), channel_id=1, source_target_pairs={{0,2},{2,0},{4,6},{6,4},{8,10},{10,8},{12,14},{14,12},{1,3},{3,1},... | collective-permute-start | bytes 196616 | tf_op jit(solution)/shard_map/ppermute | solution.py:339
  21.6 1.7 %collective-permute-done.9.prefix_ref.rest_11_ = bf16[256,128]{1,0:T(8,128)(2,1)S(1)} collective-permute-done((bf16[256,128]{1,0:T(8,128)(2,1)S(1)}, bf16[256,128]{1,0:T(8,128)(2,1)S(1)}, u32[]{:S(2)}, u32[]{:S(2)}) %collective-permute-start.9) | collective-permute-done | bytes 65568 | tf_op jit(solution)/shard_map/ppermute | solution.py:339
  23.8 0.8 %collective-permute-start.10 = (bf16[272,128]{1,0:T(8,128)(2,1)S(1)}, bf16[272,128]{1,0:T(8,128)(2,1)S(1)}, u32[]{:S(2)}, u32[]{:S(2)}) collective-permute-start(bf16[272,128]{1,0:T(8,128)(2,1)S(1)} %get-tuple-element.98), channel_id=1, source_target_pairs={{0,6},{2,4},{4,2},{6,0},{8,14},{10,12},{12,10},{14,8},{1,7},{3,5},... | collective-permute-start | bytes 208904 | tf_op jit(solution)/shard_map/ppermute | solution.py:339
  25.0 0.7 %collective-permute-start.8 = (bf16[272,128]{1,0:T(8,128)(2,1)S(1)}, bf16[272,128]{1,0:T(8,128)(2,1)S(1)}, u32[]{:S(2)}, u32[]{:S(2)}) collective-permute-start(bf16[272,128]{1,0:T(8,128)(2,1)S(1)} %get-tuple-element.96), channel_id=1, source_target_pairs={{0,4},{2,6},{4,0},{6,2},{8,12},{10,14},{12,8},{14,10},{1,5},{3,7},... | collective-permute-start | bytes 208904 | tf_op jit(solution)/shard_map/ppermute | solution.py:339
  26.2 2.1 %collective-permute-start.6 = (bf16[272,128]{1,0:T(8,128)(2,1)S(1)}, bf16[272,128]{1,0:T(8,128)(2,1)S(1)}, u32[]{:S(2)}, u32[]{:S(2)}) collective-permute-start(bf16[272,128]{1,0:T(8,128)(2,1)S(1)} %get-tuple-element.94), channel_id=1, source_target_pairs={{0,2},{2,0},{4,6},{6,4},{8,10},{10,8},{12,14},{14,12},{1,3},{3,1},... | collective-permute-start | bytes 208904 | tf_op jit(solution)/shard_map/ppermute | solution.py:339
  28.9 2.1 %shard_map.110 = (bf16[192,1024]{1,0:T(8,128)(2,1)}, bf16[192,1024]{1,0:T(8,128)(2,1)S(1)}, bf16[8,192,192]{2,1,0:T(8,128)(2,1)S(1)}) custom-call(s32[1]{0:T(128)} %bitcast.place_ref, s32[1]{0:T(128)} %bitcast.1.side_ref, bf16[192,1024]{1,0:T(8,128)(2,1)S(1)} %get-tuple-element.75.key_ref.refs_0_, bf16[192,1024]{1,0:T(8,128)(2,1)S(1)} %get-tuple-element.76.value_ref.refs_1_, ...), custom_call_target="tpu_custom_call" | custom-call | flops 1000 | bytes 1000 | tf_op jit(solution)/shard_map/pallas_call | solution.py:55
  31.1 2.3 %collective-permute-start.11 = (bf16[272,128]{1,0:T(8,128)(2,1)S(1)}, bf16[272,128]{1,0:T(8,128)(2,1)S(1)}, u32[]{:S(2)}, u32[]{:S(2)}) collective-permute-start(bf16[272,128]{1,0:T(8,128)(2,1)S(1)} %get-tuple-element.113), channel_id=1, source_target_pairs={{0,8},{2,10},{4,12},{6,14},{8,0},{10,2},{12,4},{14,6},{1,9},{3,11}... | collective-permute-start | bytes 208904 | tf_op jit(solution)/shard_map/ppermute | solution.py:339
  33.4 0.7 %shard_map.112 = (f32[192,1024]{1,0:T(8,128)S(1)}, f32[192,1024]{1,0:T(8,128)S(1)}) custom-call(s32[1]{0:T(128)} %bitcast.place_ref, bf16[192,1024]{1,0:T(8,128)(2,1)S(1)} %get-tuple-element.77.query_ref, bf16[8,192,192]{2,1,0:T(8,128)(2,1)S(1)} %get-tuple-element.114.score_ref, bf16[8,192,192]{2,1,0:T(8,128)(2,1)S(1)} %get-tuple-element.115.grad_score_ref, ...), custom_call_target="tpu_custom_call" | custom-call | flops 1000 | bytes 1000 | tf_op jit(solution)/shard_map/pallas_call | solution.py:55
  34.1 2.2 %collective-permute-done.11.got_ref = bf16[272,128]{1,0:T(8,128)(2,1)S(1)} collective-permute-done((bf16[272,128]{1,0:T(8,128)(2,1)S(1)}, bf16[272,128]{1,0:T(8,128)(2,1)S(1)}, u32[]{:S(2)}, u32[]{:S(2)}) %collective-permute-start.11) | collective-permute-done | bytes 69664 | tf_op jit(solution)/shard_map/ppermute | solution.py:339
  36.5 2.0 %collective-permute-start.14 = (bf16[272,128]{1,0:T(8,128)(2,1)S(1)}, bf16[272,128]{1,0:T(8,128)(2,1)S(1)}, u32[]{:S(2)}, u32[]{:S(2)}) collective-permute-start(bf16[272,128]{1,0:T(8,128)(2,1)S(1)} %get-tuple-element.128), channel_id=1, source_target_pairs={{0,2},{2,0},{4,6},{6,4},{8,10},{10,8},{12,14},{14,12},{1,3},{3,1},... | collective-permute-start | bytes 208904 | tf_op jit(solution)/shard_map/ppermute | solution.py:339
  38.5 1.6 %collective-permute-start.15 = (bf16[272,128]{1,0:T(8,128)(2,1)S(1)}, bf16[272,128]{1,0:T(8,128)(2,1)S(1)}, u32[]{:S(2)}, u32[]{:S(2)}) collective-permute-start(bf16[272,128]{1,0:T(8,128)(2,1)S(1)} %get-tuple-element.137), channel_id=1, source_target_pairs={{0,6},{2,4},{4,2},{6,0},{8,14},{10,12},{12,10},{14,8},{1,7},{3,5},... | collective-permute-start | bytes 208904 | tf_op jit(solution)/shard_map/ppermute | solution.py:339
  40.3 1.1 %collective-permute-done.14.refs_4_.rest_1_ = bf16[272,128]{1,0:T(8,128)(2,1)S(1)} collective-permute-done((bf16[272,128]{1,0:T(8,128)(2,1)S(1)}, bf16[272,128]{1,0:T(8,128)(2,1)S(1)}, u32[]{:S(2)}, u32[]{:S(2)}) %collective-permute-start.14) | collective-permute-done | bytes 69664 | tf_op jit(solution)/shard_map/ppermute | solution.py:339
  41.5 1.4 %shard_map.116 = (bf16[192,1024]{1,0:T(8,128)(2,1)}, bf16[192,1024]{1,0:T(8,128)(2,1)}, bf16[192,1024]{1,0:T(8,128)(2,1)}) custom-call(s32[1]{0:T(128)} %bitcast.place_ref, s32[1]{0:T(128)} %bitcast.1.side_ref, bf16[1024,2048]{1,0:T(8,128)(2,1)S(1)} %get-tuple-element.99.weight_ref, bf16[192,1024]{1,0:T(8,128)(2,1)S(1)} %collective-permute-done.13.other_ref, ...), custom_call_target="tpu_custom_call" | custom-call | flops 1000 | bytes 1000 | tf_op jit(solution)/shard_map/pallas_call | solution.py:55
  44.1 0.9 %shard_map.118 = (bf16[192,1024]{1,0:T(8,128)(2,1)}, bf16[192,1024]{1,0:T(8,128)(2,1)}, f32[1,1024]{1,0:T(1,128)}) custom-call(s32[1]{0:T(128)} %bitcast.place_ref, bf16[192,1024]{1,0:T(8,128)(2,1)S(1)} %get-tuple-element.75.key_ref.refs_0_, ...), custom_call_target="tpu_custom_call", output_to_operand_aliasing={{0}: (11, {}), {1}: (12, {})} | custom-call | flops 1000 | bytes 1000 | tf_op jit(solution)/shard_map/pallas_call | solution.py:55
  (28 shorter events, 4.3 us)
Async XLA Ops:
  0.6 22.7 %copy-start = (f32[1024]{0:T(1024)S(1)}, f32[1024]{0:T(1024)}, u32[]{:S(2)}) copy-start(f32[1024]{0:T(1024)} %param.10) | copy-start | bytes 12292
  0.6 6.3 %collective-permute-start.3 = (bf16[192,1024]{1,0:T(8,128)(2,1)}, bf16[192,1024]{1,0:T(8,128)(2,1)S(1)}, u32[]{:S(2)}, u32[]{:S(2)}) collective-permute-start(bf16[192,1024]{1,0:T(8,128)(2,1)} %own_hbm.1), channel_id=1, source_target_pairs={{0,1},{1,0},{2,3},{3,2},{4,5},{5,4},{6,7},{7,6},{8,9},{9,8},{10,11... | collective-permute-start | bytes 1179656 | tf_op jit(solution)/shard_map/ppermute | solution.py:343
  2.7 7.6 %collective-permute-start = (bf16[256,128]{1,0:T(8,128)(2,1)S(1)}, bf16[256,128]{1,0:T(8,128)(2,1)S(1)}, u32[]{:S(2)}, u32[]{:S(2)}) collective-permute-start(bf16[256,128]{1,0:T(8,128)(2,1)S(1)} %get-tuple-element.79), channel_id=1, source_target_pairs={{0,2},{2,0},{4,6},{6,4},{8,10},{10,8},{12,14},{14,12},{1,3},{3,1},... | collective-permute-start | bytes 196616 | tf_op jit(solution)/shard_map/ppermute | solution.py:339
  5.3 5.0 %collective-permute-start.1 = (bf16[256,128]{1,0:T(8,128)(2,1)S(1)}, bf16[256,128]{1,0:T(8,128)(2,1)S(1)}, u32[]{:S(2)}, u32[]{:S(2)}) collective-permute-start(bf16[256,128]{1,0:T(8,128)(2,1)S(1)} %get-tuple-element.80), channel_id=1, source_target_pairs={{0,4},{2,6},{4,0},{6,2},{8,12},{10,14},{12,8},{14,10},{1,5},{3,7},... | collective-permute-start | bytes 196616 | tf_op jit(solution)/shard_map/ppermute | solution.py:339
  6.9 5.2 %collective-permute-start.2 = (bf16[256,128]{1,0:T(8,128)(2,1)S(1)}, bf16[256,128]{1,0:T(8,128)(2,1)S(1)}, u32[]{:S(2)}, u32[]{:S(2)}) collective-permute-start(bf16[256,128]{1,0:T(8,128)(2,1)S(1)} %get-tuple-element.81), channel_id=1, source_target_pairs={{0,6},{2,4},{4,2},{6,0},{8,14},{10,12},{12,10},{14,8},{1,7},{3,5},... | collective-permute-start | bytes 196616 | tf_op jit(solution)/shard_map/ppermute | solution.py:339
  12.1 5.8 %collective-permute-start.4 = (bf16[256,128]{1,0:T(8,128)(2,1)S(1)}, bf16[256,128]{1,0:T(8,128)(2,1)S(1)}, u32[]{:S(2)}, u32[]{:S(2)}) collective-permute-start(bf16[256,128]{1,0:T(8,128)(2,1)S(1)} %shard_map.104), channel_id=1, source_target_pairs={{0,8},{2,10},{4,12},{6,14},{8,0},{10,2},{12,4},{14,6},{1,9},{3,11}... | collective-permute-start | bytes 196616 | tf_op jit(solution)/shard_map/ppermute | solution.py:339
  18.0 5.2 %collective-permute-start.9 = (bf16[256,128]{1,0:T(8,128)(2,1)S(1)}, bf16[256,128]{1,0:T(8,128)(2,1)S(1)}, u32[]{:S(2)}, u32[]{:S(2)}) collective-permute-start(bf16[256,128]{1,0:T(8,128)(2,1)S(1)} %get-tuple-element.97), channel_id=1, source_target_pairs={{0,6},{2,4},{4,2},{6,0},{8,14},{10,12},{12,10},{14,8},{1,7},{3,5},... | collective-permute-start | bytes 196616 | tf_op jit(solution)/shard_map/ppermute | solution.py:339
  18.9 5.7 %collective-permute-start.7 = (bf16[256,128]{1,0:T(8,128)(2,1)S(1)}, bf16[256,128]{1,0:T(8,128)(2,1)S(1)}, u32[]{:S(2)}, u32[]{:S(2)}) collective-permute-start(bf16[256,128]{1,0:T(8,128)(2,1)S(1)} %get-tuple-element.95), channel_id=1, source_target_pairs={{0,4},{2,6},{4,0},{6,2},{8,12},{10,14},{12,8},{14,10},{1,5},{3,7},... | collective-permute-start | bytes 196616 | tf_op jit(solution)/shard_map/ppermute | solution.py:339
  19.5 6.3 %collective-permute-start.5 = (bf16[256,128]{1,0:T(8,128)(2,1)S(1)}, bf16[256,128]{1,0:T(8,128)(2,1)S(1)}, u32[]{:S(2)}, u32[]{:S(2)}) collective-permute-start(bf16[256,128]{1,0:T(8,128)(2,1)S(1)} %get-tuple-element.93), channel_id=1, source_target_pairs={{0,2},{2,0},{4,6},{6,4},{8,10},{10,8},{12,14},{14,12},{1,3},{3,1},... | collective-permute-start | bytes 196616 | tf_op jit(solution)/shard_map/ppermute | solution.py:339
  23.8 7.2 %collective-permute-start.10 = (bf16[272,128]{1,0:T(8,128)(2,1)S(1)}, bf16[272,128]{1,0:T(8,128)(2,1)S(1)}, u32[]{:S(2)}, u32[]{:S(2)}) collective-permute-start(bf16[272,128]{1,0:T(8,128)(2,1)S(1)} %get-tuple-element.98), channel_id=1, source_target_pairs={{0,6},{2,4},{4,2},{6,0},{8,14},{10,12},{12,10},{14,8},{1,7},{3,5},... | collective-permute-start | bytes 208904 | tf_op jit(solution)/shard_map/ppermute | solution.py:339
  25.0 5.9 %collective-permute-start.8 = (bf16[272,128]{1,0:T(8,128)(2,1)S(1)}, bf16[272,128]{1,0:T(8,128)(2,1)S(1)}, u32[]{:S(2)}, u32[]{:S(2)}) collective-permute-start(bf16[272,128]{1,0:T(8,128)(2,1)S(1)} %get-tuple-element.96), channel_id=1, source_target_pairs={{0,4},{2,6},{4,0},{6,2},{8,12},{10,14},{12,8},{14,10},{1,5},{3,7},... | collective-permute-start | bytes 208904 | tf_op jit(solution)/shard_map/ppermute | solution.py:339
  26.2 4.7 %collective-permute-start.6 = (bf16[272,128]{1,0:T(8,128)(2,1)S(1)}, bf16[272,128]{1,0:T(8,128)(2,1)S(1)}, u32[]{:S(2)}, u32[]{:S(2)}) collective-permute-start(bf16[272,128]{1,0:T(8,128)(2,1)S(1)} %get-tuple-element.94), channel_id=1, source_target_pairs={{0,2},{2,0},{4,6},{6,4},{8,10},{10,8},{12,14},{14,12},{1,3},{3,1},... | collective-permute-start | bytes 208904 | tf_op jit(solution)/shard_map/ppermute | solution.py:339
  31.1 5.3 %collective-permute-start.11 = (bf16[272,128]{1,0:T(8,128)(2,1)S(1)}, bf16[272,128]{1,0:T(8,128)(2,1)S(1)}, u32[]{:S(2)}, u32[]{:S(2)}) collective-permute-start(bf16[272,128]{1,0:T(8,128)(2,1)S(1)} %get-tuple-element.113), channel_id=1, source_target_pairs={{0,8},{2,10},{4,12},{6,14},{8,0},{10,2},{12,4},{14,6},{1,9},{3,11}... | collective-permute-start | bytes 208904 | tf_op jit(solution)/shard_map/ppermute | solution.py:339
  36.3 5.2 %collective-permute-start.13 = (bf16[192,1024]{1,0:T(8,128)(2,1)S(1)}, bf16[192,1024]{1,0:T(8,128)(2,1)S(1)}, u32[]{:S(2)}, u32[]{:S(2)}) collective-permute-start(bf16[192,1024]{1,0:T(8,128)(2,1)S(1)} %get-tuple-element.122), channel_id=1, source_target_pairs={{0,1},{1,0},{2,3},{3,2},{4,5},{5,4},{6,7},{7,6},{8,9},{9,8},{10,11... | collective-permute-start | bytes 1179656 | tf_op jit(solution)/shard_map/ppermute | solution.py:343
  36.5 4.8 %collective-permute-start.14 = (bf16[272,128]{1,0:T(8,128)(2,1)S(1)}, bf16[272,128]{1,0:T(8,128)(2,1)S(1)}, u32[]{:S(2)}, u32[]{:S(2)}) collective-permute-start(bf16[272,128]{1,0:T(8,128)(2,1)S(1)} %get-tuple-element.128), channel_id=1, source_target_pairs={{0,2},{2,0},{4,6},{6,4},{8,10},{10,8},{12,14},{14,12},{1,3},{3,1},... | collective-permute-start | bytes 208904 | tf_op jit(solution)/shard_map/ppermute | solution.py:339
  38.5 5.0 %collective-permute-start.12 = (bf16[272,128]{1,0:T(8,128)(2,1)S(1)}, bf16[272,128]{1,0:T(8,128)(2,1)S(1)}, u32[]{:S(2)}, u32[]{:S(2)}) collective-permute-start(bf16[272,128]{1,0:T(8,128)(2,1)S(1)} %get-tuple-element.121), channel_id=1, source_target_pairs={{0,4},{2,6},{4,0},{6,2},{8,12},{10,14},{12,8},{14,10},{1,5},{3,7},... | collective-permute-start | bytes 208904 | tf_op jit(solution)/shard_map/ppermute | solution.py:339
  38.5 5.6 %collective-permute-start.15 = (bf16[272,128]{1,0:T(8,128)(2,1)S(1)}, bf16[272,128]{1,0:T(8,128)(2,1)S(1)}, u32[]{:S(2)}, u32[]{:S(2)}) collective-permute-start(bf16[272,128]{1,0:T(8,128)(2,1)S(1)} %get-tuple-element.137), channel_id=1, source_target_pairs={{0,6},{2,4},{4,2},{6,0},{8,14},{10,12},{12,10},{14,8},{1,7},{3,5},... | collective-permute-start | bytes 208904 | tf_op jit(solution)/shard_map/ppermute | solution.py:339
